TPU v7x, 32 devices: a whole 2x2x4 slice. The times are simulated.
32 devices in a mesh: src: 4 (over x, core), rcv: 8 (over z, y).
Axes of the slice: x: 2, y: 2, z: 4, core: 2. Of those that a mesh axis runs over, the one named last changes fastest.
Arguments:
- wavefield: bfloat16 [1024, 1024, 256], P('src', 'rcv'), may hold values from -6 to 6
- inverse_wavelet: float32 [2, 64], replicated, may hold values from -0.05 to 0.05
Outputs:
- primaries: bfloat16 [1024, 1024, 256], P('src', 'rcv')
All inputs are finite; a program needn't handle non-finite values.
Results may differ from a plain program's by a relative error of at most 0.0091.
Values may be sent and summed in bfloat16 or wider, within the bound.
No kernel may reach another device: no remote copies, remote signals or barrier semaphores. Data moves between devices by JAX's collectives and lax.ppermute only.
A program may use at most 256 MiB of HBM per device.

v0:
```python
import math

import jax
import jax.numpy as jnp
from jax import lax
from jax.sharding import PartitionSpec as P

F0 = 8


def tables(count_t, count_f, first):
    times = jnp.arange(count_t, dtype=jnp.int32)
    freqs = first + jnp.arange(count_f, dtype=jnp.int32)
    phase = freqs[:, None] * times[None, :] % count_t
    angle = phase.astype(jnp.float32) * (2.0 * math.pi / count_t)
    rows = jnp.stack([jnp.cos(angle), -jnp.sin(angle)], 1).reshape(2 * count_f, count_t)
    forward = (rows / math.sqrt(count_t)).astype(jnp.bfloat16)
    inverse = (rows / math.sqrt(count_f)).astype(jnp.bfloat16)
    return (forward, inverse)


def combine(mirror_real, mirror_imag, sq_real, sq_imag, cube_real, cube_imag, wave_real, wave_imag):
    two_real = wave_real * wave_real - wave_imag * wave_imag
    two_imag = 2.0 * wave_real * wave_imag
    out_real = (
        mirror_real
        - (wave_real * sq_real - wave_imag * sq_imag)
        + (two_real * cube_real - two_imag * cube_imag)
    )
    out_imag = (
        mirror_imag
        - (wave_real * sq_imag + wave_imag * sq_real)
        + (two_real * cube_imag + two_imag * cube_real)
    )
    return (out_real, out_imag)


def multiply(left_side, right_side):
    return jnp.einsum("fmk,fkn->fmn", left_side, right_side, preferred_element_type=jnp.float32)


def complex_product(left_side, right_side):
    real_part = multiply(left_side[:, 0], right_side[:, 0]) - multiply(
        left_side[:, 1], right_side[:, 1]
    )
    imag_part = multiply(left_side[:, 0], right_side[:, 1]) + multiply(
        left_side[:, 1], right_side[:, 0]
    )
    return (real_part, imag_part)


def local(wavefield, inverse_wavelet):
    src_rows, rcv_cols, samples = wavefield.shape
    count_f = inverse_wavelet.shape[1]
    groups = lax.axis_size("rcv")
    per_dev = count_f // groups
    forward, inverse = tables(samples, count_f, F0)
    spectra = jnp.einsum(
        "ct,srt->csr", forward, wavefield, preferred_element_type=jnp.float32
    ).astype(jnp.bfloat16)
    spectra = spectra.reshape(groups, 2 * per_dev, src_rows, rcv_cols)
    slices = lax.all_to_all(spectra, "rcv", split_axis=0, concat_axis=3, tiled=True)
    total_cols = slices.shape[3]
    slices = slices.reshape(per_dev, 2, src_rows, total_cols)
    whole = lax.all_gather(slices, "src", axis=2, tiled=True).astype(jnp.float32)
    all_rows = (0.5 * (whole + jnp.swapaxes(whole, 2, 3))).astype(jnp.bfloat16)
    mirrored = lax.dynamic_slice_in_dim(all_rows, lax.axis_index("src") * src_rows, src_rows, 2)
    sq_real, sq_imag = complex_product(mirrored, all_rows)
    squared = jnp.stack([sq_real, sq_imag], 1).astype(jnp.bfloat16)
    cube_real, cube_imag = complex_product(squared, all_rows)
    wavelet = lax.dynamic_slice_in_dim(inverse_wavelet, lax.axis_index("rcv") * per_dev, per_dev, 1)
    wave_real = wavelet[0][:, None, None]
    wave_imag = wavelet[1][:, None, None]
    out_real, out_imag = combine(
        mirrored[:, 0].astype(jnp.float32),
        mirrored[:, 1].astype(jnp.float32),
        sq_real,
        sq_imag,
        cube_real,
        cube_imag,
        wave_real,
        wave_imag,
    )
    cleaned = (
        jnp.stack([out_real, out_imag], 1)
        .astype(jnp.bfloat16)
        .reshape(1, 2 * per_dev, src_rows, total_cols)
    )
    returned = lax.all_to_all(cleaned, "rcv", split_axis=3, concat_axis=0, tiled=True)
    returned = returned.reshape(2 * count_f, src_rows, rcv_cols)
    return jnp.einsum("csr,ct->srt", returned, inverse, preferred_element_type=jnp.float32).astype(
        jnp.bfloat16
    )


def solution(mesh):
    placed = (P("src", "rcv", None), P())
    return jax.shard_map(
        local, mesh=mesh, in_specs=placed, out_specs=P("src", "rcv", None), check_vma=False
    )
```

profile of v0, /device:TPU:0, one launch (start us, length us, event | category | flops | bytes accessed | tf_op | source)
XLA Modules:
  0.0 943.3 jit_solution(6739649526145548966)
XLA Ops:
  6.5 0.3 fusion.25
  6.9 0.6 multiply_convert_fusion.1
  7.5 0.1 copy.29
  7.6 11.1 %convolution_convert_fusion.1 = bf16[128,256,128]{2,0,1:T(8,128)(2,1)} fusion(bf16[128,256,1]{1,0,2:T(8,128)(2,1)S(1)} %reshape.171, bf16[256,128,256]{2,1,0:T(8,128)(2,1)} %param.2), kind=kOutput, calls=%fused_computation.18 | convolution fusion | flops 2151677952 | bytes 25231360 | tf_op jit(solution)/shard_map/ct,srt->csr/dot_general | solution.py:58
  18.8 13.0 %copy.30 = bf16[8,16,256,128]{2,3,1,0:T(8,128)(2,1)} copy(bf16[8,16,256,128]{3,1,0,2:T(8,128)(2,1)} %bitcast.70) | data formatting | bytes 16777216 | tf_op jit(solution)/shard_map/reshape | solution.py:61
  31.7 190.4 %all_to_all.30 = bf16[8,16,256,128]{2,3,1,0:T(8,128)(2,1)} all-to-all(bf16[8,16,256,128]{2,3,1,0:T(8,128)(2,1)} %copy.30), channel_id=1, replica_groups=mesh['src'=4,'rcv'=8] {'rcv'}, dimensions={0} | all-to-all | bytes 16777216 | tf_op jit(solution)/shard_map/all_to_all | solution.py:62
  222.2 7.9 copy.31
  230.0 7.4 copy.32
  237.4 0.0 all-gather.2.cloned.1.call-update
  237.4 0.1 constant_dynamic-slice_fusion
  237.5 0.5 multiply_subtract_fusion
  238.1 0.6 slice_bitcast_fusion.15
  238.6 204.0 %all-gather.2.cloned.1.call-done = bf16[8,2,1024,1024]{2,3,0,1:T(8,128)(2,1)} async-done(((bf16[8,2,256,1024]{2,3,0,1:T(8,128)(2,1)}), bf16[8,2,1024,1024]{2,3,0,1:T(8,128)(2,1)}) %all-gather.2.cloned.1.call-update) | async-done | bytes 33554448 | tf_op jit(solution)/shard_map/all_gather | solution.py:65
  442.7 46.2 %copy.33 = f32[8,2,1024,1024]{3,2,0,1:T(8,128)} copy(bf16[8,2,1024,1024]{2,3,0,1:T(8,128)(2,1)} %all-gather.2.cloned.1.call-done) | data formatting | bytes 100663296 | tf_op jit(solution)/shard_map/convert_element_type | solution.py:65
  488.8 43.1 %fusion.1 = bf16[8,2,1024,1024]{3,2,0,1:T(8,128)(2,1)} fusion(f32[8,2,1024,1024]{3,2,0,1:T(8,128)} %copy.33, bf16[8,2,1024,1024]{2,3,0,1:T(8,128)(2,1)} %all-gather.2.cloned.1.call-done), kind=kLoop, calls=%fused_computation.2 | loop fusion | flops 67108864 | bytes 134217728 | tf_op jit(solution)/shard_map/convert_element_type | solution.py:66
  532.0 14.8 %fusion.5 = f32[8,256,1024]{2,1,0:T(8,128)} fusion(bf16[8,2,1024,1024]{3,2,0,1:T(8,128)(2,1)} %fusion.1, s32[]{:T(128)S(6)} %select_n.27), kind=kOutput, calls=%fused_computation.8 | convolution fusion | flops 4294967296 | bytes 29360132 | tf_op jit(solution)/shard_map/fmk,fkn->fmn/dot_general | solution.py:39
  546.8 15.0 %fusion.4 = f32[8,256,1024]{2,1,0:T(8,128)} fusion(bf16[8,2,1024,1024]{3,2,0,1:T(8,128)(2,1)} %fusion.1, s32[]{:T(128)S(6)} %add.70, s32[]{:T(128)S(6)} %select_n.27), kind=kOutput, calls=%fused_computation.7 | convolution fusion | flops 4294967296 | bytes 29360136 | tf_op jit(solution)/shard_map/fmk,fkn->fmn/dot_general | solution.py:39
  561.8 17.2 %fusion.13 = f32[8,256,1024]{2,1,0:T(8,128)} fusion(f32[8,256,1024]{2,1,0:T(8,128)} %fusion.5, bf16[8,2,1024,1024]{3,2,0,1:T(8,128)(2,1)} %fusion.1, s32[]{:T(128)S(6)} %add.70, s32[]{:T(128)S(6)} %select_n.27), kind=kOutput, calls=%fused_computation.23 | convolution fusion | flops 4297064448 | bytes 37748744 | tf_op jit(solution)/shard_map/fmk,fkn->fmn/dot_general | solution.py:39
  579.0 16.1 %fusion.6 = f32[8,256,1024]{2,1,0:T(8,128)} fusion(bf16[8,2,1024,1024]{3,2,0,1:T(8,128)(2,1)} %fusion.1, f32[8,256,1024]{2,1,0:T(8,128)} %fusion.13), kind=kOutput, calls=%fused_computation.9 | convolution fusion | flops 4297064448 | bytes 33554432 | tf_op jit(solution)/shard_map/fmk,fkn->fmn/dot_general | solution.py:39
  595.1 15.9 %fusion.3 = f32[8,256,1024]{2,1,0:T(8,128)} fusion(bf16[8,2,1024,1024]{3,2,0,1:T(8,128)(2,1)} %fusion.1, f32[8,256,1024]{2,1,0:T(8,128)} %fusion.13), kind=kOutput, calls=%fused_computation.6 | convolution fusion | flops 4297064448 | bytes 33554432 | tf_op jit(solution)/shard_map/fmk,fkn->fmn/dot_general | solution.py:39
  611.0 17.4 %fusion.14 = f32[8,256,1024]{2,1,0:T(8,128)} fusion(f32[8,256,1024]{2,1,0:T(8,128)} %fusion.4, bf16[8,2,1024,1024]{3,2,0,1:T(8,128)(2,1)} %fusion.1, s32[]{:T(128)S(6)} %select_n.27), kind=kOutput, calls=%fused_computation.24 | convolution fusion | flops 4297064448 | bytes 37748740 | tf_op jit(solution)/shard_map/fmk,fkn->fmn/dot_general | solution.py:39
  628.4 16.1 %fusion.2 = f32[8,256,1024]{2,1,0:T(8,128)} fusion(bf16[8,2,1024,1024]{3,2,0,1:T(8,128)(2,1)} %fusion.1, f32[8,256,1024]{2,1,0:T(8,128)} %fusion.14), kind=kOutput, calls=%fused_computation.5 | convolution fusion | flops 4297064448 | bytes 33554432 | tf_op jit(solution)/shard_map/fmk,fkn->fmn/dot_general | solution.py:39
  644.5 28.6 %fusion.11 = (bf16[8,1,256,1024]{3,2,0,1:T(8,128)(2,1)}, bf16[8,1,256,1024]{3,2,0,1:T(8,128)(2,1)}) fusion(f32[8,256,1024]{2,1,0:T(8,128)} %fusion.14, f32[8,256,1024]{2,1,0:T(8,128)} %fusion.13, f32[8]{0:T(128)S(1)} %copy-done.4, f32[8]{0:T(128)S(1)} %copy-done.3, f32[8]{0:T(128)S(1)} %copy-done.6, f32[8]{0:T(128)S(1)} %copy-done.5, ...), kind=kOutput, calls=%fused_computation.19 | convolution fusion | flops 4343201792 | bytes 83886216 | tf_op jit(solution)/shard_map/fmk,fkn->fmn/dot_general | solution.py:39
  673.1 7.6 pad_maximum_fusion
  680.7 8.0 copy.34
  688.7 12.5 %copy.35 = bf16[1,16,256,1024]{2,1,0,3:T(8,128)(2,1)} copy(bf16[1,16,256,1024]{3,2,1,0:T(8,128)(2,1)} %bitcast.73) | data formatting | bytes 16777216 | tf_op jit(solution)/shard_map/convert_element_type | solution.py:86
  701.2 5.6 all-to-all-start.1
  706.8 0.1 copy.38
  707.0 183.5 %all-to-all-done.1 = bf16[1,16,256,1024]{2,1,0,3:T(8,128)(2,1)} async-done(((bf16[1,16,256,1024]{2,1,0,3:T(8,128)(2,1)}), bf16[1,16,256,1024]{2,1,0,3:T(8,128)(2,1)}, u32[]{:S(2)}, u32[]{:S(2)}) %all-to-all-start.1) | async-done | bytes 8388640 | tf_op jit(solution)/shard_map/all_to_all | solution.py:89
  890.4 9.8 %copy.36 = bf16[1,16,256,1024]{2,3,1,0:T(8,128)(2,1)} copy(bf16[1,16,256,1024]{2,1,0,3:T(8,128)(2,1)} %all-to-all-done.1) | data formatting | bytes 16777216 | tf_op jit(solution)/shard_map/all_to_all | solution.py:89
  900.2 11.4 %copy.37 = bf16[8,1,16,256,128]{4,3,2,0,1:T(8,128)(2,1)} copy(bf16[8,1,16,256,128]{3,4,0,2,1:T(8,128)(2,1)} %bitcast.74) | data formatting | bytes 16777216 | tf_op jit(solution)/shard_map/all_to_all | solution.py:89
  911.7 24.3 %convolution_convert_fusion = bf16[256,128,256]{2,1,0:T(8,128)(2,1)} fusion(bf16[128,256,1]{1,0,2:T(8,128)(2,1)S(1)} %reshape.172, bf16[128,256,128]{2,1,0:T(8,128)(2,1)} %bitcast.71), kind=kOutput, calls=%fused_computation.13 | convolution fusion | flops 2155872256 | bytes 25231360 | tf_op jit(solution)/shard_map/csr,ct->srt/dot_general | solution.py:91
  (18 shorter events, 0.1 us)
Async XLA Ops:
  6.5 230.9 %copy-start = (f32[2,64]{1,0:T(2,128)S(1)}, f32[2,64]{1,0:T(2,128)}, u32[]{:S(2)}) copy-start(f32[2,64]{1,0:T(2,128)} %param.3) | copy-start | bytes 1540
  6.5 436.1 %all-gather.2.cloned.1.call-start = ((), (), s32[]{:S(2)}) async-start(), calls=%async_computation.2 | async-start | bytes 41943040 | tf_op jit(solution)/shard_map/all_gather | solution.py:65
  628.4 16.1 %copy-start.3 = (f32[8]{0:T(128)S(1)}, f32[8]{0:T(128)}, u32[]{:S(2)}) copy-start(f32[8]{0:T(128)} %get-tuple-element.11) | copy-start | bytes 100
  628.4 16.1 %copy-start.4 = (f32[8]{0:T(128)S(1)}, f32[8]{0:T(128)}, u32[]{:S(2)}) copy-start(f32[8]{0:T(128)} %get-tuple-element.12) | copy-start | bytes 100
  628.4 16.1 %copy-start.5 = (f32[8]{0:T(128)S(1)}, f32[8]{0:T(128)}, u32[]{:S(2)}) copy-start(f32[8]{0:T(128)} %get-tuple-element.9) | copy-start | bytes 100
  628.4 16.1 %copy-start.6 = (f32[8]{0:T(128)S(1)}, f32[8]{0:T(128)}, u32[]{:S(2)}) copy-start(f32[8]{0:T(128)} %get-tuple-element.10) | copy-start | bytes 100
  701.2 5.7 copy-start.2
  701.2 189.2 %all-to-all-start.1 = ((bf16[1,16,256,1024]{2,1,0,3:T(8,128)(2,1)}), bf16[1,16,256,1024]{2,1,0,3:T(8,128)(2,1)}, u32[]{:S(2)}, u32[]{:S(2)}) async-start(bf16[1,16,256,1024]{2,1,0,3:T(8,128)(2,1)} %copy.35), calls=%async_computation.1 | async-start | bytes 16777216 | tf_op jit(solution)/shard_map/all_to_all | solution.py:89
  911.7 24.3 %copy-start.1 = (f32[2,64]{1,0:T(2,128)S(1)}, f32[2,64]{1,0:T(2,128)}, u32[]{:S(2)}) copy-start(f32[2,64]{1,0:T(2,128)} %param.3) | copy-start | bytes 1540
Sparse Core Ops, SparseCore 0:
  237.5 205.0 all-gather.1
where the time goes:
time: 950 us; the launch traced here: 943 us
  waiting for transfers between devices  388 us (41%)
  blocking collectives  190 us (20%)
  matrix products  177 us (19%)
  local copies, waits for them, and re-layouts  117 us (12%)
  other arithmetic  52.3 us (6%)
  between operations  13.9 us (1%)
    all_gather x1, waiting for transfers between devices, local(): lax.all_gather(slices, 'src', axis=2, tiled=True).astype(jnp.float32)  204 us
    all_to_all x1, blocking collectives, local(): lax.all_to_all(spectra, 'rcv', split_axis=0, concat_axis=3, tiled=True)  190 us
    all_to_all x1, waiting for transfers between devices, local(): lax.all_to_all(cleaned, 'rcv', split_axis=3, concat_axis=0, tiled=True)  183 us
    dot_general x8, matrix products, multiply(): jnp.einsum('fmk,fkn->fmn', left_side, right_side, preferred_element_type=...  141 us
    convert_element_type x1, local copies, waits for them, and re-layouts, local(): lax.all_gather(slices, 'src', axis=2, tiled=True).astype(jnp.float32)  46.2 us
    convert_element_type x1, other arithmetic, local(): all_rows = (0.5 * (whole + jnp.swapaxes(whole, 2, 3))).astype(jnp.bfloat16)  43.1 us
    dot_general x1, matrix products, local(): jnp.einsum('csr,ct->srt', returned, inverse, preferred_element_type=jnp.f...  24.3 us
    all_to_all x2, local copies, waits for them, and re-layouts, local(): lax.all_to_all(cleaned, 'rcv', split_axis=3, concat_axis=0, tiled=True)  21.2 us
  transfers between devices with their start and end apart: 2, of which 2 were waited for; matrix products, arithmetic and copies ran while one was open for 0% of the time, Pallas kernels for 0%

commit v1 on v0

--- a/solution.py
+++ b/solution.py
@@ -49,7 +49,7 @@
     return (real_part, imag_part)
 
 
-def local(wavefield, inverse_wavelet):
+def local_sliced(wavefield, inverse_wavelet):
     src_rows, rcv_cols, samples = wavefield.shape
     count_f = inverse_wavelet.shape[1]
     groups = lax.axis_size("rcv")
@@ -93,8 +93,75 @@
     )
 
 
+AXES = ("src", "rcv")
+
+
+def owned_frequency(matrix, wave_real, wave_imag):
+    values = matrix.astype(jnp.float32)
+    mirrored = (0.5 * (values + jnp.swapaxes(values, 1, 2))).astype(jnp.bfloat16)
+    whole = mirrored[None]
+    sq_real, sq_imag = complex_product(whole, whole)
+    squared = jnp.stack([sq_real, sq_imag], 1).astype(jnp.bfloat16)
+    cube_real, cube_imag = complex_product(squared, whole)
+    out_real, out_imag = combine(
+        mirrored[0].astype(jnp.float32),
+        mirrored[1].astype(jnp.float32),
+        sq_real[0],
+        sq_imag[0],
+        cube_real[0],
+        cube_imag[0],
+        wave_real,
+        wave_imag,
+    )
+    return out_real.astype(jnp.bfloat16), out_imag.astype(jnp.bfloat16)
+
+
+def local_whole(wavefield, inverse_wavelet):
+    src_rows, rcv_cols, samples = wavefield.shape
+    count_f = inverse_wavelet.shape[1]
+    sources, groups = lax.axis_size("src"), lax.axis_size("rcv")
+    devices = sources * groups
+    me = lax.axis_index(AXES)
+    forward, inverse = tables(samples, count_f, F0)
+    chunks = count_f // devices
+    width = 2 * devices
+    returned = []
+    for chunk in range(chunks):
+        rows = slice(chunk * width, (chunk + 1) * width)
+        spectra = jnp.einsum(
+            "ct,srt->csr", forward[rows], wavefield, preferred_element_type=jnp.float32
+        ).astype(jnp.bfloat16)
+        spectra = spectra.reshape(devices, 2, src_rows, rcv_cols)
+        slices = lax.all_to_all(spectra, AXES, 0, 0, tiled=True)
+        slices = slices.reshape(sources, groups, 2, src_rows, rcv_cols)
+        matrix = slices.transpose(2, 0, 3, 1, 4).reshape(
+            2, sources * src_rows, groups * rcv_cols
+        )
+        wavelet = lax.dynamic_index_in_dim(
+            inverse_wavelet, chunk * devices + me, 1, keepdims=False
+        )
+        out_real, out_imag = owned_frequency(matrix, wavelet[0], wavelet[1])
+        cleaned = jnp.stack([out_real, out_imag]).reshape(
+            2, sources, src_rows, groups, rcv_cols
+        )
+        cleaned = cleaned.transpose(1, 3, 0, 2, 4).reshape(devices, 2, src_rows, rcv_cols)
+        back = lax.all_to_all(cleaned, AXES, 0, 0, tiled=True)
+        returned.append(back.reshape(width, src_rows, rcv_cols))
+    total = jnp.concatenate(returned, 0)
+    return jnp.einsum("csr,ct->srt", total, inverse, preferred_element_type=jnp.float32).astype(
+        jnp.bfloat16
+    )
+
+
 def solution(mesh):
     placed = (P("src", "rcv", None), P())
+
+    def local(wavefield, inverse_wavelet):
+        devices = lax.axis_size("src") * lax.axis_size("rcv")
+        if inverse_wavelet.shape[1] % devices:
+            return local_sliced(wavefield, inverse_wavelet)
+        return local_whole(wavefield, inverse_wavelet)
+
     return jax.shard_map(
         local, mesh=mesh, in_specs=placed, out_specs=P("src", "rcv", None), check_vma=False
     )

time: 950 us -> 455 us (0.48)
  waiting for transfers between devices: 388 us -> 195 us
  blocking collectives: 190 us -> 0 us
  matrix products: 177 us -> 92.9 us
  other arithmetic: 52.3 us -> 28.5 us
  local copies, waits for them, and re-layouts: 117 us -> 104 us
  starting transfers between devices: 5.65 us -> 18.6 us
    all_gather x1 -> x0, waiting for transfers between devices: 204 us -> none  [local(): lax.all_gather(slices, 'src', axis=2, tiled=True).astype(jnp.float32)]
    all_to_all x1 -> x0, blocking collectives: 190 us -> none  [local(): lax.all_to_all(spectra, 'rcv', split_axis=0, concat_axis=3, tiled=True)]
    dot_general x8 -> x16, matrix products: 141 us -> 54.8 us  [multiply(): jnp.einsum('fmk,fkn->fmn', left_side, right_side, preferred_element_type=...]
    all_to_all x3 -> x0, local copies, waits for them, and re-layouts: 29.1 us -> none  [the longest x2 21.2 us: local(): lax.all_to_all(cleaned, 'rcv', split_axis=3, concat_axis=0, tiled=True)]
    convert_element_type x1 -> x3, other arithmetic: 43.1 us -> 22.8 us  [the longest x2 16.2 us: owned_frequency(): (0.5 * (values + jnp.swapaxes(values, 1, 2))).astype(jnp.bfloat16)]
    reshape x2 -> x4, local copies, waits for them, and re-layouts: 20.3 us -> 36.4 us  [the longest x2 18.9 us: local_whole(): returned.append(back.reshape(width, src_rows, rcv_cols))]
    all_to_all x1 -> x4, starting transfers between devices: 5.65 us -> 18.6 us  [the longest x2 11.2 us: local_whole(): slices = lax.all_to_all(spectra, AXES, 0, 0, tiled=True)]
    all_to_all x1 -> x4, waiting for transfers between devices: 183 us -> 195 us  [the longest x2 106 us: local_whole(): back = lax.all_to_all(cleaned, AXES, 0, 0, tiled=True)]
  transfers between devices with their start and end apart: 2 -> 4, of which waited for: 2 -> 4; matrix products, arithmetic and copies ran while one was open for 0% -> 40% of each run, Pallas kernels for 0% -> 0%
where the time goes in v1:
time: 455 us; the launch traced here: 447 us
  waiting for transfers between devices  195 us (43%)
  local copies, waits for them, and re-layouts  104 us (23%)
  matrix products  92.9 us (20%)
  other arithmetic  28.5 us (6%)
  starting transfers between devices  18.6 us (4%)
  between operations  8.12 us (2%)
    all_to_all x2, waiting for transfers between devices, local_whole(): back = lax.all_to_all(cleaned, AXES, 0, 0, tiled=True)  106 us
    all_to_all x2, waiting for transfers between devices, local_whole(): slices = lax.all_to_all(spectra, AXES, 0, 0, tiled=True)  89.6 us
    convert_element_type x6, local copies, waits for them, and re-layouts, owned_frequency(): values = matrix.astype(jnp.float32)  61.7 us
    dot_general x16, matrix products, multiply(): jnp.einsum('fmk,fkn->fmn', left_side, right_side, preferred_element_type=...  54.8 us
    dot_general x2, matrix products, local_whole(): jnp.einsum('ct,srt->csr', forward[rows], wavefield, preferred_element_typ...  25.8 us
    reshape x2, local copies, waits for them, and re-layouts, local_whole(): returned.append(back.reshape(width, src_rows, rcv_cols))  18.9 us
    reshape x2, local copies, waits for them, and re-layouts, local_whole(): spectra = spectra.reshape(devices, 2, src_rows, rcv_cols)  17.5 us
    convert_element_type x2, other arithmetic, owned_frequency(): (0.5 * (values + jnp.swapaxes(values, 1, 2))).astype(jnp.bfloat16)  16.2 us
  transfers between devices with their start and end apart: 4, of which 4 were waited for; matrix products, arithmetic and copies ran while one was open for 40% of the time, Pallas kernels for 0%

profile of v1, /device:TPU:0, one launch (start us, length us, event | category | flops | bytes accessed | tf_op | source)
XLA Modules:
  0.0 446.9 jit_solution(2060891212202533321)
XLA Ops:
  1.1 12.9 %convolution_convert_fusion.1 = bf16[64,256,128]{2,0,1:T(8,128)(2,1)} fusion(bf16[64,256,1]{1,0,2:T(8,128)(2,1)S(1)} %reshape.372, bf16[256,128,256]{2,1,0:T(8,128)(2,1)} %param.2), kind=kOutput, calls=%fused_computation.25 | convolution fusion | flops 1075838976 | bytes 21004288 | tf_op jit(solution)/shard_map/ct,srt->csr/dot_general | solution.py:131
  14.0 9.0 %copy.48 = bf16[32,2,256,128]{3,2,1,0:T(8,128)(2,1)} copy(bf16[32,2,256,128]{3,1,0,2:T(2,128)(2,1)} %bitcast.145) | data formatting | bytes 8388608 | tf_op jit(solution)/shard_map/reshape | solution.py:134
  23.0 7.7 %all-to-all-start.2 = ((bf16[32,2,256,128]{3,2,1,0:T(8,128)(2,1)}), bf16[32,2,256,128]{3,2,1,0:T(8,128)(2,1)}, u32[]{:S(2)}, u32[]{:S(2)}) async-start(bf16[32,2,256,128]{3,2,1,0:T(8,128)(2,1)} %copy.48), calls=%async_computation.2 | async-start | bytes 8388608 | tf_op jit(solution)/shard_map/all_to_all | solution.py:135
  30.8 12.9 %convolution_convert_fusion.2 = bf16[64,256,128]{2,0,1:T(8,128)(2,1)} fusion(bf16[64,256,1]{1,0,2:T(8,128)(2,1)S(1)} %reshape.371, bf16[256,128,256]{2,1,0:T(8,128)(2,1)} %param.2), kind=kOutput, calls=%fused_computation.26 | convolution fusion | flops 1075838976 | bytes 21004288 | tf_op jit(solution)/shard_map/ct,srt->csr/dot_general | solution.py:131
  43.7 8.5 %copy.42 = bf16[32,2,256,128]{3,1,2,0:T(2,128)(2,1)} copy(bf16[32,2,256,128]{3,1,0,2:T(2,128)(2,1)} %bitcast.146) | data formatting | bytes 8388608 | tf_op jit(solution)/shard_map/reshape | solution.py:134
  52.2 74.3 %all-to-all-done.2 = bf16[32,2,256,128]{3,2,1,0:T(8,128)(2,1)} async-done(((bf16[32,2,256,128]{3,2,1,0:T(8,128)(2,1)}), bf16[32,2,256,128]{3,2,1,0:T(8,128)(2,1)}, u32[]{:S(2)}, u32[]{:S(2)}) %all-to-all-start.2) | async-done | bytes 4194336 | tf_op jit(solution)/shard_map/all_to_all | solution.py:135
  126.5 3.6 all-to-all-start
  134.1 6.7 %convert_bitcast_fusion = f32[2,4,256,8,128]{4,2,0,3,1:T(8,128)} fusion(bf16[4,8,2,256,128]{4,3,2,1,0:T(8,128)(2,1)} %bitcast.34), kind=kLoop, calls=%fused_computation.4 | loop fusion | flops 2097152 | bytes 12582912 | tf_op jit(solution)/shard_map/convert_element_type | solution.py:100
  140.8 10.0 %copy.49 = f32[2,4,256,8,128]{2,1,4,3,0:T(4,128)} copy(f32[2,4,256,8,128]{4,2,0,3,1:T(8,128)} %convert_bitcast_fusion) | data formatting | bytes 16777216 | tf_op jit(solution)/shard_map/convert_element_type | solution.py:100
  150.7 10.7 %reshape.368 = f32[2,1024,1024]{1,2,0:T(8,128)} reshape(f32[2,4,256,8,128]{2,1,4,3,0:T(4,128)} %copy.49) | data formatting | bytes 16777216 | tf_op jit(solution)/shard_map/convert_element_type | solution.py:100
  161.4 9.1 %copy.50 = f32[2,1024,1024]{2,1,0:T(8,128)} copy(f32[2,1024,1024]{1,2,0:T(8,128)} %reshape.368) | data formatting | bytes 16777216 | tf_op jit(solution)/shard_map/convert_element_type | solution.py:100
  170.6 8.1 %fusion.4 = bf16[2,1024,1024]{2,1,0:T(8,128)(2,1)S(1)} fusion(f32[2,1024,1024]{2,1,0:T(8,128)} %copy.50, f32[2,1024,1024]{1,2,0:T(8,128)} %reshape.368), kind=kLoop, calls=%fused_computation.7 | loop fusion | flops 6291456 | bytes 20971520 | tf_op jit(solution)/shard_map/convert_element_type | solution.py:101
  188.1 4.3 fusion.19
  192.4 2.5 convolution_add_fusion.1
  194.9 2.4 convolution_add_fusion
  197.3 8.7 %fusion.13 = (bf16[128,8,8,128]{3,1,2,0:T(8,128)(2,1)S(1)}, bf16[128,8,8,128]{3,1,2,0:T(8,128)(2,1)S(1)}) fusion(f32[1024,1024]{1,0:T(8,128)S(1)} %convolution_add_fusion, f32[1024,1024]{1,0:T(8,128)S(1)} %convolution_add_fusion.1, f32[1024,1024]{1,0:T(8,128)} %copy-done.2, bf16[2,1024,1024]{2,1,0:T(8,128)(2,1)S(1)} %fusion.4, f32[]{:T(128)S(6)} %mul.227, ...), kind=kOutput, calls=%fused_computation.29 | convolution fusion | flops 2170552320 | bytes 31457296 | tf_op jit(solution)/shard_map/fmk,fkn->fmn/dot_general | solution.py:39
  210.5 15.3 %all-to-all-done = bf16[32,2,256,128]{3,1,2,0:T(2,128)(2,1)} async-done(((bf16[32,2,256,128]{3,1,2,0:T(2,128)(2,1)}), bf16[32,2,256,128]{3,1,2,0:T(2,128)(2,1)}, u32[]{:S(2)}, u32[]{:S(2)}) %all-to-all-start) | async-done | bytes 4194336 | tf_op jit(solution)/shard_map/all_to_all | solution.py:135
  225.8 3.6 all-to-all-start.3
  233.4 12.3 %copy.43 = f32[4,8,2,256,128]{3,0,4,1,2:T(4,128)} copy(bf16[4,8,2,256,128]{4,2,3,1,0:T(2,128)(2,1)} %bitcast.32) | data formatting | bytes 12582912 | tf_op jit(solution)/shard_map/convert_element_type | solution.py:100
  245.7 10.8 %reshape.367 = f32[2,1024,1024]{1,2,0:T(8,128)} reshape(f32[2,4,256,8,128]{2,1,4,3,0:T(4,128)} %bitcast.144) | data formatting | bytes 16777216 | tf_op jit(solution)/shard_map/convert_element_type | solution.py:100
  256.5 8.9 %copy.44 = f32[2,1024,1024]{2,1,0:T(8,128)} copy(f32[2,1024,1024]{1,2,0:T(8,128)} %reshape.367) | data formatting | bytes 16777216 | tf_op jit(solution)/shard_map/convert_element_type | solution.py:100
  265.4 8.1 %fusion.6 = bf16[2,1024,1024]{2,1,0:T(8,128)(2,1)S(1)} fusion(f32[2,1024,1024]{2,1,0:T(8,128)} %copy.44, f32[2,1024,1024]{1,2,0:T(8,128)} %reshape.367), kind=kLoop, calls=%fused_computation.10 | loop fusion | flops 6291456 | bytes 20971520 | tf_op jit(solution)/shard_map/convert_element_type | solution.py:101
  282.9 4.3 fusion.15
  287.2 2.6 convolution_add_fusion.3
  289.8 2.4 convolution_add_fusion.2
  292.2 8.9 %fusion.11 = (bf16[128,8,8,128]{3,1,2,0:T(8,128)(2,1)S(1)}, bf16[128,8,8,128]{3,1,2,0:T(8,128)(2,1)S(1)}) fusion(f32[1024,1024]{1,0:T(8,128)S(1)} %convolution_add_fusion.2, f32[1024,1024]{1,0:T(8,128)S(1)} %convolution_add_fusion.3, f32[1024,1024]{1,0:T(8,128)} %copy-done.3, bf16[2,1024,1024]{2,1,0:T(8,128)(2,1)S(1)} %fusion.6, f32[]{:T(128)S(6)} %mul.210, ...), kind=kOutput, calls=%fused_computation.27 | convolution fusion | flops 2170552320 | bytes 31457296 | tf_op jit(solution)/shard_map/fmk,fkn->fmn/dot_general | solution.py:39
  305.8 19.4 %all-to-all-done.3 = bf16[32,2,256,128]{3,2,1,0:T(8,128)(2,1)} async-done(((bf16[32,2,256,128]{3,2,1,0:T(8,128)(2,1)}), bf16[32,2,256,128]{3,2,1,0:T(8,128)(2,1)}, u32[]{:S(2)}, u32[]{:S(2)}) %all-to-all-start.3) | async-done | bytes 4194336 | tf_op jit(solution)/shard_map/all_to_all | solution.py:148
  325.2 3.7 all-to-all-start.1
  329.0 9.5 %copy.54 = bf16[64,256,128]{0,2,1:T(8,128)(2,1)} copy(bf16[64,256,128]{2,1,0:T(8,128)(2,1)} %bitcast.31) | data formatting | bytes 8388608 | tf_op jit(solution)/shard_map/reshape | solution.py:149
  338.5 86.2 %all-to-all-done.1 = bf16[32,2,256,128]{3,2,1,0:T(8,128)(2,1)} async-done(((bf16[32,2,256,128]{3,2,1,0:T(8,128)(2,1)}), bf16[32,2,256,128]{3,2,1,0:T(8,128)(2,1)}, u32[]{:S(2)}, u32[]{:S(2)}) %all-to-all-start.1) | async-done | bytes 4194336 | tf_op jit(solution)/shard_map/all_to_all | solution.py:148
  424.7 9.5 %copy.53 = bf16[64,256,128]{0,2,1:T(8,128)(2,1)} copy(bf16[64,256,128]{2,1,0:T(8,128)(2,1)} %bitcast.15) | data formatting | bytes 8388608 | tf_op jit(solution)/shard_map/reshape | solution.py:149
  434.1 12.3 %convolution_convert_fusion = bf16[256,128,256]{2,1,0:T(8,128)(2,1)} fusion(bf16[128,256,1]{1,0,2:T(8,128)(2,1)S(1)} %reshape.373, bf16[64,256,128]{0,2,1:T(8,128)(2,1)} %copy.54, bf16[64,256,128]{0,2,1:T(8,128)(2,1)} %copy.53), kind=kOutput, calls=%fused_computation | convolution fusion | flops 2172649472 | bytes 25231360 | tf_op jit(solution)/shard_map/csr,ct->srt/dot_general | solution.py:151
  (38 shorter events, 29.8 us)
Async XLA Ops:
  23.0 103.5 %all-to-all-start.2 = ((bf16[32,2,256,128]{3,2,1,0:T(8,128)(2,1)}), bf16[32,2,256,128]{3,2,1,0:T(8,128)(2,1)}, u32[]{:S(2)}, u32[]{:S(2)}) async-start(bf16[32,2,256,128]{3,2,1,0:T(8,128)(2,1)} %copy.48), calls=%async_computation.2 | async-start | bytes 8388608 | tf_op jit(solution)/shard_map/all_to_all | solution.py:135
  52.2 77.9 %copy-start.1 = (f32[2,64]{1,0:T(2,128)S(1)}, f32[2,64]{1,0:T(2,128)}, u32[]{:S(2)}) copy-start(f32[2,64]{1,0:T(2,128)} %param.3) | copy-start | bytes 1540
  126.5 99.3 %all-to-all-start = ((bf16[32,2,256,128]{3,1,2,0:T(2,128)(2,1)}), bf16[32,2,256,128]{3,1,2,0:T(2,128)(2,1)}, u32[]{:S(2)}, u32[]{:S(2)}) async-start(bf16[32,2,256,128]{3,1,2,0:T(2,128)(2,1)} %copy.42), calls=%async_computation | async-start | bytes 8388608 | tf_op jit(solution)/shard_map/all_to_all | solution.py:135
  185.7 2.4 copy-start.2
  225.8 99.3 %all-to-all-start.3 = ((bf16[32,2,256,128]{3,2,1,0:T(8,128)(2,1)}), bf16[32,2,256,128]{3,2,1,0:T(8,128)(2,1)}, u32[]{:S(2)}, u32[]{:S(2)}) async-start(bf16[32,2,256,128]{3,2,1,0:T(8,128)(2,1)} %bitcast.147), calls=%async_computation.3 | async-start | bytes 8388608 | tf_op jit(solution)/shard_map/all_to_all | solution.py:148
  280.5 2.4 copy-start.3
  325.2 3.7 copy-start
  325.2 99.5 %all-to-all-start.1 = ((bf16[32,2,256,128]{3,2,1,0:T(8,128)(2,1)}), bf16[32,2,256,128]{3,2,1,0:T(8,128)(2,1)}, u32[]{:S(2)}, u32[]{:S(2)}) async-start(bf16[32,2,256,128]{3,2,1,0:T(8,128)(2,1)} %bitcast.148), calls=%async_computation.1 | async-start | bytes 8388608 | tf_op jit(solution)/shard_map/all_to_all | solution.py:148

commit v2 on v0

--- a/solution.py
+++ b/solution.py
@@ -1,8 +1,11 @@
+import functools
 import math
 
 import jax
 import jax.numpy as jnp
 from jax import lax
+from jax.experimental import pallas as pl
+from jax.experimental.pallas import tpu as pltpu
 from jax.sharding import PartitionSpec as P
 
 F0 = 8
@@ -49,7 +52,7 @@
     return (real_part, imag_part)
 
 
-def local(wavefield, inverse_wavelet):
+def local_sliced(wavefield, inverse_wavelet):
     src_rows, rcv_cols, samples = wavefield.shape
     count_f = inverse_wavelet.shape[1]
     groups = lax.axis_size("rcv")
@@ -93,8 +96,142 @@
     )
 
 
+NT_DIMS = (((1,), (1,)), ((), ()))
+TN_DIMS = (((0,), (0,)), ((), ()))
+
+def dft_kernel(table_ref, wave_ref, out_ref, held):
+    rows, cols, samples = wave_ref.shape
+    bins = table_ref.shape[0]
+    flat = wave_ref[...].reshape(rows * cols, samples)
+    spec = lax.dot_general(table_ref[...], flat, NT_DIMS, preferred_element_type=jnp.float32)
+    for row in range(rows):
+        held[pl.ds(row, bins, stride=rows), :] = spec[:, row * cols:(row + 1) * cols]
+    out_ref[...] = held[...].reshape(bins, rows, cols).astype(out_ref.dtype)
+
+def dft(table, wave, step=16):
+    rows, cols, samples = wave.shape
+    bins = table.shape[0]
+    return pl.pallas_call(
+        dft_kernel, grid=(rows // step,),
+        in_specs=[pl.BlockSpec((bins, samples), lambda i: (0, 0)),
+                  pl.BlockSpec((step, cols, samples), lambda i: (i, 0, 0))],
+        out_specs=pl.BlockSpec((bins, step, cols), lambda i: (0, i, 0)),
+        out_shape=jax.ShapeDtypeStruct((bins, rows, cols), jnp.bfloat16),
+        scratch_shapes=[pltpu.VMEM((bins * step, cols), jnp.float32)],
+        cost_estimate=pl.CostEstimate(flops=2 * bins * samples * rows * cols, bytes_accessed=2 * rows * cols * (samples + bins), transcendentals=0),
+        name="forward_table",
+    )(table, wave)
+
+def inverse_kernel(table_ref, *refs):
+    *coeffs, out_ref, held = refs
+    rows, cols, samples = out_ref.shape
+    start = 0
+    for ref in coeffs:
+        n = ref.shape[0]
+        held[start * rows:(start + n) * rows, :] = ref[...].astype(jnp.float32).reshape(n * rows, cols)
+        start += n
+    table = table_ref[...]
+    for row in range(rows):
+        lhs = held[pl.ds(row, start, stride=rows), :].astype(jnp.bfloat16)
+        out_ref[row] = lax.dot_general(lhs, table, TN_DIMS, preferred_element_type=jnp.float32).astype(out_ref.dtype)
+
+def inverse_t(table, coeffs, step=16):
+    bins, samples = table.shape
+    _, rows, cols = coeffs[0].shape
+    return pl.pallas_call(
+        inverse_kernel, grid=(rows // step,),
+        in_specs=[pl.BlockSpec((bins, samples), lambda i: (0, 0))] +
+                 [pl.BlockSpec((c.shape[0], step, cols), lambda i: (0, i, 0)) for c in coeffs],
+        out_specs=pl.BlockSpec((step, cols, samples), lambda i: (i, 0, 0)),
+        out_shape=jax.ShapeDtypeStruct((rows, cols, samples), jnp.bfloat16),
+        scratch_shapes=[pltpu.VMEM((bins * step, cols), jnp.float32)],
+        cost_estimate=pl.CostEstimate(flops=2 * bins * samples * rows * cols, bytes_accessed=2 * rows * cols * (samples + bins), transcendentals=0),
+        name="inverse_table",
+    )(table, *coeffs)
+
+def owner_kernel(wave_ref, recv_ref, out_ref, held, *, sources, groups):
+    _, _, rows, cols = recv_ref.shape
+    per = rows // cols
+    total = sources * rows
+    def mirror(block, carry):
+        src, half = block // per, block % per
+        for part in range(2):
+            for col in range(groups):
+                a = recv_ref[src * groups + col, part, pl.ds(pl.multiple_of(half * cols, cols), cols), :].astype(jnp.float32)
+                b = recv_ref[(col // per) * groups + block, part, (col % per) * cols:(col % per + 1) * cols, :].astype(jnp.float32)
+                held[part, pl.ds(pl.multiple_of(block * cols, cols), cols), col * cols:(col + 1) * cols] = (0.5 * (a + b.T)).astype(jnp.bfloat16)
+        return carry
+    lax.fori_loop(0, groups, mirror, 0)
+    wr, wi = wave_ref[0], wave_ref[1]
+    tr, ti = wr * wr - wi * wi, 2.0 * wr * wi
+    def dot(a, b): return jnp.dot(a, b, preferred_element_type=jnp.float32)
+    def product(src, carry):
+        sl = pl.ds(pl.multiple_of(src * rows, rows), rows)
+        mr, mi = held[0, sl, :], held[1, sl, :]
+        sr = dot(mr, held[0]) - dot(mi, held[1])
+        si = dot(mr, held[1]) + dot(mi, held[0])
+        br, bi = sr.astype(jnp.bfloat16), si.astype(jnp.bfloat16)
+        cr = dot(br, held[0]) - dot(bi, held[1])
+        ore = mr.astype(jnp.float32) - (wr * sr - wi * si) + (tr * cr)
+        oim = mi.astype(jnp.float32) - (wr * si + wi * sr) + (ti * cr)
+        ci = dot(br, held[1]) + dot(bi, held[0])
+        ore = (ore - ti * ci).astype(out_ref.dtype)
+        oim = (oim + tr * ci).astype(out_ref.dtype)
+        for col in range(groups):
+            out_ref[src * groups + col, 0] = ore[:, col * cols:(col + 1) * cols]
+            out_ref[src * groups + col, 1] = oim[:, col * cols:(col + 1) * cols]
+        return carry
+    lax.fori_loop(0, sources, product, 0)
+
+def owner(wave, recv, sources, groups):
+    devices, _, rows, cols = recv.shape
+    total = sources * rows
+    return pl.pallas_call(
+        functools.partial(owner_kernel, sources=sources, groups=groups),
+        in_specs=[pl.BlockSpec(memory_space=pltpu.SMEM), pl.BlockSpec(memory_space=pltpu.VMEM)],
+        out_specs=pl.BlockSpec(memory_space=pltpu.VMEM),
+        out_shape=jax.ShapeDtypeStruct(recv.shape, recv.dtype),
+        scratch_shapes=[pltpu.VMEM((2, total, total), jnp.bfloat16)],
+        cost_estimate=pl.CostEstimate(flops=16 * total**3, bytes_accessed=4 * recv.size, transcendentals=0),
+        compiler_params=pltpu.CompilerParams(vmem_limit_bytes=56 << 20),
+        name="owned_frequency",
+    )(wave, recv)
+
+
+AXES = ("src", "rcv")
+
+
+def local_whole(wavefield, inverse_wavelet):
+    src_rows, rcv_cols, samples = wavefield.shape
+    count_f = inverse_wavelet.shape[1]
+    sources, groups = lax.axis_size("src"), lax.axis_size("rcv")
+    devices = sources * groups
+    me = lax.axis_index(AXES)
+    forward, inverse = tables(samples, count_f, F0)
+    width = 2 * devices
+    returned = []
+    for chunk in range(count_f // devices):
+        spectra = dft(forward[chunk * width : (chunk + 1) * width], wavefield, 64)
+        spectra = spectra.reshape(devices, 2, src_rows, rcv_cols)
+        slices = lax.all_to_all(spectra, AXES, 0, 0, tiled=True)
+        wavelet = lax.dynamic_index_in_dim(
+            inverse_wavelet, chunk * devices + me, 1, keepdims=False
+        )
+        cleaned = owner(wavelet, slices, sources, groups)
+        back = lax.all_to_all(cleaned, AXES, 0, 0, tiled=True)
+        returned.append(back.reshape(width, src_rows, rcv_cols))
+    return inverse_t(inverse, returned, 16)
+
+
 def solution(mesh):
     placed = (P("src", "rcv", None), P())
+
+    def local(wavefield, inverse_wavelet):
+        devices = lax.axis_size("src") * lax.axis_size("rcv")
+        if inverse_wavelet.shape[1] % devices:
+            return local_sliced(wavefield, inverse_wavelet)
+        return local_whole(wavefield, inverse_wavelet)
+
     return jax.shard_map(
         local, mesh=mesh, in_specs=placed, out_specs=P("src", "rcv", None), check_vma=False
     )

time: 950 us -> 432 us (0.45)
  blocking collectives: 190 us -> 0 us
  matrix products: 177 us -> 0 us
  local copies, waits for them, and re-layouts: 117 us -> 2.75 us
  Pallas kernels: 0 us -> 91 us
  waiting for transfers between devices: 388 us -> 319 us
  other arithmetic: 52.3 us -> 0.36 us
  between operations: 13.9 us -> 0.1 us
  starting transfers between devices: 5.65 us -> 18.5 us
    all_gather x1 -> x0, waiting for transfers between devices: 204 us -> none  [local(): lax.all_gather(slices, 'src', axis=2, tiled=True).astype(jnp.float32)]
    all_to_all x1 -> x0, blocking collectives: 190 us -> none  [local(): lax.all_to_all(spectra, 'rcv', split_axis=0, concat_axis=3, tiled=True)]
    dot_general x10 -> x0, matrix products: 177 us -> none  [the longest x8 141 us: multiply(): jnp.einsum('fmk,fkn->fmn', left_side, right_side, preferred_element_type=...]
    all_to_all x1 -> x4, waiting for transfers between devices: 183 us -> 319 us  [the longest x2 166 us: local_whole(): back = lax.all_to_all(cleaned, AXES, 0, 0, tiled=True)]
    pallas_call x0 -> x5, Pallas kernels: none -> 91 us  [the longest x2 50 us: owner(): pl.pallas_call(functools.partial(owner_kernel, sources=sources, groups=gr...]
    convert_element_type x4 -> x0, local copies, waits for them, and re-layouts: 58.7 us -> none  [the longest x1 46.2 us: local(): lax.all_gather(slices, 'src', axis=2, tiled=True).astype(jnp.float32)]
    convert_element_type x1 -> x0, other arithmetic: 43.1 us -> none  [local(): all_rows = (0.5 * (whole + jnp.swapaxes(whole, 2, 3))).astype(jnp.bfloat16)]
    all_to_all x3 -> x0, local copies, waits for them, and re-layouts: 29.1 us -> none  [the longest x2 21.2 us: local(): lax.all_to_all(cleaned, 'rcv', split_axis=3, concat_axis=0, tiled=True)]
  transfers between devices with their start and end apart: 2 -> 4, of which waited for: 2 -> 4; matrix products, arithmetic and copies ran while one was open for 0% -> 0% of each run, Pallas kernels for 0% -> 14%
where the time goes in v2:
time: 432 us
  waiting for transfers between devices  319 us (74%)
  Pallas kernels  91 us (21%)
  starting transfers between devices  18.5 us (4%)
    all_to_all x2, waiting for transfers between devices, local_whole(): back = lax.all_to_all(cleaned, AXES, 0, 0, tiled=True)  166 us
    all_to_all x2, waiting for transfers between devices, local_whole(): slices = lax.all_to_all(spectra, AXES, 0, 0, tiled=True)  153 us
    pallas_call x2, Pallas kernels, owner(): pl.pallas_call(functools.partial(owner_kernel, sources=sources, groups=gr...  50 us
    pallas_call x2, Pallas kernels, dft(): pl.pallas_call(dft_kernel, grid=(rows // step,), in_specs=[pl.BlockSpec((...  23.5 us
    pallas_call x1, Pallas kernels, inverse_t(): pl.pallas_call(inverse_kernel, grid=(rows // step,), in_specs=[pl.BlockSp...  17.5 us
    all_to_all x2, starting transfers between devices, local_whole(): slices = lax.all_to_all(spectra, AXES, 0, 0, tiled=True)  11.2 us
  transfers between devices with their start and end apart: 4, of which 4 were waited for; matrix products, arithmetic and copies ran while one was open for 0% of the time, Pallas kernels for 14%

profile of v2, /device:TPU:0, one launch (start us, length us, event | category | flops | bytes accessed | tf_op | source)
XLA Modules:
  0.0 431.6 jit_solution(13864300184114792339)
XLA Ops:
  0.0 0.3 fusion.6
  0.4 0.6 slice.13.table_ref
  1.1 11.7 %forward_table.2 = bf16[64,256,128]{2,1,0:T(8,128)(2,1)} custom-call(bf16[64,256]{1,0:T(8,128)(2,1)} %slice.13.table_ref, bf16[256,128,256]{2,1,0:T(8,128)(2,1)} %wave_ref.3), custom_call_target="tpu_custom_call" | custom-call | flops 1073741824 | bytes 20971520 | tf_op jit(solution)/shard_map/forward_table/pallas_call | solution.py:114
  12.7 7.5 %all-to-all-start = ((bf16[32,2,256,128]{3,2,1,0:T(8,128)(2,1)}), bf16[32,2,256,128]{3,2,1,0:T(8,128)(2,1)}, u32[]{:S(2)}, u32[]{:S(2)}) async-start(bf16[32,2,256,128]{3,2,1,0:T(8,128)(2,1)} %bitcast.5), calls=%async_computation | async-start | bytes 8388608 | tf_op jit(solution)/shard_map/all_to_all | solution.py:216
  20.2 0.6 slice.15.table_ref
  20.9 11.8 %forward_table.3 = bf16[64,256,128]{2,1,0:T(8,128)(2,1)} custom-call(bf16[64,256]{1,0:T(8,128)(2,1)} %slice.15.table_ref, bf16[256,128,256]{2,1,0:T(8,128)(2,1)} %wave_ref.3), custom_call_target="tpu_custom_call" | custom-call | flops 1073741824 | bytes 20971520 | tf_op jit(solution)/shard_map/forward_table/pallas_call | solution.py:114
  32.6 83.3 %all-to-all-done.recv_ref = bf16[32,2,256,128]{3,2,1,0:T(8,128)(2,1)} async-done(((bf16[32,2,256,128]{3,2,1,0:T(8,128)(2,1)}), bf16[32,2,256,128]{3,2,1,0:T(8,128)(2,1)}, u32[]{:S(2)}, u32[]{:S(2)}) %all-to-all-start) | async-done | bytes 4194336 | tf_op jit(solution)/shard_map/all_to_all | solution.py:216
  116.0 0.0 copy-start
  116.0 3.7 all-to-all-start.2
  119.7 0.0 copy-done
  119.7 0.7 dynamic-slice_reduce_fusion
  120.4 25.0 %owned_frequency.2 = bf16[32,2,256,128]{3,2,1,0:T(8,128)(2,1)} custom-call(f32[2]{0:T(128)} %get-tuple-element.6.wave_ref, bf16[32,2,256,128]{3,2,1,0:T(8,128)(2,1)} %all-to-all-done.recv_ref), custom_call_target="tpu_custom_call" | custom-call | flops 17179869184 | bytes 8388608 | tf_op jit(solution)/shard_map/owned_frequency/pallas_call | solution.py:189
  145.5 70.0 %all-to-all-done.2.recv_ref = bf16[32,2,256,128]{3,2,1,0:T(8,128)(2,1)} async-done(((bf16[32,2,256,128]{3,2,1,0:T(8,128)(2,1)}), bf16[32,2,256,128]{3,2,1,0:T(8,128)(2,1)}, u32[]{:S(2)}, u32[]{:S(2)}) %all-to-all-start.2) | async-done | bytes 4194336 | tf_op jit(solution)/shard_map/all_to_all | solution.py:216
  215.4 3.7 all-to-all-start.1
  219.2 25.0 %owned_frequency.3 = bf16[32,2,256,128]{3,2,1,0:T(8,128)(2,1)} custom-call(f32[2]{0:T(128)} %get-tuple-element.5.wave_ref, bf16[32,2,256,128]{3,2,1,0:T(8,128)(2,1)} %all-to-all-done.2.recv_ref), custom_call_target="tpu_custom_call" | custom-call | flops 17179869184 | bytes 8388608 | tf_op jit(solution)/shard_map/owned_frequency/pallas_call | solution.py:189
  244.2 70.6 %all-to-all-done.1 = bf16[32,2,256,128]{3,2,1,0:T(8,128)(2,1)} async-done(((bf16[32,2,256,128]{3,2,1,0:T(8,128)(2,1)}), bf16[32,2,256,128]{3,2,1,0:T(8,128)(2,1)}, u32[]{:S(2)}, u32[]{:S(2)}) %all-to-all-start.1) | async-done | bytes 4194336 | tf_op jit(solution)/shard_map/all_to_all | solution.py:221
  314.8 3.6 all-to-all-start.3
  318.4 0.1 copy.3
  318.4 0.6 convert_element_type.27.table_ref
  319.1 95.0 %all-to-all-done.3 = bf16[32,2,256,128]{3,2,1,0:T(8,128)(2,1)} async-done(((bf16[32,2,256,128]{3,2,1,0:T(8,128)(2,1)}), bf16[32,2,256,128]{3,2,1,0:T(8,128)(2,1)}, u32[]{:S(2)}, u32[]{:S(2)}) %all-to-all-start.3) | async-done | bytes 4194336 | tf_op jit(solution)/shard_map/all_to_all | solution.py:221
  414.1 17.5 %inverse_table.1 = bf16[256,128,256]{2,1,0:T(8,128)(2,1)} custom-call(bf16[128,256]{1,0:T(8,128)(2,1)} %convert_element_type.27.table_ref, bf16[64,256,128]{2,1,0:T(8,128)(2,1)} %bitcast.1.refs_0_, bf16[64,256,128]{2,1,0:T(8,128)(2,1)} %bitcast.3.refs_1_), custom_call_target="tpu_custom_call" | custom-call | flops 2147483648 | bytes 25165824 | tf_op jit(solution)/shard_map/inverse_table/pallas_call | solution.py:141
  (5 shorter events, 0.1 us)
Async XLA Ops:
  12.7 103.2 %all-to-all-start = ((bf16[32,2,256,128]{3,2,1,0:T(8,128)(2,1)}), bf16[32,2,256,128]{3,2,1,0:T(8,128)(2,1)}, u32[]{:S(2)}, u32[]{:S(2)}) async-start(bf16[32,2,256,128]{3,2,1,0:T(8,128)(2,1)} %bitcast.5), calls=%async_computation | async-start | bytes 8388608 | tf_op jit(solution)/shard_map/all_to_all | solution.py:216
  116.0 3.7 copy-start
  116.0 99.5 %all-to-all-start.2 = ((bf16[32,2,256,128]{3,2,1,0:T(8,128)(2,1)}), bf16[32,2,256,128]{3,2,1,0:T(8,128)(2,1)}, u32[]{:S(2)}, u32[]{:S(2)}) async-start(bf16[32,2,256,128]{3,2,1,0:T(8,128)(2,1)} %bitcast.4), calls=%async_computation.2 | async-start | bytes 8388608 | tf_op jit(solution)/shard_map/all_to_all | solution.py:216
  215.4 99.3 %all-to-all-start.1 = ((bf16[32,2,256,128]{3,2,1,0:T(8,128)(2,1)}), bf16[32,2,256,128]{3,2,1,0:T(8,128)(2,1)}, u32[]{:S(2)}, u32[]{:S(2)}) async-start(bf16[32,2,256,128]{3,2,1,0:T(8,128)(2,1)} %owned_frequency.2), calls=%async_computation.1 | async-start | bytes 8388608 | tf_op jit(solution)/shard_map/all_to_all | solution.py:221
  314.8 99.3 %all-to-all-start.3 = ((bf16[32,2,256,128]{3,2,1,0:T(8,128)(2,1)}), bf16[32,2,256,128]{3,2,1,0:T(8,128)(2,1)}, u32[]{:S(2)}, u32[]{:S(2)}) async-start(bf16[32,2,256,128]{3,2,1,0:T(8,128)(2,1)} %owned_frequency.3), calls=%async_computation.3 | async-start | bytes 8388608 | tf_op jit(solution)/shard_map/all_to_all | solution.py:221

commit v3 on v2

--- a/solution.py
+++ b/solution.py
@@ -149,56 +149,349 @@
         name="inverse_table",
     )(table, *coeffs)
 
-def owner_kernel(wave_ref, recv_ref, out_ref, held, *, sources, groups):
-    _, _, rows, cols = recv_ref.shape
-    per = rows // cols
-    total = sources * rows
-    def mirror(block, carry):
-        src, half = block // per, block % per
-        for part in range(2):
+
+def tri(value, other, upper):
+    row = lax.broadcasted_iota(jnp.int32, value.shape, 0)
+    col = lax.broadcasted_iota(jnp.int32, value.shape, 1)
+    return jnp.where(row <= col, value, other) if upper else jnp.where(row > col, value, other)
+
+
+def diagonal(value):
+    row = lax.broadcasted_iota(jnp.int32, value.shape, 0)
+    col = lax.broadcasted_iota(jnp.int32, value.shape, 1)
+    return jnp.sum(jnp.where(row == col, value, 0.0), axis=0, keepdims=True)
+
+
+def with_diagonal(value, line):
+    row = lax.broadcasted_iota(jnp.int32, value.shape, 0)
+    col = lax.broadcasted_iota(jnp.int32, value.shape, 1)
+    return jnp.where(row == col, jnp.broadcast_to(line, value.shape), value)
+
+
+EXTRA = 8
+
+
+def fold_kernel(place_ref, whole_ref, swap_ref, *refs):
+    *hand_refs, out_ref = refs
+    count, length, cols = whole_ref.shape
+    piece = hand_refs[0].shape[1]
+    kept = length - piece
+    diagonal_device, side = place_ref[0], place_ref[1]
+
+    def each(d, carry):
+        @pl.when(diagonal_device == 1)
+        def _():
+            for half in range(2):
+                real = whole_ref[d, half * cols : (half + 1) * cols].astype(jnp.float32)
+                imag = whole_ref[d, (2 + half) * cols : (3 + half) * cols].astype(jnp.float32)
+                span = slice(half * cols, (half + 1) * cols)
+
+                @pl.when(side == half)
+                def _():
+                    mean_real = 0.5 * (real + real.T)
+                    mean_imag = 0.5 * (imag + imag.T)
+                    out_ref[d, span] = tri(mean_real, mean_imag, True).astype(out_ref.dtype)
+                    line = jnp.broadcast_to(diagonal(mean_imag), (EXTRA, cols))
+                    out_ref[d, kept:] = line.astype(out_ref.dtype)
+
+                @pl.when(side != half)
+                def _():
+                    own = imag if half else real
+                    mean = 0.5 * (own + swap_ref[d].astype(jnp.float32).T)
+                    out_ref[d, span] = mean.astype(out_ref.dtype)
+
+            for index, hand_ref in enumerate(hand_refs):
+                start = 2 * cols + index * piece
+                out_ref[d, start : start + piece] = hand_ref[d]
+
+        @pl.when(diagonal_device == 0)
+        def _():
+            out_ref[d, :kept] = whole_ref[d, :kept]
+            out_ref[d, kept:] = jnp.zeros((EXTRA, cols), out_ref.dtype)
+
+        return carry
+
+    lax.fori_loop(0, count, each, 0)
+
+
+def unfold_kernel(place_ref, folded_ref, swap_ref, *refs):
+    *hand_refs, out_ref = refs
+    count, length, cols = out_ref.shape
+    piece = hand_refs[0].shape[1]
+    kept = length - piece
+    diagonal_device, side, turn = place_ref[0], place_ref[1], place_ref[2]
+
+    def each(d, carry):
+        @pl.when(diagonal_device == 1)
+        def _():
+            for half in range(2):
+                own = folded_ref[d, half * cols : (half + 1) * cols]
+                real = slice(half * cols, (half + 1) * cols)
+                imag = slice((2 + half) * cols, (3 + half) * cols)
+
+                @pl.when(side == half)
+                def _():
+                    packed = own.astype(jnp.float32)
+                    line = folded_ref[d, kept:].astype(jnp.float32)[:1]
+                    out_ref[d, real] = tri(packed, packed.T, True).astype(out_ref.dtype)
+                    lower = with_diagonal(tri(packed, packed.T, False), line)
+                    out_ref[d, imag] = lower.astype(out_ref.dtype)
+
+                @pl.when(side != half)
+                def _():
+                    other = swap_ref[d].astype(jnp.float32).T.astype(out_ref.dtype)
+                    out_ref[d, imag if half else real] = own
+                    out_ref[d, real if half else imag] = other
+
+        @pl.when(diagonal_device == 0)
+        def _():
+            out_ref[d, :kept] = folded_ref[d, :kept]
+
+            for index, hand_ref in enumerate(hand_refs):
+
+                @pl.when(turn == index + 1)
+                def _():
+                    out_ref[d, kept:] = hand_ref[d]
+
+        return carry
+
+    lax.fori_loop(0, count, each, 0)
+
+
+def per_device(kernel, place, first, swap, hands, shape, name, step=4):
+    devices = first.shape[0]
+
+    def spec(array_shape):
+        rest = len(array_shape) - 1
+        return pl.BlockSpec((step,) + tuple(array_shape[1:]), lambda i: (i,) + (0,) * rest)
+
+    return pl.pallas_call(
+        kernel,
+        grid=(devices // step,),
+        in_specs=[pl.BlockSpec(memory_space=pltpu.SMEM)]
+        + [spec(a.shape) for a in (first, swap, *hands)],
+        out_specs=spec(shape),
+        out_shape=jax.ShapeDtypeStruct(shape, first.dtype),
+        cost_estimate=pl.CostEstimate(
+            flops=4 * first.size, bytes_accessed=8 * first.size, transcendentals=0
+        ),
+        name=name,
+    )(place, first, swap, *hands)
+
+
+def owner_kernel(wave_ref, recv_ref, out_ref, held, done, *, sources, groups, cols, fold_in, fold_out):
+    halves = groups // sources
+    rows = halves * cols
+    piece = cols // 2
+    kept = 2 * rows - piece
+
+    def at(block):
+        return pl.ds(pl.multiple_of(block * cols, cols), cols)
+
+    def load(d, start):
+        return recv_ref[d, start * cols : (start + 1) * cols].astype(jnp.float32)
+
+    def slot(turn):
+        return slice(2 * cols + (turn - 1) * piece, 2 * cols + turn * piece)
+
+    def load_kept(part, half, src, col, owner_src, turn):
+        if part == 0 or half == 0:
+            return load(src * groups + col, part * halves + half)
+        upper = recv_ref[src * groups + col, kept - piece : kept].astype(jnp.float32)
+        lower = recv_ref[owner_src * groups + col, slot(turn)].astype(jnp.float32)
+        return jnp.concatenate([upper, lower], 0)
+
+    def put(part, row, col, value):
+        held[part, at(row), at(col)] = value.astype(jnp.bfloat16)
+
+    def mirror_whole(src, carry):
+        for half in range(halves):
+            block = src * halves + half
+            for part in range(2):
+                for col in range(groups):
+                    a = load(src * groups + col, part * halves + half)
+                    b = load((col // halves) * groups + block, part * halves + col % halves)
+                    put(part, block, col, 0.5 * (a + b.T))
+        return carry
+
+    def mirror_folded(src, carry):
+        for turn in range(1, sources):
+            other = src ^ turn
+            for half in range(halves):
+                row = src * halves + half
+                for side in range(halves):
+                    col = other * halves + side
+                    for part in range(2):
+                        a = load_kept(part, half, src, col, other, turn)
+                        b = load_kept(part, side, other, row, src, turn)
+                        put(part, row, col, 0.5 * (a + b.T))
+        low, high = src * halves, src * halves + 1
+        for side in range(halves):
+            block = src * halves + side
+            d = src * groups + block
+            packed = load(d, side)
+            line = recv_ref[d, kept:].astype(jnp.float32)[:1]
+            put(0, block, block, tri(packed, packed.T, True))
+            put(1, block, block, with_diagonal(tri(packed, packed.T, False), line))
+        real = load(src * groups + high, 0)
+        imag = load(src * groups + low, 1)
+        put(0, low, high, real)
+        put(0, high, low, real.T)
+        put(1, high, low, imag)
+        put(1, low, high, imag.T)
+        return carry
+
+    lax.fori_loop(0, sources, mirror_folded if fold_in else mirror_whole, 0)
+
+    wave_real, wave_imag = wave_ref[0], wave_ref[1]
+    two_real = wave_real * wave_real - wave_imag * wave_imag
+    two_imag = 2.0 * wave_real * wave_imag
+
+    def dot(left, right):
+        return jnp.dot(left, right, preferred_element_type=jnp.float32)
+
+    def product(src, carry):
+        span = pl.ds(pl.multiple_of(src * rows, rows), rows)
+        real, imag = held[0, span, :], held[1, span, :]
+        sq_real = dot(real, held[0]) - dot(imag, held[1])
+        sq_imag = dot(real, held[1]) + dot(imag, held[0])
+        out_real = real.astype(jnp.float32) - (wave_real * sq_real - wave_imag * sq_imag)
+        out_imag = imag.astype(jnp.float32) - (wave_real * sq_imag + wave_imag * sq_real)
+        left_real, left_imag = sq_real.astype(jnp.bfloat16), sq_imag.astype(jnp.bfloat16)
+        cube_real = dot(left_real, held[0]) - dot(left_imag, held[1])
+        cube_imag = dot(left_real, held[1]) + dot(left_imag, held[0])
+        out_real = (out_real + (two_real * cube_real - two_imag * cube_imag)).astype(jnp.bfloat16)
+        out_imag = (out_imag + (two_real * cube_imag + two_imag * cube_real)).astype(jnp.bfloat16)
+        if fold_out:
+            done[0, span, :] = out_real
+            done[1, span, :] = out_imag
+        else:
             for col in range(groups):
-                a = recv_ref[src * groups + col, part, pl.ds(pl.multiple_of(half * cols, cols), cols), :].astype(jnp.float32)
-                b = recv_ref[(col // per) * groups + block, part, (col % per) * cols:(col % per + 1) * cols, :].astype(jnp.float32)
-                held[part, pl.ds(pl.multiple_of(block * cols, cols), cols), col * cols:(col + 1) * cols] = (0.5 * (a + b.T)).astype(jnp.bfloat16)
+                out_ref[src * groups + col, :rows] = out_real[:, col * cols : (col + 1) * cols]
+                out_ref[src * groups + col, rows:] = out_imag[:, col * cols : (col + 1) * cols]
         return carry
-    lax.fori_loop(0, groups, mirror, 0)
-    wr, wi = wave_ref[0], wave_ref[1]
-    tr, ti = wr * wr - wi * wi, 2.0 * wr * wi
-    def dot(a, b): return jnp.dot(a, b, preferred_element_type=jnp.float32)
-    def product(src, carry):
-        sl = pl.ds(pl.multiple_of(src * rows, rows), rows)
-        mr, mi = held[0, sl, :], held[1, sl, :]
-        sr = dot(mr, held[0]) - dot(mi, held[1])
-        si = dot(mr, held[1]) + dot(mi, held[0])
-        br, bi = sr.astype(jnp.bfloat16), si.astype(jnp.bfloat16)
-        cr = dot(br, held[0]) - dot(bi, held[1])
-        ore = mr.astype(jnp.float32) - (wr * sr - wi * si) + (tr * cr)
-        oim = mi.astype(jnp.float32) - (wr * si + wi * sr) + (ti * cr)
-        ci = dot(br, held[1]) + dot(bi, held[0])
-        ore = (ore - ti * ci).astype(out_ref.dtype)
-        oim = (oim + tr * ci).astype(out_ref.dtype)
-        for col in range(groups):
-            out_ref[src * groups + col, 0] = ore[:, col * cols:(col + 1) * cols]
-            out_ref[src * groups + col, 1] = oim[:, col * cols:(col + 1) * cols]
+
+    lax.fori_loop(0, sources, product, 0)
+    if not fold_out:
+        return
+
+    def pack(src, carry):
+        span = pl.ds(pl.multiple_of(src * rows, rows), rows)
+        for turn in range(1, sources):
+            other = src ^ turn
+            for side in range(halves):
+                col = other * halves + side
+                d = src * groups + col
+                imag = done[1, span, at(col)]
+                out_ref[d, :rows] = done[0, span, at(col)]
+                out_ref[d, rows:kept] = imag[: rows - piece]
+                out_ref[d, kept:] = jnp.zeros((EXTRA, cols), jnp.bfloat16)
+                out_ref[other * groups + col, slot(turn)] = imag[rows - piece :]
+        for side in range(halves):
+            block = src * halves + side
+            d = src * groups + block
+            real = done[0, at(block), at(block)].astype(jnp.float32)
+            imag = done[1, at(block), at(block)].astype(jnp.float32)
+            out_ref[d, side * cols : (side + 1) * cols] = tri(real, imag, True).astype(jnp.bfloat16)
+            line = jnp.broadcast_to(diagonal(imag), (EXTRA, cols))
+            out_ref[d, kept:] = line.astype(jnp.bfloat16)
+        low, high = src * halves, src * halves + 1
+        out_ref[src * groups + high, :cols] = done[0, at(low), at(high)]
+        out_ref[src * groups + low, cols : 2 * cols] = done[1, at(high), at(low)]
         return carry
-    lax.fori_loop(0, sources, product, 0)
-
-def owner(wave, recv, sources, groups):
-    devices, _, rows, cols = recv.shape
-    total = sources * rows
+
+    lax.fori_loop(0, sources, pack, 0)
+
+
+def owner(wave, recv, sources, groups, fold_in, fold_out):
+    devices, length, cols = recv.shape
+    total = groups * cols
+    whole = 2 * (total // sources)
+    out_shape = (devices, whole - cols // 2 + EXTRA if fold_out else whole, cols)
     return pl.pallas_call(
-        functools.partial(owner_kernel, sources=sources, groups=groups),
-        in_specs=[pl.BlockSpec(memory_space=pltpu.SMEM), pl.BlockSpec(memory_space=pltpu.VMEM)],
+        functools.partial(
+            owner_kernel,
+            sources=sources,
+            groups=groups,
+            cols=cols,
+            fold_in=fold_in,
+            fold_out=fold_out,
+        ),
+        in_specs=[
+            pl.BlockSpec(memory_space=pltpu.SMEM),
+            pl.BlockSpec(memory_space=pltpu.VMEM),
+        ],
         out_specs=pl.BlockSpec(memory_space=pltpu.VMEM),
-        out_shape=jax.ShapeDtypeStruct(recv.shape, recv.dtype),
-        scratch_shapes=[pltpu.VMEM((2, total, total), jnp.bfloat16)],
-        cost_estimate=pl.CostEstimate(flops=16 * total**3, bytes_accessed=4 * recv.size, transcendentals=0),
+        out_shape=jax.ShapeDtypeStruct(out_shape, recv.dtype),
+        scratch_shapes=[
+            pltpu.VMEM((2, total, total), jnp.bfloat16),
+            pltpu.VMEM((2, total, total) if fold_out else (2, 16, 128), jnp.bfloat16),
+        ],
+        cost_estimate=pl.CostEstimate(
+            flops=16 * total**3, bytes_accessed=4 * recv.size, transcendentals=0
+        ),
         compiler_params=pltpu.CompilerParams(vmem_limit_bytes=56 << 20),
         name="owned_frequency",
     )(wave, recv)
 
 
 AXES = ("src", "rcv")
+
+
+def swap_pairs(sources, groups):
+    halves = groups // sources
+    return [
+        (src * groups + src * halves + side, src * groups + src * halves + 1 - side)
+        for src in range(sources)
+        for side in range(halves)
+    ]
+
+
+def hand_pairs(sources, groups, turn, back):
+    pairs = []
+    for col in range(groups):
+        src = col // (groups // sources)
+        pair = ((src ^ turn) * groups + col, src * groups + col)
+        pairs.append(pair[::-1] if back else pair)
+    return pairs
+
+
+def where_am_i(sources, groups):
+    halves = groups // sources
+    src, col = lax.axis_index("src"), lax.axis_index("rcv")
+    turn = src ^ (col // halves)
+    return turn, col % halves
+
+
+def fold(spectra, sources, groups):
+    devices, length, cols = spectra.shape
+    piece = cols // 2
+    turn, side = where_am_i(sources, groups)
+    block = lax.dynamic_slice_in_dim(spectra, jnp.where(side == 0, 1, 2) * cols, cols, 1)
+    swap = lax.ppermute(block, AXES, swap_pairs(sources, groups))
+    last = spectra[:, length - piece :]
+    hands = [
+        lax.ppermute(last, AXES, hand_pairs(sources, groups, t, False)) for t in range(1, sources)
+    ]
+    place = jnp.stack([(turn == 0).astype(jnp.int32), side, turn]).astype(jnp.int32)
+    shape = (devices, length - piece + EXTRA, cols)
+    return per_device(fold_kernel, place, spectra, swap, hands, shape, "fold")
+
+
+def unfold(folded, sources, groups):
+    devices, length, cols = folded.shape
+    piece = cols // 2
+    turn, side = where_am_i(sources, groups)
+    block = lax.dynamic_slice_in_dim(folded, (1 - side) * cols, cols, 1)
+    swap = lax.ppermute(block, AXES, swap_pairs(sources, groups))
+    hands = []
+    for t in range(1, sources):
+        start = 2 * cols + (t - 1) * piece
+        pairs = hand_pairs(sources, groups, t, True)
+        hands.append(lax.ppermute(folded[:, start : start + piece], AXES, pairs))
+    place = jnp.stack([(turn == 0).astype(jnp.int32), side, turn]).astype(jnp.int32)
+    shape = (devices, length - EXTRA + piece, cols)
+    return per_device(unfold_kernel, place, folded, swap, hands, shape, "unfold")
 
 
 def local_whole(wavefield, inverse_wavelet):
@@ -209,16 +502,22 @@
     me = lax.axis_index(AXES)
     forward, inverse = tables(samples, count_f, F0)
     width = 2 * devices
+    chunks = count_f // devices
     returned = []
-    for chunk in range(count_f // devices):
+    for chunk in range(chunks):
+        fold_in, fold_out = chunk > 0, chunk < chunks - 1
         spectra = dft(forward[chunk * width : (chunk + 1) * width], wavefield, 64)
-        spectra = spectra.reshape(devices, 2, src_rows, rcv_cols)
+        spectra = spectra.reshape(devices, 2 * src_rows, rcv_cols)
+        if fold_in:
+            spectra = fold(spectra, sources, groups)
         slices = lax.all_to_all(spectra, AXES, 0, 0, tiled=True)
         wavelet = lax.dynamic_index_in_dim(
             inverse_wavelet, chunk * devices + me, 1, keepdims=False
         )
-        cleaned = owner(wavelet, slices, sources, groups)
+        cleaned = owner(wavelet, slices, sources, groups, fold_in, fold_out)
         back = lax.all_to_all(cleaned, AXES, 0, 0, tiled=True)
+        if fold_out:
+            back = unfold(back, sources, groups)
         returned.append(back.reshape(width, src_rows, rcv_cols))
     return inverse_t(inverse, returned, 16)
 
@@ -227,10 +526,11 @@
     placed = (P("src", "rcv", None), P())
 
     def local(wavefield, inverse_wavelet):
-        devices = lax.axis_size("src") * lax.axis_size("rcv")
-        if inverse_wavelet.shape[1] % devices:
-            return local_sliced(wavefield, inverse_wavelet)
-        return local_whole(wavefield, inverse_wavelet)
+        sources, groups = lax.axis_size("src"), lax.axis_size("rcv")
+        fits = inverse_wavelet.shape[1] % (sources * groups) == 0
+        if fits and sources == 4 and groups == 2 * sources:
+            return local_whole(wavefield, inverse_wavelet)
+        return local_sliced(wavefield, inverse_wavelet)
 
     return jax.shard_map(
         local, mesh=mesh, in_specs=placed, out_specs=P("src", "rcv", None), check_vma=False

time: 432 us -> 413 us (0.956)
  waiting for transfers between devices: 319 us -> 251 us
  Pallas kernels: 91 us -> 113 us
  starting transfers between devices: 18.5 us -> 35.6 us
  local copies, waits for them, and re-layouts: 2.75 us -> 10.9 us
    all_to_all x2, waiting for transfers between devices: 166 us -> 90.2 us  [local_whole(): back = lax.all_to_all(cleaned, AXES, 0, 0, tiled=True)]
    ppermute x0 -> x8, waiting for transfers between devices: none -> 71.9 us  [the longest x3 27.2 us: unfold(): hands.append(lax.ppermute(folded[:, start:start + piece], AXES, pairs))]
    all_to_all x2, waiting for transfers between devices: 153 us -> 88.6 us  [local_whole(): slices = lax.all_to_all(spectra, AXES, 0, 0, tiled=True)]
    pallas_call x0 -> x2, Pallas kernels: none -> 21.2 us  [per_device(): pl.pallas_call(kernel, grid=(devices // step,), in_specs=[pl.BlockSpec(me...]
    ppermute x0 -> x8, starting transfers between devices: none -> 17.2 us  [the longest x3 6.28 us: unfold(): hands.append(lax.ppermute(folded[:, start:start + piece], AXES, pairs))]
  transfers between devices with their start and end apart: 4 -> 12, of which waited for: 4 -> 10; matrix products, arithmetic and copies ran while one was open for 0% -> 2% of each run, Pallas kernels for 14% -> 20%
where the time goes in v3:
time: 413 us; the launch traced here: 412 us
  waiting for transfers between devices  251 us (61%)
  Pallas kernels  113 us (27%)
  starting transfers between devices  35.6 us (9%)
  local copies, waits for them, and re-layouts  10.9 us (3%)
    all_to_all x2, waiting for transfers between devices, local_whole(): back = lax.all_to_all(cleaned, AXES, 0, 0, tiled=True)  90.2 us
    all_to_all x2, waiting for transfers between devices, local_whole(): slices = lax.all_to_all(spectra, AXES, 0, 0, tiled=True)  88.6 us
    pallas_call x2, Pallas kernels, owner(): pl.pallas_call(functools.partial(owner_kernel, sources=sources, groups=gr...  51 us
    ppermute x3, waiting for transfers between devices, unfold(): hands.append(lax.ppermute(folded[:, start:start + piece], AXES, pairs))  27.2 us
    pallas_call x2, Pallas kernels, dft(): pl.pallas_call(dft_kernel, grid=(rows // step,), in_specs=[pl.BlockSpec((...  23.5 us
    pallas_call x2, Pallas kernels, per_device(): pl.pallas_call(kernel, grid=(devices // step,), in_specs=[pl.BlockSpec(me...  21.2 us
    ppermute x3, waiting for transfers between devices, fold(): lax.ppermute(last, AXES, hand_pairs(sources, groups, t, False))  20.7 us
    pallas_call x1, Pallas kernels, inverse_t(): pl.pallas_call(inverse_kernel, grid=(rows // step,), in_specs=[pl.BlockSp...  17.5 us
  transfers between devices with their start and end apart: 12, of which 10 were waited for; matrix products, arithmetic and copies ran while one was open for 2% of the time, Pallas kernels for 20%

profile of v3, /device:TPU:0, one launch (start us, length us, event | category | flops | bytes accessed | tf_op | source)
XLA Modules:
  0.0 411.6 jit_solution(13132033699265815045)
XLA Ops:
  1.1 11.7 %forward_table.2 = bf16[64,256,128]{2,1,0:T(8,128)(2,1)} custom-call(bf16[64,256]{1,0:T(8,128)(2,1)} %slice.25.table_ref, bf16[256,128,256]{2,1,0:T(8,128)(2,1)} %wave_ref.3), custom_call_target="tpu_custom_call" | custom-call | flops 1073741824 | bytes 20971520 | tf_op jit(solution)/shard_map/forward_table/pallas_call | solution.py:114
  12.8 7.5 %all-to-all-start = ((bf16[32,512,128]{2,1,0:T(8,128)(2,1)}), bf16[32,512,128]{2,1,0:T(8,128)(2,1)}, u32[]{:S(2)}, u32[]{:S(2)}) async-start(bf16[32,512,128]{2,1,0:T(8,128)(2,1)} %bitcast.10), calls=%async_computation | async-start | bytes 8388608 | tf_op jit(solution)/shard_map/all_to_all | solution.py:513
  20.9 11.8 %forward_table.3 = bf16[64,256,128]{2,1,0:T(8,128)(2,1)} custom-call(bf16[64,256]{1,0:T(8,128)(2,1)} %slice.30.table_ref, bf16[256,128,256]{2,1,0:T(8,128)(2,1)} %wave_ref.3), custom_call_target="tpu_custom_call" | custom-call | flops 1073741824 | bytes 20971520 | tf_op jit(solution)/shard_map/forward_table/pallas_call | solution.py:114
  32.7 1.3 constant_dynamic-slice_fusion
  34.0 3.6 collective-permute-start.4
  38.7 1.3 collective-permute-start.7
  40.0 1.3 collective-permute-start.6
  41.3 1.3 collective-permute-start.5
  43.3 18.2 %collective-permute-done.7.refs_2_ = bf16[32,64,128]{2,1,0:T(8,128)(2,1)S(1)} collective-permute-done((bf16[32,64,128]{2,1,0:T(8,128)(2,1)S(1)}, bf16[32,64,128]{2,1,0:T(8,128)(2,1)S(1)}, u32[]{:S(2)}, u32[]{:S(2)}) %collective-permute-start.7) | collective-permute-done | bytes 524320 | tf_op jit(solution)/shard_map/ppermute | solution.py:474
  61.5 2.5 collective-permute-done.6.refs_1_
  64.0 10.8 %collective-permute-done.4.swap_ref = bf16[32,128,128]{2,1,0:T(8,128)(2,1)S(1)} collective-permute-done((bf16[32,128,128]{2,1,0:T(8,128)(2,1)S(1)}, bf16[32,128,128]{2,1,0:T(8,128)(2,1)S(1)}, u32[]{:S(2)}, u32[]{:S(2)}) %collective-permute-start.4) | collective-permute-done | bytes 1048608 | tf_op jit(solution)/shard_map/ppermute | solution.py:471
  75.8 10.8 %fold.1 = bf16[32,456,128]{2,1,0:T(8,128)(2,1)} custom-call(s32[3]{0:T(128)} %pad_add_fusion.place_ref, bf16[32,512,128]{2,1,0:T(8,128)(2,1)} %bitcast.9, bf16[32,128,128]{2,1,0:T(8,128)(2,1)} %copy-done, bf16[32,64,128]{2,1,0:T(8,128)(2,1)} %collective-permute-done.5.refs_0_, bf16[32,64,128]{2,1,0:T(8,128)(2,1)} %collective-permute-done.6.refs_1_, ...), custom_call_target="tpu_custom_call" | custom-call | flops 8388608 | bytes 16777216 | tf_op jit(solution)/shard_map/fold/pallas_call | solution.py:268
  86.6 29.4 %all-to-all-done.recv_ref = bf16[32,512,128]{2,1,0:T(8,128)(2,1)} async-done(((bf16[32,512,128]{2,1,0:T(8,128)(2,1)}), bf16[32,512,128]{2,1,0:T(8,128)(2,1)}, u32[]{:S(2)}, u32[]{:S(2)}) %all-to-all-start) | async-done | bytes 4194336 | tf_op jit(solution)/shard_map/all_to_all | solution.py:513
  116.0 3.6 all-to-all-start.2
  120.4 25.8 %owned_frequency.2 = bf16[32,456,128]{2,1,0:T(8,128)(2,1)} custom-call(f32[2]{0:T(128)} %get-tuple-element.6.wave_ref, bf16[32,512,128]{2,1,0:T(8,128)(2,1)} %all-to-all-done.recv_ref), custom_call_target="tpu_custom_call" | custom-call | flops 17179869184 | bytes 8388608 | tf_op jit(solution)/shard_map/owned_frequency/pallas_call | solution.py:411
  146.2 59.2 %all-to-all-done.2.recv_ref = bf16[32,456,128]{2,1,0:T(8,128)(2,1)} async-done(((bf16[32,456,128]{2,1,0:T(8,128)(2,1)}), bf16[32,456,128]{2,1,0:T(8,128)(2,1)}, u32[]{:S(2)}, u32[]{:S(2)}) %all-to-all-start.2) | async-done | bytes 3735584 | tf_op jit(solution)/shard_map/all_to_all | solution.py:513
  205.4 3.7 all-to-all-start.1
  209.1 25.2 %owned_frequency.3 = bf16[32,512,128]{2,1,0:T(8,128)(2,1)} custom-call(f32[2]{0:T(128)} %get-tuple-element.5.wave_ref, bf16[32,456,128]{2,1,0:T(8,128)(2,1)} %all-to-all-done.2.recv_ref), custom_call_target="tpu_custom_call" | custom-call | flops 17179869184 | bytes 7471104 | tf_op jit(solution)/shard_map/owned_frequency/pallas_call | solution.py:411
  234.3 60.4 %all-to-all-done.1.folded_ref = bf16[32,456,128]{2,1,0:T(8,128)(2,1)} async-done(((bf16[32,456,128]{2,1,0:T(8,128)(2,1)}), bf16[32,456,128]{2,1,0:T(8,128)(2,1)}, u32[]{:S(2)}, u32[]{:S(2)}) %all-to-all-start.1) | async-done | bytes 3735584 | tf_op jit(solution)/shard_map/all_to_all | solution.py:518
  294.7 3.6 all-to-all-start.3
  298.3 1.3 constant_dynamic-slice_fusion.1
  299.6 3.5 collective-permute-start
  303.1 2.3 fusion.7
  305.4 2.1 collective-permute-start.3
  307.6 2.1 collective-permute-start.2
  309.7 2.1 collective-permute-start.1
  312.5 19.0 %collective-permute-done.3.refs_2_ = bf16[32,64,128]{2,1,0:T(8,128)(2,1)} collective-permute-done((bf16[32,64,128]{2,1,0:T(8,128)(2,1)}, bf16[32,64,128]{2,1,0:T(8,128)(2,1)}, u32[]{:S(2)}, u32[]{:S(2)}) %collective-permute-start.3) | collective-permute-done | bytes 524320 | tf_op jit(solution)/shard_map/ppermute | solution.py:491
  331.4 8.3 %collective-permute-done.2.refs_1_ = bf16[32,64,128]{2,1,0:T(8,128)(2,1)} collective-permute-done((bf16[32,64,128]{2,1,0:T(8,128)(2,1)S(1)}, bf16[32,64,128]{2,1,0:T(8,128)(2,1)}, u32[]{:S(2)}, u32[]{:S(2)}) %collective-permute-start.2) | collective-permute-done | bytes 524320 | tf_op jit(solution)/shard_map/ppermute | solution.py:491
  339.7 13.1 %collective-permute-done.swap_ref = bf16[32,128,128]{2,1,0:T(8,128)(2,1)S(1)} collective-permute-done((bf16[32,128,128]{2,1,0:T(8,128)(2,1)S(1)}, bf16[32,128,128]{2,1,0:T(8,128)(2,1)S(1)}, u32[]{:S(2)}, u32[]{:S(2)}) %collective-permute-start) | collective-permute-done | bytes 1048608 | tf_op jit(solution)/shard_map/ppermute | solution.py:486
  353.9 10.5 %unfold.1 = bf16[32,512,128]{2,1,0:T(8,128)(2,1)} custom-call(s32[3]{0:T(128)} %pad_add_fusion.place_ref, bf16[32,456,128]{2,1,0:T(8,128)(2,1)} %all-to-all-done.1.folded_ref, bf16[32,128,128]{2,1,0:T(8,128)(2,1)} %copy-done.1, bf16[32,64,128]{2,1,0:T(8,128)(2,1)} %collective-permute-done.1.refs_0_, bf16[32,64,128]{2,1,0:T(8,128)(2,1)} %collective-permute-done.2.refs_1_, ...), custom_call_target="tpu_custom_call" | custom-call | flops 7471104 | bytes 14942208 | tf_op jit(solution)/shard_map/unfold/pallas_call | solution.py:268
  364.3 29.7 %all-to-all-done.3 = bf16[32,512,128]{2,1,0:T(8,128)(2,1)} async-done(((bf16[32,512,128]{2,1,0:T(8,128)(2,1)}), bf16[32,512,128]{2,1,0:T(8,128)(2,1)}, u32[]{:S(2)}, u32[]{:S(2)}) %all-to-all-start.3) | async-done | bytes 4194336 | tf_op jit(solution)/shard_map/all_to_all | solution.py:518
  394.1 17.5 %inverse_table.1 = bf16[256,128,256]{2,1,0:T(8,128)(2,1)} custom-call(bf16[128,256]{1,0:T(8,128)(2,1)} %convert_element_type.29.table_ref, bf16[64,256,128]{2,1,0:T(8,128)(2,1)} %bitcast.11, bf16[64,256,128]{2,1,0:T(8,128)(2,1)} %bitcast.6.refs_1_), custom_call_target="tpu_custom_call" | custom-call | flops 2147483648 | bytes 25165824 | tf_op jit(solution)/shard_map/inverse_table/pallas_call | solution.py:141
  (23 shorter events, 7.0 us)
Async XLA Ops:
  12.8 103.3 %all-to-all-start = ((bf16[32,512,128]{2,1,0:T(8,128)(2,1)}), bf16[32,512,128]{2,1,0:T(8,128)(2,1)}, u32[]{:S(2)}, u32[]{:S(2)}) async-start(bf16[32,512,128]{2,1,0:T(8,128)(2,1)} %bitcast.10), calls=%async_computation | async-start | bytes 8388608 | tf_op jit(solution)/shard_map/all_to_all | solution.py:513
  34.0 40.8 %collective-permute-start.4 = (bf16[32,128,128]{2,1,0:T(8,128)(2,1)S(1)}, bf16[32,128,128]{2,1,0:T(8,128)(2,1)S(1)}, u32[]{:S(2)}, u32[]{:S(2)}) collective-permute-start(bf16[32,128,128]{2,1,0:T(8,128)(2,1)S(1)} %constant_dynamic-slice_fusion), channel_id=1, source_target_pairs={{0,1},{1,0},{10,11},{11,10},{20,21},{21,20},{30,31},{31,30}} | collective-permute-start | bytes 3145736 | tf_op jit(solution)/shard_map/ppermute | solution.py:471
  38.7 22.8 %collective-permute-start.7 = (bf16[32,64,128]{2,1,0:T(8,128)(2,1)S(1)}, bf16[32,64,128]{2,1,0:T(8,128)(2,1)S(1)}, u32[]{:S(2)}, u32[]{:S(2)}) collective-permute-start(bf16[32,64,128]{2,1,0:T(8,128)(2,1)S(1)} %slice.37), channel_id=1, source_target_pairs={{24,0},{25,1},{18,10},{19,11},{12,20},{13,21},{6,30},{7,31}} | collective-permute-start | bytes 1572872 | tf_op jit(solution)/shard_map/ppermute | solution.py:474
  40.0 24.0 %collective-permute-start.6 = (bf16[32,64,128]{2,1,0:T(8,128)(2,1)S(1)}, bf16[32,64,128]{2,1,0:T(8,128)(2,1)}, u32[]{:S(2)}, u32[]{:S(2)}) collective-permute-start(bf16[32,64,128]{2,1,0:T(8,128)(2,1)S(1)} %slice.37), channel_id=1, source_target_pairs={{16,0},{17,1},{26,10},{27,11},{4,20},{5,21},{14,30},{15,31}} | collective-permute-start | bytes 1572872 | tf_op jit(solution)/shard_map/ppermute | solution.py:474
  41.3 22.7 %collective-permute-start.5 = (bf16[32,64,128]{2,1,0:T(8,128)(2,1)S(1)}, bf16[32,64,128]{2,1,0:T(8,128)(2,1)}, u32[]{:S(2)}, u32[]{:S(2)}) collective-permute-start(bf16[32,64,128]{2,1,0:T(8,128)(2,1)S(1)} %slice.37), channel_id=1, source_target_pairs={{8,0},{9,1},{2,10},{3,11},{28,20},{29,21},{22,30},{23,31}} | collective-permute-start | bytes 1572872 | tf_op jit(solution)/shard_map/ppermute | solution.py:474
  61.5 13.3 %copy-start.2 = (bf16[32,64,128]{2,1,0:T(8,128)(2,1)}, bf16[32,64,128]{2,1,0:T(8,128)(2,1)S(1)}, u32[]{:S(2)}) copy-start(bf16[32,64,128]{2,1,0:T(8,128)(2,1)S(1)} %collective-permute-done.7.refs_2_) | copy-start | bytes 1572868
  74.8 1.0 copy-start
  86.6 33.0 %copy-start.3 = (f32[2,64]{1,0:T(2,128)S(1)}, f32[2,64]{1,0:T(2,128)}, u32[]{:S(2)}) copy-start(f32[2,64]{1,0:T(2,128)} %param.3) | copy-start | bytes 1540
  116.0 89.4 %all-to-all-start.2 = ((bf16[32,456,128]{2,1,0:T(8,128)(2,1)}), bf16[32,456,128]{2,1,0:T(8,128)(2,1)}, u32[]{:S(2)}, u32[]{:S(2)}) async-start(bf16[32,456,128]{2,1,0:T(8,128)(2,1)} %fold.1), calls=%async_computation.2 | async-start | bytes 7471104 | tf_op jit(solution)/shard_map/all_to_all | solution.py:513
  205.4 89.3 %all-to-all-start.1 = ((bf16[32,456,128]{2,1,0:T(8,128)(2,1)}), bf16[32,456,128]{2,1,0:T(8,128)(2,1)}, u32[]{:S(2)}, u32[]{:S(2)}) async-start(bf16[32,456,128]{2,1,0:T(8,128)(2,1)} %owned_frequency.2), calls=%async_computation.1 | async-start | bytes 7471104 | tf_op jit(solution)/shard_map/all_to_all | solution.py:518
  294.7 99.3 %all-to-all-start.3 = ((bf16[32,512,128]{2,1,0:T(8,128)(2,1)}), bf16[32,512,128]{2,1,0:T(8,128)(2,1)}, u32[]{:S(2)}, u32[]{:S(2)}) async-start(bf16[32,512,128]{2,1,0:T(8,128)(2,1)} %owned_frequency.3), calls=%async_computation.3 | async-start | bytes 8388608 | tf_op jit(solution)/shard_map/all_to_all | solution.py:518
  299.6 53.2 %collective-permute-start = (bf16[32,128,128]{2,1,0:T(8,128)(2,1)S(1)}, bf16[32,128,128]{2,1,0:T(8,128)(2,1)S(1)}, u32[]{:S(2)}, u32[]{:S(2)}) collective-permute-start(bf16[32,128,128]{2,1,0:T(8,128)(2,1)S(1)} %constant_dynamic-slice_fusion.1), channel_id=1, source_target_pairs={{0,1},{1,0},{10,11},{11,10},{20,21},{21,20},{30,31},{31,30}} | collective-permute-start | bytes 3145736 | tf_op jit(solution)/shard_map/ppermute | solution.py:486
  305.4 26.0 %collective-permute-start.3 = (bf16[32,64,128]{2,1,0:T(8,128)(2,1)}, bf16[32,64,128]{2,1,0:T(8,128)(2,1)}, u32[]{:S(2)}, u32[]{:S(2)}) collective-permute-start(bf16[32,64,128]{2,1,0:T(8,128)(2,1)} %get-tuple-element.7), channel_id=1, source_target_pairs={{0,24},{1,25},{10,18},{11,19},{20,12},{21,13},{30,6},{31,7}} | collective-permute-start | bytes 1572872 | tf_op jit(solution)/shard_map/ppermute | solution.py:491
  307.6 32.1 %collective-permute-start.2 = (bf16[32,64,128]{2,1,0:T(8,128)(2,1)S(1)}, bf16[32,64,128]{2,1,0:T(8,128)(2,1)}, u32[]{:S(2)}, u32[]{:S(2)}) collective-permute-start(bf16[32,64,128]{2,1,0:T(8,128)(2,1)S(1)} %get-tuple-element.8), channel_id=1, source_target_pairs={{0,16},{1,17},{10,26},{11,27},{20,4},{21,5},{30,14},{31,15}} | collective-permute-start | bytes 1572872 | tf_op jit(solution)/shard_map/ppermute | solution.py:491
  309.7 30.0 %collective-permute-start.1 = (bf16[32,64,128]{2,1,0:T(8,128)(2,1)S(1)}, bf16[32,64,128]{2,1,0:T(8,128)(2,1)}, u32[]{:S(2)}, u32[]{:S(2)}) collective-permute-start(bf16[32,64,128]{2,1,0:T(8,128)(2,1)S(1)} %get-tuple-element.9), channel_id=1, source_target_pairs={{0,8},{1,9},{10,2},{11,3},{20,28},{21,29},{30,22},{31,23}} | collective-permute-start | bytes 1572872 | tf_op jit(solution)/shard_map/ppermute | solution.py:491
  352.8 1.0 copy-start.1

commit v4 on v3

--- a/solution.py
+++ b/solution.py
@@ -98,56 +98,75 @@
 
 NT_DIMS = (((1,), (1,)), ((), ()))
 TN_DIMS = (((0,), (0,)), ((), ()))
-
-def dft_kernel(table_ref, wave_ref, out_ref, held):
+EDGE = 32
+
+
+def dft_kernel(table_ref, wave_ref, out_ref, *, group):
     rows, cols, samples = wave_ref.shape
-    bins = table_ref.shape[0]
-    flat = wave_ref[...].reshape(rows * cols, samples)
-    spec = lax.dot_general(table_ref[...], flat, NT_DIMS, preferred_element_type=jnp.float32)
-    for row in range(rows):
-        held[pl.ds(row, bins, stride=rows), :] = spec[:, row * cols:(row + 1) * cols]
-    out_ref[...] = held[...].reshape(bins, rows, cols).astype(out_ref.dtype)
-
-def dft(table, wave, step=16):
-    rows, cols, samples = wave.shape
+    for first in range(0, rows, group):
+        flat = wave_ref[first : first + group].reshape(group * cols, samples)
+        values = lax.dot_general(flat, table_ref[...], NT_DIMS, preferred_element_type=jnp.float32)
+        turned = [values[row * cols : (row + 1) * cols].T for row in range(group)]
+        stacked = jnp.swapaxes(jnp.stack(turned, 0), 0, 1)
+        out_ref[:, first : first + group, :] = stacked.astype(out_ref.dtype)
+
+
+def dft(table, wave, start, count, step):
+    _, cols, samples = wave.shape
     bins = table.shape[0]
+    skip = start // step
     return pl.pallas_call(
-        dft_kernel, grid=(rows // step,),
-        in_specs=[pl.BlockSpec((bins, samples), lambda i: (0, 0)),
-                  pl.BlockSpec((step, cols, samples), lambda i: (i, 0, 0))],
+        functools.partial(dft_kernel, group=16),
+        grid=(count // step,),
+        in_specs=[
+            pl.BlockSpec((bins, samples), lambda i: (0, 0)),
+            pl.BlockSpec((step, cols, samples), lambda i: (i + skip, 0, 0)),
+        ],
         out_specs=pl.BlockSpec((bins, step, cols), lambda i: (0, i, 0)),
-        out_shape=jax.ShapeDtypeStruct((bins, rows, cols), jnp.bfloat16),
-        scratch_shapes=[pltpu.VMEM((bins * step, cols), jnp.float32)],
-        cost_estimate=pl.CostEstimate(flops=2 * bins * samples * rows * cols, bytes_accessed=2 * rows * cols * (samples + bins), transcendentals=0),
+        out_shape=jax.ShapeDtypeStruct((bins, count, cols), jnp.bfloat16),
+        cost_estimate=pl.CostEstimate(
+            flops=2 * bins * samples * count * cols,
+            bytes_accessed=2 * count * cols * (samples + bins),
+            transcendentals=0,
+        ),
         name="forward_table",
     )(table, wave)
 
-def inverse_kernel(table_ref, *refs):
-    *coeffs, out_ref, held = refs
-    rows, cols, samples = out_ref.shape
-    start = 0
-    for ref in coeffs:
-        n = ref.shape[0]
-        held[start * rows:(start + n) * rows, :] = ref[...].astype(jnp.float32).reshape(n * rows, cols)
-        start += n
+
+def inverse_kernel(table_ref, first_ref, last_ref, *refs):
+    out_ref = refs[-1]
     table = table_ref[...]
-    for row in range(rows):
-        lhs = held[pl.ds(row, start, stride=rows), :].astype(jnp.bfloat16)
-        out_ref[row] = lax.dot_general(lhs, table, TN_DIMS, preferred_element_type=jnp.float32).astype(out_ref.dtype)
-
-def inverse_t(table, coeffs, step=16):
+    both = jnp.swapaxes(jnp.concatenate([first_ref[...], last_ref[...]], 0), 0, 1)
+    for row in range(out_ref.shape[0]):
+        out_ref[row] = lax.dot_general(
+            both[row], table, TN_DIMS, preferred_element_type=jnp.float32
+        ).astype(out_ref.dtype)
+
+
+def inverse_rows(table, first, last, start, step, prior=None):
     bins, samples = table.shape
-    _, rows, cols = coeffs[0].shape
+    half, total, cols = first.shape
+    count = last.shape[1]
+    skip = start // step
     return pl.pallas_call(
-        inverse_kernel, grid=(rows // step,),
-        in_specs=[pl.BlockSpec((bins, samples), lambda i: (0, 0))] +
-                 [pl.BlockSpec((c.shape[0], step, cols), lambda i: (0, i, 0)) for c in coeffs],
-        out_specs=pl.BlockSpec((step, cols, samples), lambda i: (i, 0, 0)),
-        out_shape=jax.ShapeDtypeStruct((rows, cols, samples), jnp.bfloat16),
-        scratch_shapes=[pltpu.VMEM((bins * step, cols), jnp.float32)],
-        cost_estimate=pl.CostEstimate(flops=2 * bins * samples * rows * cols, bytes_accessed=2 * rows * cols * (samples + bins), transcendentals=0),
+        inverse_kernel,
+        grid=(count // step,),
+        in_specs=[
+            pl.BlockSpec((bins, samples), lambda i: (0, 0)),
+            pl.BlockSpec((half, step, cols), lambda i: (0, i + skip, 0)),
+            pl.BlockSpec((bins - half, step, cols), lambda i: (0, i, 0)),
+        ]
+        + ([] if prior is None else [pl.BlockSpec(memory_space=pl.ANY)]),
+        out_specs=pl.BlockSpec((step, cols, samples), lambda i: (i + skip, 0, 0)),
+        out_shape=jax.ShapeDtypeStruct((total, cols, samples), jnp.bfloat16),
+        input_output_aliases={} if prior is None else {3: 0},
+        cost_estimate=pl.CostEstimate(
+            flops=2 * bins * samples * count * cols,
+            bytes_accessed=2 * count * cols * (samples + bins),
+            transcendentals=0,
+        ),
         name="inverse_table",
-    )(table, *coeffs)
+    )(table, first, last, *([] if prior is None else [prior]))
 
 
 def tri(value, other, upper):
@@ -279,7 +298,9 @@
     )(place, first, swap, *hands)
 
 
-def owner_kernel(wave_ref, recv_ref, out_ref, held, done, *, sources, groups, cols, fold_in, fold_out):
+def owner_kernel(wave_ref, recv_ref, *refs, sources, groups, cols, fold_in, fold_out):
+    out_refs, (held, done) = refs[:-2], refs[-2:]
+    out_ref = out_refs[0]
     halves = groups // sources
     rows = halves * cols
     piece = cols // 2
@@ -366,9 +387,13 @@
             done[0, span, :] = out_real
             done[1, span, :] = out_imag
         else:
+            top = out_refs[0].shape[1] // 2
             for col in range(groups):
-                out_ref[src * groups + col, :rows] = out_real[:, col * cols : (col + 1) * cols]
-                out_ref[src * groups + col, rows:] = out_imag[:, col * cols : (col + 1) * cols]
+                for part, value in enumerate((out_real, out_imag)):
+                    tile = value[:, col * cols : (col + 1) * cols]
+                    d = src * groups + col
+                    out_refs[0][d, part * top : (part + 1) * top] = tile[:top]
+                    out_refs[1][d, part * (rows - top) : (part + 1) * (rows - top)] = tile[top:]
         return carry
 
     lax.fori_loop(0, sources, product, 0)
@@ -404,10 +429,10 @@
 
 
 def owner(wave, recv, sources, groups, fold_in, fold_out):
-    devices, length, cols = recv.shape
+    devices, _, cols = recv.shape
     total = groups * cols
     whole = 2 * (total // sources)
-    out_shape = (devices, whole - cols // 2 + EXTRA if fold_out else whole, cols)
+    lengths = [whole - cols // 2 + EXTRA] if fold_out else [whole - 2 * EDGE, 2 * EDGE]
     return pl.pallas_call(
         functools.partial(
             owner_kernel,
@@ -421,14 +446,16 @@
             pl.BlockSpec(memory_space=pltpu.SMEM),
             pl.BlockSpec(memory_space=pltpu.VMEM),
         ],
-        out_specs=pl.BlockSpec(memory_space=pltpu.VMEM),
-        out_shape=jax.ShapeDtypeStruct(out_shape, recv.dtype),
+        out_specs=[pl.BlockSpec(memory_space=pltpu.VMEM)] * len(lengths),
+        out_shape=[jax.ShapeDtypeStruct((devices, n, cols), recv.dtype) for n in lengths],
         scratch_shapes=[
             pltpu.VMEM((2, total, total), jnp.bfloat16),
             pltpu.VMEM((2, total, total) if fold_out else (2, 16, 128), jnp.bfloat16),
         ],
         cost_estimate=pl.CostEstimate(
-            flops=16 * total**3, bytes_accessed=4 * recv.size, transcendentals=0
+            flops=16 * total**3,
+            bytes_accessed=8 * devices * whole * cols,
+            transcendentals=0,
         ),
         compiler_params=pltpu.CompilerParams(vmem_limit_bytes=56 << 20),
         name="owned_frequency",
@@ -494,6 +521,10 @@
     return per_device(unfold_kernel, place, folded, swap, hands, shape, "unfold")
 
 
+def exchange(array):
+    return lax.all_to_all(array, AXES, 0, 0, tiled=True)
+
+
 def local_whole(wavefield, inverse_wavelet):
     src_rows, rcv_cols, samples = wavefield.shape
     count_f = inverse_wavelet.shape[1]
@@ -502,24 +533,26 @@
     me = lax.axis_index(AXES)
     forward, inverse = tables(samples, count_f, F0)
     width = 2 * devices
-    chunks = count_f // devices
-    returned = []
-    for chunk in range(chunks):
-        fold_in, fold_out = chunk > 0, chunk < chunks - 1
-        spectra = dft(forward[chunk * width : (chunk + 1) * width], wavefield, 64)
-        spectra = spectra.reshape(devices, 2 * src_rows, rcv_cols)
-        if fold_in:
-            spectra = fold(spectra, sources, groups)
-        slices = lax.all_to_all(spectra, AXES, 0, 0, tiled=True)
-        wavelet = lax.dynamic_index_in_dim(
-            inverse_wavelet, chunk * devices + me, 1, keepdims=False
-        )
-        cleaned = owner(wavelet, slices, sources, groups, fold_in, fold_out)
-        back = lax.all_to_all(cleaned, AXES, 0, 0, tiled=True)
-        if fold_out:
-            back = unfold(back, sources, groups)
-        returned.append(back.reshape(width, src_rows, rcv_cols))
-    return inverse_t(inverse, returned, 16)
+    wavelets = [
+        lax.dynamic_index_in_dim(inverse_wavelet, start + me, 1, keepdims=False)
+        for start in range(0, count_f, devices)
+    ]
+
+    def spectra(chunk, start, count, step):
+        rows = dft(forward[chunk * width : (chunk + 1) * width], wavefield, start, count, step)
+        return rows.reshape(devices, 2 * count, rcv_cols)
+
+    plain = exchange(spectra(0, 0, src_rows, 2 * EDGE))
+    folded = exchange(fold(spectra(1, 0, src_rows, 2 * EDGE), sources, groups))
+    (cleaned,) = owner(wavelets[0], plain, sources, groups, False, True)
+    first = unfold(exchange(cleaned), sources, groups).reshape(width, src_rows, rcv_cols)
+    most, rest = owner(wavelets[1], folded, sources, groups, True, False)
+    most, rest, first = lax.optimization_barrier((exchange(most), rest, first))
+    rest = exchange(rest)
+    most = most.reshape(width, src_rows - EDGE, rcv_cols)
+    rest = rest.reshape(width, EDGE, rcv_cols)
+    out = inverse_rows(inverse, first, most, 0, EDGE)
+    return inverse_rows(inverse, first, rest, src_rows - EDGE, EDGE, out)
 
 
 def solution(mesh):
@@ -527,7 +560,7 @@
 
     def local(wavefield, inverse_wavelet):
         sources, groups = lax.axis_size("src"), lax.axis_size("rcv")
-        fits = inverse_wavelet.shape[1] % (sources * groups) == 0
+        fits = inverse_wavelet.shape[1] == 2 * sources * groups
         if fits and sources == 4 and groups == 2 * sources:
             return local_whole(wavefield, inverse_wavelet)
         return local_sliced(wavefield, inverse_wavelet)

time: 413 us -> 406 us (0.983)
  Pallas kernels: 113 us -> 108 us
    pallas_call x3 -> x4, Pallas kernels: 41 us -> 36.2 us  [the longest x2 21.1 us: dft(): pl.pallas_call(functools.partial(dft_kernel, group=16), grid=(count // st...]
    all_to_all x4 -> x5, starting transfers between devices: 18.3 us -> 20.9 us  [exchange(): return lax.all_to_all(array, AXES, 0, 0, tiled=True)]
    all_to_all x4 -> x5, waiting for transfers between devices: 179 us -> 176 us  [exchange(): return lax.all_to_all(array, AXES, 0, 0, tiled=True)]
  transfers between devices with their start and end apart: 12 -> 13, of which waited for: 10 -> 11; matrix products, arithmetic and copies ran while one was open for 2% -> 2% of each run, Pallas kernels for 20% -> 23%
where the time goes in v4:
time: 406 us; the launch traced here: 404 us
  waiting for transfers between devices  248 us (61%)
  Pallas kernels  108 us (27%)
  starting transfers between devices  35.9 us (9%)
  local copies, waits for them, and re-layouts  10.8 us (3%)
    all_to_all x5, waiting for transfers between devices, exchange(): return lax.all_to_all(array, AXES, 0, 0, tiled=True)  176 us
    pallas_call x2, Pallas kernels, owner(): pl.pallas_call(functools.partial(owner_kernel, sources=sources, groups=gr...  50.9 us
    ppermute x3, waiting for transfers between devices, unfold(): hands.append(lax.ppermute(folded[:, start:start + piece], AXES, pairs))  29 us
    ppermute x3, waiting for transfers between devices, fold(): lax.ppermute(last, AXES, hand_pairs(sources, groups, t, False))  21.9 us
    pallas_call x2, Pallas kernels, per_device(): pl.pallas_call(kernel, grid=(devices // step,), in_specs=[pl.BlockSpec(me...  21.2 us
    pallas_call x2, Pallas kernels, dft(): pl.pallas_call(functools.partial(dft_kernel, group=16), grid=(count // st...  21.1 us
    all_to_all x5, starting transfers between devices, exchange(): return lax.all_to_all(array, AXES, 0, 0, tiled=True)  20.9 us
    pallas_call x2, Pallas kernels, inverse_rows(): pl.pallas_call(inverse_kernel, grid=(count // step,), in_specs=[pl.BlockS...  15.1 us
  transfers between devices with their start and end apart: 13, of which 11 were waited for; matrix products, arithmetic and copies ran while one was open for 2% of the time, Pallas kernels for 23%

profile of v4, /device:TPU:0, one launch (start us, length us, event | category | flops | bytes accessed | tf_op | source)
XLA Modules:
  0.0 404.4 jit_solution(15099883751161339127)
XLA Ops:
  1.1 10.5 %forward_table.3 = bf16[64,256,128]{2,1,0:T(8,128)(2,1)} custom-call(bf16[64,256]{1,0:T(8,128)(2,1)} %slice.28.table_ref, bf16[256,128,256]{2,1,0:T(8,128)(2,1)} %wave_ref.3), custom_call_target="tpu_custom_call" | custom-call | flops 1073741824 | bytes 20971520 | tf_op jit(solution)/shard_map/forward_table/pallas_call | solution.py:118
  11.5 7.5 %all-to-all-start.2 = ((bf16[32,512,128]{2,1,0:T(8,128)(2,1)}), bf16[32,512,128]{2,1,0:T(8,128)(2,1)}, u32[]{:S(2)}, u32[]{:S(2)}) async-start(bf16[32,512,128]{2,1,0:T(8,128)(2,1)} %bitcast.13), calls=%async_computation.2 | async-start | bytes 8388608 | tf_op jit(solution)/shard_map/all_to_all | solution.py:525
  19.7 10.6 %forward_table.2 = bf16[64,256,128]{2,1,0:T(8,128)(2,1)} custom-call(bf16[64,256]{1,0:T(8,128)(2,1)} %slice.25.table_ref, bf16[256,128,256]{2,1,0:T(8,128)(2,1)} %wave_ref.3), custom_call_target="tpu_custom_call" | custom-call | flops 1073741824 | bytes 20971520 | tf_op jit(solution)/shard_map/forward_table/pallas_call | solution.py:118
  30.3 1.3 constant_dynamic-slice_fusion.1
  31.6 3.6 collective-permute-start
  36.4 1.3 collective-permute-start.3
  40.9 21.0 %collective-permute-done.3.refs_2_ = bf16[32,64,128]{2,1,0:T(8,128)(2,1)S(1)} collective-permute-done((bf16[32,64,128]{2,1,0:T(8,128)(2,1)S(1)}, bf16[32,64,128]{2,1,0:T(8,128)(2,1)S(1)}, u32[]{:S(2)}, u32[]{:S(2)}) %collective-permute-start.3) | collective-permute-done | bytes 524320 | tf_op jit(solution)/shard_map/ppermute | solution.py:501
  62.8 10.8 %collective-permute-done.swap_ref = bf16[32,128,128]{2,1,0:T(8,128)(2,1)S(1)} collective-permute-done((bf16[32,128,128]{2,1,0:T(8,128)(2,1)S(1)}, bf16[32,128,128]{2,1,0:T(8,128)(2,1)S(1)}, u32[]{:S(2)}, u32[]{:S(2)}) %collective-permute-start) | collective-permute-done | bytes 1048608 | tf_op jit(solution)/shard_map/ppermute | solution.py:498
  74.6 10.8 %fold.1 = bf16[32,456,128]{2,1,0:T(8,128)(2,1)} custom-call(s32[3]{0:T(128)} %pad_add_fusion.place_ref, bf16[32,512,128]{2,1,0:T(8,128)(2,1)} %bitcast.12, bf16[32,128,128]{2,1,0:T(8,128)(2,1)} %copy-done.1, bf16[32,64,128]{2,1,0:T(8,128)(2,1)} %collective-permute-done.1.refs_0_, bf16[32,64,128]{2,1,0:T(8,128)(2,1)} %collective-permute-done.2.refs_1_, ...), custom_call_target="tpu_custom_call" | custom-call | flops 8388608 | bytes 16777216 | tf_op jit(solution)/shard_map/fold/pallas_call | solution.py:287
  85.3 29.5 %all-to-all-done.2.recv_ref = bf16[32,512,128]{2,1,0:T(8,128)(2,1)} async-done(((bf16[32,512,128]{2,1,0:T(8,128)(2,1)}), bf16[32,512,128]{2,1,0:T(8,128)(2,1)}, u32[]{:S(2)}, u32[]{:S(2)}) %all-to-all-start.2) | async-done | bytes 4194336 | tf_op jit(solution)/shard_map/all_to_all | solution.py:525
  114.8 3.6 all-to-all-start
  119.2 25.9 %owned_frequency.3 = bf16[32,456,128]{2,1,0:T(8,128)(2,1)} custom-call(f32[2]{0:T(128)} %get-tuple-element.15.wave_ref, bf16[32,512,128]{2,1,0:T(8,128)(2,1)} %all-to-all-done.2.recv_ref), custom_call_target="tpu_custom_call" | custom-call | flops 17179869184 | bytes 16777216 | tf_op jit(solution)/shard_map/owned_frequency/pallas_call | solution.py:436
  145.1 59.1 %all-to-all-done.recv_ref = bf16[32,456,128]{2,1,0:T(8,128)(2,1)} async-done(((bf16[32,456,128]{2,1,0:T(8,128)(2,1)}), bf16[32,456,128]{2,1,0:T(8,128)(2,1)}, u32[]{:S(2)}, u32[]{:S(2)}) %all-to-all-start) | async-done | bytes 3735584 | tf_op jit(solution)/shard_map/all_to_all | solution.py:525
  204.2 3.8 all-to-all-start.3
  207.9 25.1 %owned_frequency.2 = (bf16[32,448,128]{2,1,0:T(8,128)(2,1)}, bf16[32,64,128]{2,1,0:T(8,128)(2,1)}) custom-call(f32[2]{0:T(128)} %get-tuple-element.16.wave_ref, bf16[32,456,128]{2,1,0:T(8,128)(2,1)} %all-to-all-done.recv_ref), custom_call_target="tpu_custom_call" | custom-call | flops 17179869184 | bytes 16777216 | tf_op jit(solution)/shard_map/owned_frequency/pallas_call | solution.py:436
  233.0 60.5 %all-to-all-done.3.folded_ref = bf16[32,456,128]{2,1,0:T(8,128)(2,1)} async-done(((bf16[32,456,128]{2,1,0:T(8,128)(2,1)}), bf16[32,456,128]{2,1,0:T(8,128)(2,1)}, u32[]{:S(2)}, u32[]{:S(2)}) %all-to-all-start.3) | async-done | bytes 3735584 | tf_op jit(solution)/shard_map/all_to_all | solution.py:525
  293.6 3.6 all-to-all-start.1
  297.1 1.3 constant_dynamic-slice_fusion
  298.5 3.5 collective-permute-start.4
  302.0 1.5 fusion.7
  303.5 1.3 collective-permute-start.7
  304.8 1.3 collective-permute-start.6
  306.1 1.3 collective-permute-start.5
  307.5 19.5 %collective-permute-done.7.refs_2_ = bf16[32,64,128]{2,1,0:T(8,128)(2,1)S(1)} collective-permute-done((bf16[32,64,128]{2,1,0:T(8,128)(2,1)S(1)}, bf16[32,64,128]{2,1,0:T(8,128)(2,1)S(1)}, u32[]{:S(2)}, u32[]{:S(2)}) %collective-permute-start.7) | collective-permute-done | bytes 524320 | tf_op jit(solution)/shard_map/ppermute | solution.py:518
  326.9 9.6 %collective-permute-done.6.refs_1_ = bf16[32,64,128]{2,1,0:T(8,128)(2,1)S(1)} collective-permute-done((bf16[32,64,128]{2,1,0:T(8,128)(2,1)S(1)}, bf16[32,64,128]{2,1,0:T(8,128)(2,1)S(1)}, u32[]{:S(2)}, u32[]{:S(2)}) %collective-permute-start.6) | collective-permute-done | bytes 524320 | tf_op jit(solution)/shard_map/ppermute | solution.py:518
  336.5 10.1 %collective-permute-done.4.swap_ref = bf16[32,128,128]{2,1,0:T(8,128)(2,1)S(1)} collective-permute-done((bf16[32,128,128]{2,1,0:T(8,128)(2,1)S(1)}, bf16[32,128,128]{2,1,0:T(8,128)(2,1)S(1)}, u32[]{:S(2)}, u32[]{:S(2)}) %collective-permute-start.4) | collective-permute-done | bytes 1048608 | tf_op jit(solution)/shard_map/ppermute | solution.py:513
  347.6 10.4 %unfold.1 = bf16[32,512,128]{2,1,0:T(8,128)(2,1)} custom-call(s32[3]{0:T(128)} %pad_add_fusion.place_ref, bf16[32,456,128]{2,1,0:T(8,128)(2,1)} %all-to-all-done.3.folded_ref, bf16[32,128,128]{2,1,0:T(8,128)(2,1)} %copy-done.2, bf16[32,64,128]{2,1,0:T(8,128)(2,1)} %copy-done.6, bf16[32,64,128]{2,1,0:T(8,128)(2,1)} %copy-done.5, bf16[32,64,128]{2,1,0:T(8,128)(2,1)} %copy-done.4), custom_call_target="tpu_custom_call" | custom-call | flops 7471104 | bytes 14942208 | tf_op jit(solution)/shard_map/unfold/pallas_call | solution.py:287
  358.1 23.4 %all-to-all-done.1 = bf16[32,448,128]{2,1,0:T(8,128)(2,1)} async-done(((bf16[32,448,128]{2,1,0:T(8,128)(2,1)}), bf16[32,448,128]{2,1,0:T(8,128)(2,1)}, u32[]{:S(2)}, u32[]{:S(2)}) %all-to-all-start.1) | async-done | bytes 3670048 | tf_op jit(solution)/shard_map/all_to_all | solution.py:525
  381.5 2.6 all-to-all-start.4
  384.8 11.7 %inverse_table.2.refs_0_ = bf16[256,128,256]{2,1,0:T(8,128)(2,1)} custom-call(bf16[128,256]{1,0:T(8,128)(2,1)} %convert_element_type.29.table_ref, bf16[64,256,128]{2,1,0:T(8,128)(2,1)} %bitcast.8, bf16[64,224,128]{2,1,0:T(8,128)(2,1)} %bitcast.7.last_ref), custom_call_target="tpu_custom_call" | custom-call | flops 1879048192 | bytes 22020096 | tf_op jit(solution)/shard_map/inverse_table/pallas_call | solution.py:151
  396.6 3.7 all-to-all-done.4
  401.1 3.3 inverse_table.3
  (34 shorter events, 11.1 us)
Async XLA Ops:
  11.5 103.3 %all-to-all-start.2 = ((bf16[32,512,128]{2,1,0:T(8,128)(2,1)}), bf16[32,512,128]{2,1,0:T(8,128)(2,1)}, u32[]{:S(2)}, u32[]{:S(2)}) async-start(bf16[32,512,128]{2,1,0:T(8,128)(2,1)} %bitcast.13), calls=%async_computation.2 | async-start | bytes 8388608 | tf_op jit(solution)/shard_map/all_to_all | solution.py:525
  31.6 41.9 %collective-permute-start = (bf16[32,128,128]{2,1,0:T(8,128)(2,1)S(1)}, bf16[32,128,128]{2,1,0:T(8,128)(2,1)S(1)}, u32[]{:S(2)}, u32[]{:S(2)}) collective-permute-start(bf16[32,128,128]{2,1,0:T(8,128)(2,1)S(1)} %constant_dynamic-slice_fusion.1), channel_id=1, source_target_pairs={{0,1},{1,0},{10,11},{11,10},{20,21},{21,20},{30,31},{31,30}} | collective-permute-start | bytes 3145736 | tf_op jit(solution)/shard_map/ppermute | solution.py:498
  36.4 25.6 %collective-permute-start.3 = (bf16[32,64,128]{2,1,0:T(8,128)(2,1)S(1)}, bf16[32,64,128]{2,1,0:T(8,128)(2,1)S(1)}, u32[]{:S(2)}, u32[]{:S(2)}) collective-permute-start(bf16[32,64,128]{2,1,0:T(8,128)(2,1)S(1)} %slice.33), channel_id=1, source_target_pairs={{24,0},{25,1},{18,10},{19,11},{12,20},{13,21},{6,30},{7,31}} | collective-permute-start | bytes 1572872 | tf_op jit(solution)/shard_map/ppermute | solution.py:501
  37.7 25.1 %collective-permute-start.2 = (bf16[32,64,128]{2,1,0:T(8,128)(2,1)S(1)}, bf16[32,64,128]{2,1,0:T(8,128)(2,1)}, u32[]{:S(2)}, u32[]{:S(2)}) collective-permute-start(bf16[32,64,128]{2,1,0:T(8,128)(2,1)S(1)} %slice.33), channel_id=1, source_target_pairs={{16,0},{17,1},{26,10},{27,11},{4,20},{5,21},{14,30},{15,31}} | collective-permute-start | bytes 1572872 | tf_op jit(solution)/shard_map/ppermute | solution.py:501
  39.0 23.9 %collective-permute-start.1 = (bf16[32,64,128]{2,1,0:T(8,128)(2,1)S(1)}, bf16[32,64,128]{2,1,0:T(8,128)(2,1)}, u32[]{:S(2)}, u32[]{:S(2)}) collective-permute-start(bf16[32,64,128]{2,1,0:T(8,128)(2,1)S(1)} %slice.33), channel_id=1, source_target_pairs={{8,0},{9,1},{2,10},{3,11},{28,20},{29,21},{22,30},{23,31}} | collective-permute-start | bytes 1572872 | tf_op jit(solution)/shard_map/ppermute | solution.py:501
  61.9 11.7 %copy-start.3 = (bf16[32,64,128]{2,1,0:T(8,128)(2,1)}, bf16[32,64,128]{2,1,0:T(8,128)(2,1)S(1)}, u32[]{:S(2)}) copy-start(bf16[32,64,128]{2,1,0:T(8,128)(2,1)S(1)} %collective-permute-done.3.refs_2_) | copy-start | bytes 1572868
  73.6 1.0 copy-start.1
  85.3 33.1 %copy-start.7 = (f32[2,64]{1,0:T(2,128)S(1)}, f32[2,64]{1,0:T(2,128)}, u32[]{:S(2)}) copy-start(f32[2,64]{1,0:T(2,128)} %param.3) | copy-start | bytes 1540
  114.8 89.4 %all-to-all-start = ((bf16[32,456,128]{2,1,0:T(8,128)(2,1)}), bf16[32,456,128]{2,1,0:T(8,128)(2,1)}, u32[]{:S(2)}, u32[]{:S(2)}) async-start(bf16[32,456,128]{2,1,0:T(8,128)(2,1)} %fold.1), calls=%async_computation | async-start | bytes 7471104 | tf_op jit(solution)/shard_map/all_to_all | solution.py:525
  204.2 89.4 %all-to-all-start.3 = ((bf16[32,456,128]{2,1,0:T(8,128)(2,1)}), bf16[32,456,128]{2,1,0:T(8,128)(2,1)}, u32[]{:S(2)}, u32[]{:S(2)}) async-start(bf16[32,456,128]{2,1,0:T(8,128)(2,1)} %owned_frequency.3), calls=%async_computation.3 | async-start | bytes 7471104 | tf_op jit(solution)/shard_map/all_to_all | solution.py:525
  293.6 87.9 %all-to-all-start.1 = ((bf16[32,448,128]{2,1,0:T(8,128)(2,1)}), bf16[32,448,128]{2,1,0:T(8,128)(2,1)}, u32[]{:S(2)}, u32[]{:S(2)}) async-start(bf16[32,448,128]{2,1,0:T(8,128)(2,1)} %get-tuple-element.10), calls=%async_computation.1 | async-start | bytes 7340032 | tf_op jit(solution)/shard_map/all_to_all | solution.py:525
  298.5 48.2 %collective-permute-start.4 = (bf16[32,128,128]{2,1,0:T(8,128)(2,1)S(1)}, bf16[32,128,128]{2,1,0:T(8,128)(2,1)S(1)}, u32[]{:S(2)}, u32[]{:S(2)}) collective-permute-start(bf16[32,128,128]{2,1,0:T(8,128)(2,1)S(1)} %constant_dynamic-slice_fusion), channel_id=1, source_target_pairs={{0,1},{1,0},{10,11},{11,10},{20,21},{21,20},{30,31},{31,30}} | collective-permute-start | bytes 3145736 | tf_op jit(solution)/shard_map/ppermute | solution.py:513
  303.5 23.5 %collective-permute-start.7 = (bf16[32,64,128]{2,1,0:T(8,128)(2,1)S(1)}, bf16[32,64,128]{2,1,0:T(8,128)(2,1)S(1)}, u32[]{:S(2)}, u32[]{:S(2)}) collective-permute-start(bf16[32,64,128]{2,1,0:T(8,128)(2,1)S(1)} %get-tuple-element.17), channel_id=1, source_target_pairs={{0,24},{1,25},{10,18},{11,19},{20,12},{21,13},{30,6},{31,7}} | collective-permute-start | bytes 1572872 | tf_op jit(solution)/shard_map/ppermute | solution.py:518
  304.8 31.7 %collective-permute-start.6 = (bf16[32,64,128]{2,1,0:T(8,128)(2,1)S(1)}, bf16[32,64,128]{2,1,0:T(8,128)(2,1)S(1)}, u32[]{:S(2)}, u32[]{:S(2)}) collective-permute-start(bf16[32,64,128]{2,1,0:T(8,128)(2,1)S(1)} %get-tuple-element.18), channel_id=1, source_target_pairs={{0,16},{1,17},{10,26},{11,27},{20,4},{21,5},{30,14},{31,15}} | collective-permute-start | bytes 1572872 | tf_op jit(solution)/shard_map/ppermute | solution.py:518
  306.1 30.4 %collective-permute-start.5 = (bf16[32,64,128]{2,1,0:T(8,128)(2,1)S(1)}, bf16[32,64,128]{2,1,0:T(8,128)(2,1)S(1)}, u32[]{:S(2)}, u32[]{:S(2)}) collective-permute-start(bf16[32,64,128]{2,1,0:T(8,128)(2,1)S(1)} %get-tuple-element.19), channel_id=1, source_target_pairs={{0,8},{1,9},{10,2},{11,3},{20,28},{21,29},{30,22},{31,23}} | collective-permute-start | bytes 1572872 | tf_op jit(solution)/shard_map/ppermute | solution.py:518
  326.9 19.7 %copy-start.4 = (bf16[32,64,128]{2,1,0:T(8,128)(2,1)}, bf16[32,64,128]{2,1,0:T(8,128)(2,1)S(1)}, u32[]{:S(2)}) copy-start(bf16[32,64,128]{2,1,0:T(8,128)(2,1)S(1)} %collective-permute-done.7.refs_2_) | copy-start | bytes 1572868
  336.5 10.2 %copy-start.5 = (bf16[32,64,128]{2,1,0:T(8,128)(2,1)}, bf16[32,64,128]{2,1,0:T(8,128)(2,1)S(1)}, u32[]{:S(2)}) copy-start(bf16[32,64,128]{2,1,0:T(8,128)(2,1)S(1)} %collective-permute-done.6.refs_1_) | copy-start | bytes 1572868
  336.5 10.2 %copy-start.6 = (bf16[32,64,128]{2,1,0:T(8,128)(2,1)}, bf16[32,64,128]{2,1,0:T(8,128)(2,1)S(1)}, u32[]{:S(2)}) copy-start(bf16[32,64,128]{2,1,0:T(8,128)(2,1)S(1)} %collective-permute-done.5.refs_0_) | copy-start | bytes 1572868
  346.7 1.0 copy-start.2
  381.5 18.8 %all-to-all-start.4 = ((bf16[32,64,128]{2,1,0:T(8,128)(2,1)}), bf16[32,64,128]{2,1,0:T(8,128)(2,1)S(1)}, u32[]{:S(2)}, u32[]{:S(2)}) async-start(bf16[32,64,128]{2,1,0:T(8,128)(2,1)} %get-tuple-element.13), calls=%async_computation.4 | async-start | bytes 1048576 | tf_op jit(solution)/shard_map/all_to_all | solution.py:525
  400.3 0.8 copy-start

commit v5 on v4

--- a/solution.py
+++ b/solution.py
@@ -190,19 +190,21 @@
 EXTRA = 8
 
 
-def fold_kernel(place_ref, whole_ref, swap_ref, *refs):
-    *hand_refs, out_ref = refs
+def fold_kernel(place_ref, whole_ref, swap_ref, two_ref, three_ref, last_ref, out_ref):
     count, length, cols = whole_ref.shape
-    piece = hand_refs[0].shape[1]
-    kept = length - piece
-    diagonal_device, side = place_ref[0], place_ref[1]
+    kept = out_ref.shape[1] - EXTRA
+    turn, side, lower = place_ref[0], place_ref[1], place_ref[2]
+
+    def plane(d, part, half):
+        start = (2 * part + half) * cols
+        return whole_ref[d, start : start + cols]
 
     def each(d, carry):
-        @pl.when(diagonal_device == 1)
+        @pl.when(turn == 0)
         def _():
             for half in range(2):
-                real = whole_ref[d, half * cols : (half + 1) * cols].astype(jnp.float32)
-                imag = whole_ref[d, (2 + half) * cols : (3 + half) * cols].astype(jnp.float32)
+                real = plane(d, 0, half).astype(jnp.float32)
+                imag = plane(d, 1, half).astype(jnp.float32)
                 span = slice(half * cols, (half + 1) * cols)
 
                 @pl.when(side == half)
@@ -219,11 +221,29 @@
                     mean = 0.5 * (own + swap_ref[d].astype(jnp.float32).T)
                     out_ref[d, span] = mean.astype(out_ref.dtype)
 
-            for index, hand_ref in enumerate(hand_refs):
-                start = 2 * cols + index * piece
-                out_ref[d, start : start + piece] = hand_ref[d]
-
-        @pl.when(diagonal_device == 0)
+            middle = 2 * cols + two_ref.shape[1]
+            out_ref[d, 2 * cols : middle] = two_ref[d]
+            out_ref[d, middle:kept] = three_ref[d]
+
+        @pl.when(turn == 1)
+        def _():
+            for half in range(2):
+
+                @pl.when(side == half)
+                def _():
+                    own = jnp.where(lower == 1, plane(d, 0, half), plane(d, 1, half))
+                    mean = 0.5 * (own.astype(jnp.float32) + swap_ref[d].astype(jnp.float32).T)
+                    out_ref[d, :cols] = mean.astype(out_ref.dtype)
+
+                @pl.when(side != half)
+                def _():
+                    out_ref[d, cols : 2 * cols] = plane(d, 0, half)
+                    out_ref[d, 2 * cols : 3 * cols] = plane(d, 1, half)
+
+            out_ref[d, 3 * cols : kept] = last_ref[d]
+            out_ref[d, kept:] = jnp.zeros((EXTRA, cols), out_ref.dtype)
+
+        @pl.when(turn > 1)
         def _():
             out_ref[d, :kept] = whole_ref[d, :kept]
             out_ref[d, kept:] = jnp.zeros((EXTRA, cols), out_ref.dtype)
@@ -233,15 +253,13 @@
     lax.fori_loop(0, count, each, 0)
 
 
-def unfold_kernel(place_ref, folded_ref, swap_ref, *refs):
-    *hand_refs, out_ref = refs
+def unfold_kernel(place_ref, folded_ref, swap_ref, two_ref, three_ref, last_ref, out_ref):
     count, length, cols = out_ref.shape
-    piece = hand_refs[0].shape[1]
-    kept = length - piece
-    diagonal_device, side, turn = place_ref[0], place_ref[1], place_ref[2]
+    kept = folded_ref.shape[1] - EXTRA
+    turn, side, lower = place_ref[0], place_ref[1], place_ref[2]
 
     def each(d, carry):
-        @pl.when(diagonal_device == 1)
+        @pl.when(turn == 0)
         def _():
             for half in range(2):
                 own = folded_ref[d, half * cols : (half + 1) * cols]
@@ -253,8 +271,8 @@
                     packed = own.astype(jnp.float32)
                     line = folded_ref[d, kept:].astype(jnp.float32)[:1]
                     out_ref[d, real] = tri(packed, packed.T, True).astype(out_ref.dtype)
-                    lower = with_diagonal(tri(packed, packed.T, False), line)
-                    out_ref[d, imag] = lower.astype(out_ref.dtype)
+                    below = with_diagonal(tri(packed, packed.T, False), line)
+                    out_ref[d, imag] = below.astype(out_ref.dtype)
 
                 @pl.when(side != half)
                 def _():
@@ -262,22 +280,44 @@
                     out_ref[d, imag if half else real] = own
                     out_ref[d, real if half else imag] = other
 
-        @pl.when(diagonal_device == 0)
+        @pl.when(turn == 1)
+        def _():
+            for half in range(2):
+                real = slice(half * cols, (half + 1) * cols)
+                imag = slice((2 + half) * cols, (3 + half) * cols)
+
+                @pl.when(side == half)
+                def _():
+                    own = folded_ref[d, :cols]
+                    other = swap_ref[d].astype(jnp.float32).T.astype(out_ref.dtype)
+                    out_ref[d, real] = jnp.where(lower == 1, own, other)
+                    out_ref[d, imag] = jnp.where(lower == 1, other, own)
+
+                @pl.when(side != half)
+                def _():
+                    out_ref[d, real] = folded_ref[d, cols : 2 * cols]
+                    out_ref[d, imag] = folded_ref[d, 2 * cols : 3 * cols]
+
+        @pl.when(turn > 1)
         def _():
             out_ref[d, :kept] = folded_ref[d, :kept]
 
-            for index, hand_ref in enumerate(hand_refs):
-
-                @pl.when(turn == index + 1)
-                def _():
-                    out_ref[d, kept:] = hand_ref[d]
+        @pl.when(turn == 2)
+        def _():
+            out_ref[d, kept:] = two_ref[d]
+
+        @pl.when(turn == 3)
+        def _():
+            middle = kept + three_ref.shape[1]
+            out_ref[d, kept:middle] = three_ref[d]
+            out_ref[d, middle:] = last_ref[d]
 
         return carry
 
     lax.fori_loop(0, count, each, 0)
 
 
-def per_device(kernel, place, first, swap, hands, shape, name, step=4):
+def per_device(kernel, place, first, swap, hands, shape, name, step=8):
     devices = first.shape[0]
 
     def spec(array_shape):
@@ -303,8 +343,8 @@
     out_ref = out_refs[0]
     halves = groups // sources
     rows = halves * cols
-    piece = cols // 2
-    kept = 2 * rows - piece
+    quarter = cols // 4
+    kept = 3 * cols + quarter
 
     def at(block):
         return pl.ds(pl.multiple_of(block * cols, cols), cols)
@@ -312,15 +352,22 @@
     def load(d, start):
         return recv_ref[d, start * cols : (start + 1) * cols].astype(jnp.float32)
 
-    def slot(turn):
-        return slice(2 * cols + (turn - 1) * piece, 2 * cols + turn * piece)
+    def moved(src, col, turn):
+        two, three = 2 * cols, 2 * cols + 3 * quarter
+        if turn == 2:
+            return [(src * groups + col, two, three)]
+        return [
+            (src * groups + col, three, kept),
+            ((src ^ 1) * groups + col, 3 * cols, kept),
+        ]
 
     def load_kept(part, half, src, col, owner_src, turn):
         if part == 0 or half == 0:
             return load(src * groups + col, part * halves + half)
-        upper = recv_ref[src * groups + col, kept - piece : kept].astype(jnp.float32)
-        lower = recv_ref[owner_src * groups + col, slot(turn)].astype(jnp.float32)
-        return jnp.concatenate([upper, lower], 0)
+        spans = [(src * groups + col, 3 * cols, kept)] + moved(owner_src, col, turn)
+        return jnp.concatenate(
+            [recv_ref[d, start:stop].astype(jnp.float32) for d, start, stop in spans], 0
+        )
 
     def put(part, row, col, value):
         held[part, at(row), at(col)] = value.astype(jnp.bfloat16)
@@ -336,7 +383,7 @@
         return carry
 
     def mirror_folded(src, carry):
-        for turn in range(1, sources):
+        for turn in range(2, sources):
             other = src ^ turn
             for half in range(halves):
                 row = src * halves + half
@@ -362,7 +409,30 @@
         put(1, low, high, imag.T)
         return carry
 
-    lax.fori_loop(0, sources, mirror_folded if fold_in else mirror_whole, 0)
+    def mirror_near(pair, carry):
+        low, high = 2 * pair, 2 * pair + 1
+        for half in range(halves):
+            row, col = low * halves + half, high * halves + half
+            real = load(low * groups + col, 0)
+            imag = load(high * groups + row, 0)
+            put(0, row, col, real)
+            put(0, col, row, real.T)
+            put(1, col, row, imag)
+            put(1, row, col, imag.T)
+            col = high * halves + 1 - half
+            for part in range(2):
+                a = load(low * groups + col, 1 + part)
+                b = load(high * groups + row, 1 + part)
+                mean = 0.5 * (a + b.T)
+                put(part, row, col, mean)
+                put(part, col, row, mean.T)
+        return carry
+
+    if fold_in:
+        lax.fori_loop(0, sources, mirror_folded, 0)
+        lax.fori_loop(0, sources // 2, mirror_near, 0)
+    else:
+        lax.fori_loop(0, sources, mirror_whole, 0)
 
     wave_real, wave_imag = wave_ref[0], wave_ref[1]
     two_real = wave_real * wave_real - wave_imag * wave_imag
@@ -402,16 +472,19 @@
 
     def pack(src, carry):
         span = pl.ds(pl.multiple_of(src * rows, rows), rows)
-        for turn in range(1, sources):
+        for turn in range(2, sources):
             other = src ^ turn
             for side in range(halves):
                 col = other * halves + side
                 d = src * groups + col
                 imag = done[1, span, at(col)]
                 out_ref[d, :rows] = done[0, span, at(col)]
-                out_ref[d, rows:kept] = imag[: rows - piece]
+                out_ref[d, rows:kept] = imag[: kept - rows]
                 out_ref[d, kept:] = jnp.zeros((EXTRA, cols), jnp.bfloat16)
-                out_ref[other * groups + col, slot(turn)] = imag[rows - piece :]
+                first = kept - rows
+                for place, start, stop in moved(other, col, turn):
+                    out_ref[place, start:stop] = imag[first : first + stop - start]
+                    first += stop - start
         for side in range(halves):
             block = src * halves + side
             d = src * groups + block
@@ -425,14 +498,30 @@
         out_ref[src * groups + low, cols : 2 * cols] = done[1, at(high), at(low)]
         return carry
 
+    def pack_near(pair, carry):
+        low, high = 2 * pair, 2 * pair + 1
+        for half in range(halves):
+            row, col = low * halves + half, high * halves + half
+            out_ref[low * groups + col, :cols] = done[0, at(row), at(col)]
+            out_ref[high * groups + row, :cols] = done[1, at(col), at(row)]
+            col = high * halves + 1 - half
+            for part in range(2):
+                slot = slice((1 + part) * cols, (2 + part) * cols)
+                out_ref[low * groups + col, slot] = done[part, at(row), at(col)]
+                out_ref[high * groups + row, slot] = done[part, at(col), at(row)]
+            for d in (low * groups + col, high * groups + row):
+                out_ref[d, kept:] = jnp.zeros((EXTRA, cols), jnp.bfloat16)
+        return carry
+
     lax.fori_loop(0, sources, pack, 0)
+    lax.fori_loop(0, sources // 2, pack_near, 0)
 
 
 def owner(wave, recv, sources, groups, fold_in, fold_out):
     devices, _, cols = recv.shape
     total = groups * cols
     whole = 2 * (total // sources)
-    lengths = [whole - cols // 2 + EXTRA] if fold_out else [whole - 2 * EDGE, 2 * EDGE]
+    lengths = [3 * cols + cols // 4 + EXTRA] if fold_out else [whole - 2 * EDGE, 2 * EDGE]
     return pl.pallas_call(
         functools.partial(
             owner_kernel,
@@ -467,57 +556,72 @@
 
 def swap_pairs(sources, groups):
     halves = groups // sources
+    pairs = []
+    for src in range(sources):
+        for side in range(halves):
+            here = src * groups + src * halves + side
+            pairs.append((here, src * groups + src * halves + 1 - side))
+            near = src ^ 1
+            pairs.append(
+                (near * groups + src * halves + side, src * groups + near * halves + side)
+            )
+    return pairs
+
+
+def turn_pairs(sources, groups, start, stop):
+    halves = groups // sources
     return [
-        (src * groups + src * halves + side, src * groups + src * halves + 1 - side)
-        for src in range(sources)
-        for side in range(halves)
+        ((col // halves ^ start) * groups + col, (col // halves ^ stop) * groups + col)
+        for col in range(groups)
     ]
-
-
-def hand_pairs(sources, groups, turn, back):
-    pairs = []
-    for col in range(groups):
-        src = col // (groups // sources)
-        pair = ((src ^ turn) * groups + col, src * groups + col)
-        pairs.append(pair[::-1] if back else pair)
-    return pairs
 
 
 def where_am_i(sources, groups):
     halves = groups // sources
     src, col = lax.axis_index("src"), lax.axis_index("rcv")
-    turn = src ^ (col // halves)
-    return turn, col % halves
+    turn, side = src ^ (col // halves), col % halves
+    place = jnp.stack([turn, side, (src < col // halves).astype(jnp.int32)])
+    return turn, side, place.astype(jnp.int32)
+
+
+def send_rows(array, start, stop, pairs):
+    return lax.ppermute(array[:, start:stop], AXES, pairs)
 
 
 def fold(spectra, sources, groups):
     devices, length, cols = spectra.shape
-    piece = cols // 2
-    turn, side = where_am_i(sources, groups)
-    block = lax.dynamic_slice_in_dim(spectra, jnp.where(side == 0, 1, 2) * cols, cols, 1)
+    quarter = cols // 4
+    kept = 3 * cols + quarter
+    turn, side, place = where_am_i(sources, groups)
+    diagonal_plane = jnp.where(side == 0, 1, 2)
+    near_plane = jnp.where(place[2] == 1, 2 + side, side)
+    plane = jnp.where(turn == 0, diagonal_plane, near_plane)
+    block = lax.dynamic_slice_in_dim(spectra, plane * cols, cols, 1)
     swap = lax.ppermute(block, AXES, swap_pairs(sources, groups))
-    last = spectra[:, length - piece :]
     hands = [
-        lax.ppermute(last, AXES, hand_pairs(sources, groups, t, False)) for t in range(1, sources)
+        send_rows(spectra, kept, length, turn_pairs(sources, groups, 2, 0)),
+        send_rows(spectra, kept, kept + 2 * quarter, turn_pairs(sources, groups, 3, 0)),
+        send_rows(spectra, kept + 2 * quarter, length, turn_pairs(sources, groups, 3, 1)),
     ]
-    place = jnp.stack([(turn == 0).astype(jnp.int32), side, turn]).astype(jnp.int32)
-    shape = (devices, length - piece + EXTRA, cols)
+    shape = (devices, kept + EXTRA, cols)
     return per_device(fold_kernel, place, spectra, swap, hands, shape, "fold")
 
 
 def unfold(folded, sources, groups):
     devices, length, cols = folded.shape
-    piece = cols // 2
-    turn, side = where_am_i(sources, groups)
-    block = lax.dynamic_slice_in_dim(folded, (1 - side) * cols, cols, 1)
+    quarter = cols // 4
+    kept = 3 * cols + quarter
+    middle = 2 * cols + 3 * quarter
+    turn, side, place = where_am_i(sources, groups)
+    plane = jnp.where(turn == 0, 1 - side, 0)
+    block = lax.dynamic_slice_in_dim(folded, plane * cols, cols, 1)
     swap = lax.ppermute(block, AXES, swap_pairs(sources, groups))
-    hands = []
-    for t in range(1, sources):
-        start = 2 * cols + (t - 1) * piece
-        pairs = hand_pairs(sources, groups, t, True)
-        hands.append(lax.ppermute(folded[:, start : start + piece], AXES, pairs))
-    place = jnp.stack([(turn == 0).astype(jnp.int32), side, turn]).astype(jnp.int32)
-    shape = (devices, length - EXTRA + piece, cols)
+    hands = [
+        send_rows(folded, 2 * cols, middle, turn_pairs(sources, groups, 0, 2)),
+        send_rows(folded, middle, kept, turn_pairs(sources, groups, 0, 3)),
+        send_rows(folded, 3 * cols, kept, turn_pairs(sources, groups, 1, 3)),
+    ]
+    shape = (devices, 4 * cols, cols)
     return per_device(unfold_kernel, place, folded, swap, hands, shape, "unfold")
 
 

time: 406 us -> 394 us (0.970)
  waiting for transfers between devices: 248 us -> 238 us
    ppermute x6, waiting for transfers between devices: 50.9 us -> 70 us  [send_rows(): return lax.ppermute(array[:, start:stop], AXES, pairs)]
    ppermute x1, waiting for transfers between devices: 10.8 us -> 0.77 us  [fold(): swap = lax.ppermute(block, AXES, swap_pairs(sources, groups))]
    all_to_all x5, waiting for transfers between devices: 176 us -> 167 us  [exchange(): return lax.all_to_all(array, AXES, 0, 0, tiled=True)]
    ppermute x1, waiting for transfers between devices: 10.1 us -> 0.77 us  [unfold(): swap = lax.ppermute(block, AXES, swap_pairs(sources, groups))]
  transfers between devices with their start and end apart: 13 -> 13, of which waited for: 11 -> 10; matrix products, arithmetic and copies ran while one was open for 2% -> 2% of each run, Pallas kernels for 23% -> 24%
where the time goes in v5:
time: 394 us; the launch traced here: 393 us
  waiting for transfers between devices  238 us (60%)
  Pallas kernels  107 us (27%)
  starting transfers between devices  34.4 us (9%)
  local copies, waits for them, and re-layouts  12.1 us (3%)
    all_to_all x5, waiting for transfers between devices, exchange(): return lax.all_to_all(array, AXES, 0, 0, tiled=True)  167 us
    ppermute x6, waiting for transfers between devices, send_rows(): return lax.ppermute(array[:, start:stop], AXES, pairs)  70 us
    pallas_call x2, Pallas kernels, owner(): pl.pallas_call(functools.partial(owner_kernel, sources=sources, groups=gr...  51 us
    pallas_call x2, Pallas kernels, dft(): pl.pallas_call(functools.partial(dft_kernel, group=16), grid=(count // st...  21.1 us
    pallas_call x2, Pallas kernels, per_device(): pl.pallas_call(kernel, grid=(devices // step,), in_specs=[pl.BlockSpec(me...  20.1 us
    all_to_all x5, starting transfers between devices, exchange(): return lax.all_to_all(array, AXES, 0, 0, tiled=True)  19.5 us
    pallas_call x2, Pallas kernels, inverse_rows(): pl.pallas_call(inverse_kernel, grid=(count // step,), in_specs=[pl.BlockS...  15.1 us
  transfers between devices with their start and end apart: 13, of which 10 were waited for; matrix products, arithmetic and copies ran while one was open for 2% of the time, Pallas kernels for 24%

profile of v5, /device:TPU:0, one launch (start us, length us, event | category | flops | bytes accessed | tf_op | source)
XLA Modules:
  0.0 393.2 jit_solution(5189480783353321270)
XLA Ops:
  1.1 10.5 %forward_table.3 = bf16[64,256,128]{2,1,0:T(8,128)(2,1)} custom-call(bf16[64,256]{1,0:T(8,128)(2,1)} %slice.36.table_ref, bf16[256,128,256]{2,1,0:T(8,128)(2,1)} %wave_ref.3), custom_call_target="tpu_custom_call" | custom-call | flops 1073741824 | bytes 20971520 | tf_op jit(solution)/shard_map/forward_table/pallas_call | solution.py:118
  11.5 7.4 %all-to-all-start.2 = ((bf16[32,512,128]{2,1,0:T(8,128)(2,1)}), bf16[32,512,128]{2,1,0:T(8,128)(2,1)}, u32[]{:S(2)}, u32[]{:S(2)}) async-start(bf16[32,512,128]{2,1,0:T(8,128)(2,1)} %bitcast.15), calls=%async_computation.2 | async-start | bytes 8388608 | tf_op jit(solution)/shard_map/all_to_all | solution.py:629
  19.7 10.6 %forward_table.2 = bf16[64,256,128]{2,1,0:T(8,128)(2,1)} custom-call(bf16[64,256]{1,0:T(8,128)(2,1)} %slice.31.table_ref, bf16[256,128,256]{2,1,0:T(8,128)(2,1)} %wave_ref.3), custom_call_target="tpu_custom_call" | custom-call | flops 1073741824 | bytes 20971520 | tf_op jit(solution)/shard_map/forward_table/pallas_call | solution.py:118
  30.3 1.3 constant_dynamic-slice_fusion.1
  31.6 3.6 collective-permute-start
  35.2 1.2 slice.41
  36.4 1.3 collective-permute-start.1
  37.7 1.1 slice.42
  38.8 1.3 collective-permute-start.2
  42.4 23.0 %collective-permute-done.2.three_ref = bf16[32,64,128]{2,1,0:T(8,128)(2,1)S(1)} collective-permute-done((bf16[32,64,128]{2,1,0:T(8,128)(2,1)S(1)}, bf16[32,64,128]{2,1,0:T(8,128)(2,1)S(1)}, u32[]{:S(2)}, u32[]{:S(2)}) %collective-permute-start.2) | collective-permute-done | bytes 524320 | tf_op jit(solution)/shard_map/ppermute | solution.py:588
  65.4 7.4 %collective-permute-done.1.two_ref = bf16[32,96,128]{2,1,0:T(8,128)(2,1)S(1)} collective-permute-done((bf16[32,96,128]{2,1,0:T(8,128)(2,1)S(1)}, bf16[32,96,128]{2,1,0:T(8,128)(2,1)S(1)}, u32[]{:S(2)}, u32[]{:S(2)}) %collective-permute-start.1) | collective-permute-done | bytes 786464 | tf_op jit(solution)/shard_map/ppermute | solution.py:588
  73.7 1.0 copy-done.3
  74.7 10.2 %fold.1 = bf16[32,424,128]{2,1,0:T(8,128)(2,1)} custom-call(s32[3]{0:T(128)} %pad_add_fusion.place_ref, bf16[32,512,128]{2,1,0:T(8,128)(2,1)} %bitcast.14, bf16[32,128,128]{2,1,0:T(8,128)(2,1)} %copy-done.3, bf16[32,96,128]{2,1,0:T(8,128)(2,1)} %copy-done.4, bf16[32,64,128]{2,1,0:T(8,128)(2,1)} %copy-done.5, bf16[32,32,128]{2,1,0:T(8,128)(2,1)} %copy-done.7), custom_call_target="tpu_custom_call" | custom-call | flops 8388608 | bytes 16777216 | tf_op jit(solution)/shard_map/fold/pallas_call | solution.py:327
  84.9 29.9 %all-to-all-done.2.recv_ref = bf16[32,512,128]{2,1,0:T(8,128)(2,1)} async-done(((bf16[32,512,128]{2,1,0:T(8,128)(2,1)}), bf16[32,512,128]{2,1,0:T(8,128)(2,1)}, u32[]{:S(2)}, u32[]{:S(2)}) %all-to-all-start.2) | async-done | bytes 4194336 | tf_op jit(solution)/shard_map/all_to_all | solution.py:629
  114.7 2.8 all-to-all-start
  118.3 25.7 %owned_frequency.3 = bf16[32,424,128]{2,1,0:T(8,128)(2,1)} custom-call(f32[2]{0:T(128)} %get-tuple-element.15.wave_ref, bf16[32,512,128]{2,1,0:T(8,128)(2,1)} %all-to-all-done.2.recv_ref), custom_call_target="tpu_custom_call" | custom-call | flops 17179869184 | bytes 16777216 | tf_op jit(solution)/shard_map/owned_frequency/pallas_call | solution.py:525
  144.0 53.6 %all-to-all-done.recv_ref = bf16[32,424,128]{2,1,0:T(8,128)(2,1)S(1)} async-done(((bf16[32,424,128]{2,1,0:T(8,128)(2,1)}), bf16[32,424,128]{2,1,0:T(8,128)(2,1)S(1)}, u32[]{:S(2)}, u32[]{:S(2)}) %all-to-all-start) | async-done | bytes 3473440 | tf_op jit(solution)/shard_map/all_to_all | solution.py:629
  197.6 1.7 copy-done.1
  199.4 3.0 all-to-all-start.3
  202.3 25.3 %owned_frequency.2 = (bf16[32,448,128]{2,1,0:T(8,128)(2,1)}, bf16[32,64,128]{2,1,0:T(8,128)(2,1)}) custom-call(f32[2]{0:T(128)} %get-tuple-element.16.wave_ref, bf16[32,424,128]{2,1,0:T(8,128)(2,1)} %copy-done.1), custom_call_target="tpu_custom_call" | custom-call | flops 17179869184 | bytes 16777216 | tf_op jit(solution)/shard_map/owned_frequency/pallas_call | solution.py:525
  227.6 54.6 %all-to-all-done.3.folded_ref = bf16[32,424,128]{2,1,0:T(8,128)(2,1)S(1)} async-done(((bf16[32,424,128]{2,1,0:T(8,128)(2,1)}), bf16[32,424,128]{2,1,0:T(8,128)(2,1)S(1)}, u32[]{:S(2)}, u32[]{:S(2)}) %all-to-all-start.3) | async-done | bytes 3473440 | tf_op jit(solution)/shard_map/all_to_all | solution.py:629
  282.3 3.7 all-to-all-start.1
  286.1 3.5 collective-permute-start.4
  289.7 2.6 collective-permute-start.5
  292.3 1.3 collective-permute-start.6
  294.4 39.6 %collective-permute-done.6.three_ref = bf16[32,64,128]{2,1,0:T(8,128)(2,1)S(1)} collective-permute-done((bf16[32,64,128]{2,1,0:T(8,128)(2,1)S(1)}, bf16[32,64,128]{2,1,0:T(8,128)(2,1)S(1)}, u32[]{:S(2)}, u32[]{:S(2)}) %collective-permute-start.6) | collective-permute-done | bytes 524320 | tf_op jit(solution)/shard_map/ppermute | solution.py:588
  335.6 9.9 %unfold.1 = bf16[32,512,128]{2,1,0:T(8,128)(2,1)} custom-call(s32[3]{0:T(128)} %pad_add_fusion.place_ref, bf16[32,424,128]{2,1,0:T(8,128)(2,1)} %copy-done, bf16[32,128,128]{2,1,0:T(8,128)(2,1)} %collective-permute-done.4.swap_ref, bf16[32,96,128]{2,1,0:T(8,128)(2,1)} %collective-permute-done.5.two_ref, bf16[32,64,128]{2,1,0:T(8,128)(2,1)} %copy-done.6, ...), custom_call_target="tpu_custom_call" | custom-call | flops 6946816 | bytes 13893632 | tf_op jit(solution)/shard_map/unfold/pallas_call | solution.py:327
  345.5 24.7 %all-to-all-done.1 = bf16[32,448,128]{2,1,0:T(8,128)(2,1)} async-done(((bf16[32,448,128]{2,1,0:T(8,128)(2,1)}), bf16[32,448,128]{2,1,0:T(8,128)(2,1)}, u32[]{:S(2)}, u32[]{:S(2)}) %all-to-all-start.1) | async-done | bytes 3670048 | tf_op jit(solution)/shard_map/all_to_all | solution.py:629
  370.2 2.6 all-to-all-start.4
  373.6 11.7 %inverse_table.2.refs_0_ = bf16[256,128,256]{2,1,0:T(8,128)(2,1)} custom-call(bf16[128,256]{1,0:T(8,128)(2,1)} %convert_element_type.31.table_ref, bf16[64,256,128]{2,1,0:T(8,128)(2,1)} %bitcast.8, bf16[64,224,128]{2,1,0:T(8,128)(2,1)} %bitcast.7.last_ref), custom_call_target="tpu_custom_call" | custom-call | flops 1879048192 | bytes 22020096 | tf_op jit(solution)/shard_map/inverse_table/pallas_call | solution.py:151
  385.3 3.7 all-to-all-done.4
  389.9 3.3 inverse_table.3
  (42 shorter events, 9.6 us)
Async XLA Ops:
  11.5 103.2 %all-to-all-start.2 = ((bf16[32,512,128]{2,1,0:T(8,128)(2,1)}), bf16[32,512,128]{2,1,0:T(8,128)(2,1)}, u32[]{:S(2)}, u32[]{:S(2)}) async-start(bf16[32,512,128]{2,1,0:T(8,128)(2,1)} %bitcast.15), calls=%async_computation.2 | async-start | bytes 8388608 | tf_op jit(solution)/shard_map/all_to_all | solution.py:629
  31.6 41.9 %collective-permute-start = (bf16[32,128,128]{2,1,0:T(8,128)(2,1)S(1)}, bf16[32,128,128]{2,1,0:T(8,128)(2,1)S(1)}, u32[]{:S(2)}, u32[]{:S(2)}) collective-permute-start(bf16[32,128,128]{2,1,0:T(8,128)(2,1)S(1)} %constant_dynamic-slice_fusion.1), channel_id=1, source_target_pairs={{0,1},{8,2},{1,0},{9,3},{10,11},{2,8},{11,10},{3,9},{20,21},{28,22... | collective-permute-start | bytes 3145736 | tf_op jit(solution)/shard_map/ppermute | solution.py:600
  36.4 36.3 %collective-permute-start.1 = (bf16[32,96,128]{2,1,0:T(8,128)(2,1)S(1)}, bf16[32,96,128]{2,1,0:T(8,128)(2,1)S(1)}, u32[]{:S(2)}, u32[]{:S(2)}) collective-permute-start(bf16[32,96,128]{2,1,0:T(8,128)(2,1)S(1)} %slice.41), channel_id=1, source_target_pairs={{16,0},{17,1},{26,10},{27,11},{4,20},{5,21},{14,30},{15,31}} | collective-permute-start | bytes 2359304 | tf_op jit(solution)/shard_map/ppermute | solution.py:588
  38.8 26.6 %collective-permute-start.2 = (bf16[32,64,128]{2,1,0:T(8,128)(2,1)S(1)}, bf16[32,64,128]{2,1,0:T(8,128)(2,1)S(1)}, u32[]{:S(2)}, u32[]{:S(2)}) collective-permute-start(bf16[32,64,128]{2,1,0:T(8,128)(2,1)S(1)} %slice.42), channel_id=1, source_target_pairs={{24,0},{25,1},{18,10},{19,11},{12,20},{13,21},{6,30},{7,31}} | collective-permute-start | bytes 1572872 | tf_op jit(solution)/shard_map/ppermute | solution.py:588
  41.1 1.3 collective-permute-start.3
  42.4 31.2 %copy-start.7 = (bf16[32,32,128]{2,1,0:T(8,128)(2,1)}, bf16[32,32,128]{2,1,0:T(8,128)(2,1)S(1)}, u32[]{:S(2)}) copy-start(bf16[32,32,128]{2,1,0:T(8,128)(2,1)S(1)} %collective-permute-done.3.last_ref) | copy-start | bytes 786436
  65.4 8.2 %copy-start.5 = (bf16[32,64,128]{2,1,0:T(8,128)(2,1)}, bf16[32,64,128]{2,1,0:T(8,128)(2,1)S(1)}, u32[]{:S(2)}) copy-start(bf16[32,64,128]{2,1,0:T(8,128)(2,1)S(1)} %collective-permute-done.2.three_ref) | copy-start | bytes 1572868
  72.8 0.9 copy-start.4
  73.7 1.0 copy-start.3
  84.9 32.7 %copy-start.9 = (f32[2,64]{1,0:T(2,128)S(1)}, f32[2,64]{1,0:T(2,128)}, u32[]{:S(2)}) copy-start(f32[2,64]{1,0:T(2,128)} %param.3) | copy-start | bytes 1540
  114.7 82.9 %all-to-all-start = ((bf16[32,424,128]{2,1,0:T(8,128)(2,1)}), bf16[32,424,128]{2,1,0:T(8,128)(2,1)S(1)}, u32[]{:S(2)}, u32[]{:S(2)}) async-start(bf16[32,424,128]{2,1,0:T(8,128)(2,1)} %fold.1), calls=%async_computation | async-start | bytes 6946816 | tf_op jit(solution)/shard_map/all_to_all | solution.py:629
  197.6 1.7 copy-start.1
  199.4 82.9 %all-to-all-start.3 = ((bf16[32,424,128]{2,1,0:T(8,128)(2,1)}), bf16[32,424,128]{2,1,0:T(8,128)(2,1)S(1)}, u32[]{:S(2)}, u32[]{:S(2)}) async-start(bf16[32,424,128]{2,1,0:T(8,128)(2,1)} %owned_frequency.3), calls=%async_computation.3 | async-start | bytes 6946816 | tf_op jit(solution)/shard_map/all_to_all | solution.py:629
  282.2 11.4 %copy-start = (bf16[32,424,128]{2,1,0:T(8,128)(2,1)}, bf16[32,424,128]{2,1,0:T(8,128)(2,1)S(1)}, u32[]{:S(2)}) copy-start(bf16[32,424,128]{2,1,0:T(8,128)(2,1)S(1)} %all-to-all-done.3.folded_ref) | copy-start | bytes 10420228
  282.3 88.0 %all-to-all-start.1 = ((bf16[32,448,128]{2,1,0:T(8,128)(2,1)}), bf16[32,448,128]{2,1,0:T(8,128)(2,1)}, u32[]{:S(2)}, u32[]{:S(2)}) async-start(bf16[32,448,128]{2,1,0:T(8,128)(2,1)} %get-tuple-element.10), calls=%async_computation.1 | async-start | bytes 7340032 | tf_op jit(solution)/shard_map/all_to_all | solution.py:629
  286.1 49.5 %collective-permute-start.4 = (bf16[32,128,128]{2,1,0:T(8,128)(2,1)S(1)}, bf16[32,128,128]{2,1,0:T(8,128)(2,1)}, u32[]{:S(2)}, u32[]{:S(2)}) collective-permute-start(bf16[32,128,128]{2,1,0:T(8,128)(2,1)S(1)} %constant_dynamic-slice_fusion), channel_id=1, source_target_pairs={{0,1},{8,2},{1,0},{9,3},{10,11},{2,8},{11,10},{3,9},{20,21},{28,22... | collective-permute-start | bytes 3145736 | tf_op jit(solution)/shard_map/ppermute | solution.py:618
  289.7 44.4 %collective-permute-start.5 = (bf16[32,96,128]{2,1,0:T(8,128)(2,1)S(1)}, bf16[32,96,128]{2,1,0:T(8,128)(2,1)}, u32[]{:S(2)}, u32[]{:S(2)}) collective-permute-start(bf16[32,96,128]{2,1,0:T(8,128)(2,1)S(1)} %slice.45), channel_id=1, source_target_pairs={{0,16},{1,17},{10,26},{11,27},{20,4},{21,5},{30,14},{31,15}} | collective-permute-start | bytes 2359304 | tf_op jit(solution)/shard_map/ppermute | solution.py:588
  292.3 41.7 %collective-permute-start.6 = (bf16[32,64,128]{2,1,0:T(8,128)(2,1)S(1)}, bf16[32,64,128]{2,1,0:T(8,128)(2,1)S(1)}, u32[]{:S(2)}, u32[]{:S(2)}) collective-permute-start(bf16[32,64,128]{2,1,0:T(8,128)(2,1)S(1)} %slice.46), channel_id=1, source_target_pairs={{0,24},{1,25},{10,18},{11,19},{20,12},{21,13},{30,6},{31,7}} | collective-permute-start | bytes 1572872 | tf_op jit(solution)/shard_map/ppermute | solution.py:588
  293.7 0.7 collective-permute-start.7
  294.4 41.2 %copy-start.8 = (bf16[32,32,128]{2,1,0:T(8,128)(2,1)}, bf16[32,32,128]{2,1,0:T(8,128)(2,1)S(1)}, u32[]{:S(2)}) copy-start(bf16[32,32,128]{2,1,0:T(8,128)(2,1)S(1)} %collective-permute-done.7.last_ref) | copy-start | bytes 786436
  334.0 0.8 copy-start.6
  370.2 18.8 %all-to-all-start.4 = ((bf16[32,64,128]{2,1,0:T(8,128)(2,1)}), bf16[32,64,128]{2,1,0:T(8,128)(2,1)S(1)}, u32[]{:S(2)}, u32[]{:S(2)}) async-start(bf16[32,64,128]{2,1,0:T(8,128)(2,1)} %get-tuple-element.13), calls=%async_computation.4 | async-start | bytes 1048576 | tf_op jit(solution)/shard_map/all_to_all | solution.py:629
  389.1 0.8 copy-start.2

commit v6 on v5

--- a/solution.py
+++ b/solution.py
@@ -129,6 +129,7 @@
             bytes_accessed=2 * count * cols * (samples + bins),
             transcendentals=0,
         ),
+        compiler_params=pltpu.CompilerParams(vmem_limit_bytes=56 << 20),
         name="forward_table",
     )(table, wave)
 
@@ -165,6 +166,7 @@
             bytes_accessed=2 * count * cols * (samples + bins),
             transcendentals=0,
         ),
+        compiler_params=pltpu.CompilerParams(vmem_limit_bytes=56 << 20),
         name="inverse_table",
     )(table, first, last, *([] if prior is None else [prior]))
 
@@ -646,8 +648,8 @@
         rows = dft(forward[chunk * width : (chunk + 1) * width], wavefield, start, count, step)
         return rows.reshape(devices, 2 * count, rcv_cols)
 
-    plain = exchange(spectra(0, 0, src_rows, 2 * EDGE))
-    folded = exchange(fold(spectra(1, 0, src_rows, 2 * EDGE), sources, groups))
+    plain = exchange(spectra(0, 0, src_rows, src_rows // 2))
+    folded = exchange(fold(spectra(1, 0, src_rows, src_rows // 2), sources, groups))
     (cleaned,) = owner(wavelets[0], plain, sources, groups, False, True)
     first = unfold(exchange(cleaned), sources, groups).reshape(width, src_rows, rcv_cols)
     most, rest = owner(wavelets[1], folded, sources, groups, True, False)
@@ -655,7 +657,7 @@
     rest = exchange(rest)
     most = most.reshape(width, src_rows - EDGE, rcv_cols)
     rest = rest.reshape(width, EDGE, rcv_cols)
-    out = inverse_rows(inverse, first, most, 0, EDGE)
+    out = inverse_rows(inverse, first, most, 0, (src_rows - EDGE) // 2)
     return inverse_rows(inverse, first, rest, src_rows - EDGE, EDGE, out)
 
 

time: 394 us -> 394 us (level)
  transfers between devices with their start and end apart: 13 -> 13, of which waited for: 10 -> 10; matrix products, arithmetic and copies ran while one was open for 2% -> 2% of each run, Pallas kernels for 24% -> 23%
where the time goes in v6:
time: 394 us; the launch traced here: 393 us
  waiting for transfers between devices  240 us (61%)
  Pallas kernels  104 us (26%)
  starting transfers between devices  34.7 us (9%)
  local copies, waits for them, and re-layouts  12.7 us (3%)
    all_to_all x5, waiting for transfers between devices, exchange(): return lax.all_to_all(array, AXES, 0, 0, tiled=True)  168 us
    ppermute x6, waiting for transfers between devices, send_rows(): return lax.ppermute(array[:, start:stop], AXES, pairs)  71.1 us
    pallas_call x2, Pallas kernels, owner(): pl.pallas_call(functools.partial(owner_kernel, sources=sources, groups=gr...  51 us
    pallas_call x2, Pallas kernels, per_device(): pl.pallas_call(kernel, grid=(devices // step,), in_specs=[pl.BlockSpec(me...  20.1 us
    pallas_call x2, Pallas kernels, dft(): pl.pallas_call(functools.partial(dft_kernel, group=16), grid=(count // st...  20.1 us
    all_to_all x5, starting transfers between devices, exchange(): return lax.all_to_all(array, AXES, 0, 0, tiled=True)  19.7 us
    pallas_call x2, Pallas kernels, inverse_rows(): pl.pallas_call(inverse_kernel, grid=(count // step,), in_specs=[pl.BlockS...  13.1 us
  transfers between devices with their start and end apart: 13, of which 10 were waited for; matrix products, arithmetic and copies ran while one was open for 2% of the time, Pallas kernels for 23%

profile of v6, /device:TPU:0, one launch (start us, length us, event | category | flops | bytes accessed | tf_op | source)
XLA Modules:
  0.0 392.8 jit_solution(12797963723100832313)
XLA Ops:
  1.1 10.0 %forward_table.3 = bf16[64,256,128]{2,1,0:T(8,128)(2,1)} custom-call(bf16[64,256]{1,0:T(8,128)(2,1)} %slice.36.table_ref, bf16[256,128,256]{2,1,0:T(8,128)(2,1)} %wave_ref.3), custom_call_target="tpu_custom_call" | custom-call | flops 1073741824 | bytes 20971520 | tf_op jit(solution)/shard_map/forward_table/pallas_call | solution.py:118
  11.1 7.5 %all-to-all-start.2 = ((bf16[32,512,128]{2,1,0:T(8,128)(2,1)}), bf16[32,512,128]{2,1,0:T(8,128)(2,1)}, u32[]{:S(2)}, u32[]{:S(2)}) async-start(bf16[32,512,128]{2,1,0:T(8,128)(2,1)} %bitcast.15), calls=%async_computation.2 | async-start | bytes 8388608 | tf_op jit(solution)/shard_map/all_to_all | solution.py:631
  19.2 10.1 %forward_table.2 = bf16[64,256,128]{2,1,0:T(8,128)(2,1)} custom-call(bf16[64,256]{1,0:T(8,128)(2,1)} %slice.31.table_ref, bf16[256,128,256]{2,1,0:T(8,128)(2,1)} %wave_ref.3), custom_call_target="tpu_custom_call" | custom-call | flops 1073741824 | bytes 20971520 | tf_op jit(solution)/shard_map/forward_table/pallas_call | solution.py:118
  29.3 1.3 constant_dynamic-slice_fusion.1
  30.6 3.6 collective-permute-start
  34.2 1.2 slice.41
  35.4 1.3 collective-permute-start.1
  36.7 1.1 slice.42
  37.8 1.3 collective-permute-start.2
  41.4 21.5 %collective-permute-done.2.three_ref = bf16[32,64,128]{2,1,0:T(8,128)(2,1)S(1)} collective-permute-done((bf16[32,64,128]{2,1,0:T(8,128)(2,1)S(1)}, bf16[32,64,128]{2,1,0:T(8,128)(2,1)S(1)}, u32[]{:S(2)}, u32[]{:S(2)}) %collective-permute-start.2) | collective-permute-done | bytes 524320 | tf_op jit(solution)/shard_map/ppermute | solution.py:590
  62.8 10.1 %collective-permute-done.1.two_ref = bf16[32,96,128]{2,1,0:T(8,128)(2,1)S(1)} collective-permute-done((bf16[32,96,128]{2,1,0:T(8,128)(2,1)S(1)}, bf16[32,96,128]{2,1,0:T(8,128)(2,1)S(1)}, u32[]{:S(2)}, u32[]{:S(2)}) %collective-permute-start.1) | collective-permute-done | bytes 786464 | tf_op jit(solution)/shard_map/ppermute | solution.py:590
  73.8 1.0 copy-done.3
  74.8 10.2 %fold.1 = bf16[32,424,128]{2,1,0:T(8,128)(2,1)} custom-call(s32[3]{0:T(128)} %pad_add_fusion.place_ref, bf16[32,512,128]{2,1,0:T(8,128)(2,1)} %bitcast.14, bf16[32,128,128]{2,1,0:T(8,128)(2,1)} %copy-done.3, bf16[32,96,128]{2,1,0:T(8,128)(2,1)} %copy-done.4, bf16[32,64,128]{2,1,0:T(8,128)(2,1)} %copy-done.5, bf16[32,32,128]{2,1,0:T(8,128)(2,1)} %copy-done.7), custom_call_target="tpu_custom_call" | custom-call | flops 8388608 | bytes 16777216 | tf_op jit(solution)/shard_map/fold/pallas_call | solution.py:329
  85.0 29.3 %all-to-all-done.2.recv_ref = bf16[32,512,128]{2,1,0:T(8,128)(2,1)} async-done(((bf16[32,512,128]{2,1,0:T(8,128)(2,1)}), bf16[32,512,128]{2,1,0:T(8,128)(2,1)}, u32[]{:S(2)}, u32[]{:S(2)}) %all-to-all-start.2) | async-done | bytes 4194336 | tf_op jit(solution)/shard_map/all_to_all | solution.py:631
  114.3 3.0 all-to-all-start
  118.0 25.7 %owned_frequency.3 = bf16[32,424,128]{2,1,0:T(8,128)(2,1)} custom-call(f32[2]{0:T(128)} %get-tuple-element.15.wave_ref, bf16[32,512,128]{2,1,0:T(8,128)(2,1)} %all-to-all-done.2.recv_ref), custom_call_target="tpu_custom_call" | custom-call | flops 17179869184 | bytes 16777216 | tf_op jit(solution)/shard_map/owned_frequency/pallas_call | solution.py:527
  143.7 53.4 %all-to-all-done.recv_ref = bf16[32,424,128]{2,1,0:T(8,128)(2,1)S(1)} async-done(((bf16[32,424,128]{2,1,0:T(8,128)(2,1)}), bf16[32,424,128]{2,1,0:T(8,128)(2,1)S(1)}, u32[]{:S(2)}, u32[]{:S(2)}) %all-to-all-start) | async-done | bytes 3473440 | tf_op jit(solution)/shard_map/all_to_all | solution.py:631
  197.2 1.7 copy-done.1
  198.9 2.8 all-to-all-start.3
  201.7 25.3 %owned_frequency.2 = (bf16[32,448,128]{2,1,0:T(8,128)(2,1)}, bf16[32,64,128]{2,1,0:T(8,128)(2,1)}) custom-call(f32[2]{0:T(128)} %get-tuple-element.16.wave_ref, bf16[32,424,128]{2,1,0:T(8,128)(2,1)} %copy-done.1), custom_call_target="tpu_custom_call" | custom-call | flops 17179869184 | bytes 16777216 | tf_op jit(solution)/shard_map/owned_frequency/pallas_call | solution.py:527
  227.0 54.8 %all-to-all-done.3.folded_ref = bf16[32,424,128]{2,1,0:T(8,128)(2,1)S(1)} async-done(((bf16[32,424,128]{2,1,0:T(8,128)(2,1)}), bf16[32,424,128]{2,1,0:T(8,128)(2,1)S(1)}, u32[]{:S(2)}, u32[]{:S(2)}) %all-to-all-start.3) | async-done | bytes 3473440 | tf_op jit(solution)/shard_map/all_to_all | solution.py:631
  281.8 3.7 all-to-all-start.1
  285.6 3.5 collective-permute-start.4
  289.2 2.6 collective-permute-start.5
  291.9 1.3 collective-permute-start.6
  293.9 39.6 %collective-permute-done.6.three_ref = bf16[32,64,128]{2,1,0:T(8,128)(2,1)S(1)} collective-permute-done((bf16[32,64,128]{2,1,0:T(8,128)(2,1)S(1)}, bf16[32,64,128]{2,1,0:T(8,128)(2,1)S(1)}, u32[]{:S(2)}, u32[]{:S(2)}) %collective-permute-start.6) | collective-permute-done | bytes 524320 | tf_op jit(solution)/shard_map/ppermute | solution.py:590
  335.1 9.9 %unfold.1 = bf16[32,512,128]{2,1,0:T(8,128)(2,1)} custom-call(s32[3]{0:T(128)} %pad_add_fusion.place_ref, bf16[32,424,128]{2,1,0:T(8,128)(2,1)} %copy-done, bf16[32,128,128]{2,1,0:T(8,128)(2,1)} %collective-permute-done.4.swap_ref, bf16[32,96,128]{2,1,0:T(8,128)(2,1)} %collective-permute-done.5.two_ref, bf16[32,64,128]{2,1,0:T(8,128)(2,1)} %copy-done.6, ...), custom_call_target="tpu_custom_call" | custom-call | flops 6946816 | bytes 13893632 | tf_op jit(solution)/shard_map/unfold/pallas_call | solution.py:329
  345.1 24.7 %all-to-all-done.1 = bf16[32,448,128]{2,1,0:T(8,128)(2,1)} async-done(((bf16[32,448,128]{2,1,0:T(8,128)(2,1)}), bf16[32,448,128]{2,1,0:T(8,128)(2,1)}, u32[]{:S(2)}, u32[]{:S(2)}) %all-to-all-start.1) | async-done | bytes 3670048 | tf_op jit(solution)/shard_map/all_to_all | solution.py:631
  369.8 2.8 all-to-all-start.4
  373.4 9.7 %inverse_table.2.refs_0_ = bf16[256,128,256]{2,1,0:T(8,128)(2,1)} custom-call(bf16[128,256]{1,0:T(8,128)(2,1)} %convert_element_type.31.table_ref, bf16[64,256,128]{2,1,0:T(8,128)(2,1)} %bitcast.8, bf16[64,224,128]{2,1,0:T(8,128)(2,1)} %bitcast.7.last_ref), custom_call_target="tpu_custom_call" | custom-call | flops 1879048192 | bytes 22020096 | tf_op jit(solution)/shard_map/inverse_table/pallas_call | solution.py:152
  383.1 5.6 %all-to-all-done.4 = bf16[32,64,128]{2,1,0:T(8,128)(2,1)S(1)} async-done(((bf16[32,64,128]{2,1,0:T(8,128)(2,1)}), bf16[32,64,128]{2,1,0:T(8,128)(2,1)S(1)}, u32[]{:S(2)}, u32[]{:S(2)}) %all-to-all-start.4) | async-done | bytes 524320 | tf_op jit(solution)/shard_map/all_to_all | solution.py:631
  389.4 3.3 inverse_table.3
  (42 shorter events, 9.6 us)
Async XLA Ops:
  11.1 103.2 %all-to-all-start.2 = ((bf16[32,512,128]{2,1,0:T(8,128)(2,1)}), bf16[32,512,128]{2,1,0:T(8,128)(2,1)}, u32[]{:S(2)}, u32[]{:S(2)}) async-start(bf16[32,512,128]{2,1,0:T(8,128)(2,1)} %bitcast.15), calls=%async_computation.2 | async-start | bytes 8388608 | tf_op jit(solution)/shard_map/all_to_all | solution.py:631
  30.6 42.5 %collective-permute-start = (bf16[32,128,128]{2,1,0:T(8,128)(2,1)S(1)}, bf16[32,128,128]{2,1,0:T(8,128)(2,1)S(1)}, u32[]{:S(2)}, u32[]{:S(2)}) collective-permute-start(bf16[32,128,128]{2,1,0:T(8,128)(2,1)S(1)} %constant_dynamic-slice_fusion.1), channel_id=1, source_target_pairs={{0,1},{8,2},{1,0},{9,3},{10,11},{2,8},{11,10},{3,9},{20,21},{28,22... | collective-permute-start | bytes 3145736 | tf_op jit(solution)/shard_map/ppermute | solution.py:602
  35.4 37.5 %collective-permute-start.1 = (bf16[32,96,128]{2,1,0:T(8,128)(2,1)S(1)}, bf16[32,96,128]{2,1,0:T(8,128)(2,1)S(1)}, u32[]{:S(2)}, u32[]{:S(2)}) collective-permute-start(bf16[32,96,128]{2,1,0:T(8,128)(2,1)S(1)} %slice.41), channel_id=1, source_target_pairs={{16,0},{17,1},{26,10},{27,11},{4,20},{5,21},{14,30},{15,31}} | collective-permute-start | bytes 2359304 | tf_op jit(solution)/shard_map/ppermute | solution.py:590
  37.8 25.0 %collective-permute-start.2 = (bf16[32,64,128]{2,1,0:T(8,128)(2,1)S(1)}, bf16[32,64,128]{2,1,0:T(8,128)(2,1)S(1)}, u32[]{:S(2)}, u32[]{:S(2)}) collective-permute-start(bf16[32,64,128]{2,1,0:T(8,128)(2,1)S(1)} %slice.42), channel_id=1, source_target_pairs={{24,0},{25,1},{18,10},{19,11},{12,20},{13,21},{6,30},{7,31}} | collective-permute-start | bytes 1572872 | tf_op jit(solution)/shard_map/ppermute | solution.py:590
  40.1 1.3 collective-permute-start.3
  41.4 31.7 %copy-start.7 = (bf16[32,32,128]{2,1,0:T(8,128)(2,1)}, bf16[32,32,128]{2,1,0:T(8,128)(2,1)S(1)}, u32[]{:S(2)}) copy-start(bf16[32,32,128]{2,1,0:T(8,128)(2,1)S(1)} %collective-permute-done.3.last_ref) | copy-start | bytes 786436
  62.8 10.3 %copy-start.5 = (bf16[32,64,128]{2,1,0:T(8,128)(2,1)}, bf16[32,64,128]{2,1,0:T(8,128)(2,1)S(1)}, u32[]{:S(2)}) copy-start(bf16[32,64,128]{2,1,0:T(8,128)(2,1)S(1)} %collective-permute-done.2.three_ref) | copy-start | bytes 1572868
  72.9 0.9 copy-start.4
  73.8 1.0 copy-start.3
  85.0 32.3 %copy-start.9 = (f32[2,64]{1,0:T(2,128)S(1)}, f32[2,64]{1,0:T(2,128)}, u32[]{:S(2)}) copy-start(f32[2,64]{1,0:T(2,128)} %param.3) | copy-start | bytes 1540
  114.3 82.9 %all-to-all-start = ((bf16[32,424,128]{2,1,0:T(8,128)(2,1)}), bf16[32,424,128]{2,1,0:T(8,128)(2,1)S(1)}, u32[]{:S(2)}, u32[]{:S(2)}) async-start(bf16[32,424,128]{2,1,0:T(8,128)(2,1)} %fold.1), calls=%async_computation | async-start | bytes 6946816 | tf_op jit(solution)/shard_map/all_to_all | solution.py:631
  197.2 1.7 copy-start.1
  198.9 82.9 %all-to-all-start.3 = ((bf16[32,424,128]{2,1,0:T(8,128)(2,1)}), bf16[32,424,128]{2,1,0:T(8,128)(2,1)S(1)}, u32[]{:S(2)}, u32[]{:S(2)}) async-start(bf16[32,424,128]{2,1,0:T(8,128)(2,1)} %owned_frequency.3), calls=%async_computation.3 | async-start | bytes 6946816 | tf_op jit(solution)/shard_map/all_to_all | solution.py:631
  281.8 11.4 %copy-start = (bf16[32,424,128]{2,1,0:T(8,128)(2,1)}, bf16[32,424,128]{2,1,0:T(8,128)(2,1)S(1)}, u32[]{:S(2)}) copy-start(bf16[32,424,128]{2,1,0:T(8,128)(2,1)S(1)} %all-to-all-done.3.folded_ref) | copy-start | bytes 10420228
  281.8 88.0 %all-to-all-start.1 = ((bf16[32,448,128]{2,1,0:T(8,128)(2,1)}), bf16[32,448,128]{2,1,0:T(8,128)(2,1)}, u32[]{:S(2)}, u32[]{:S(2)}) async-start(bf16[32,448,128]{2,1,0:T(8,128)(2,1)} %get-tuple-element.10), calls=%async_computation.1 | async-start | bytes 7340032 | tf_op jit(solution)/shard_map/all_to_all | solution.py:631
  285.6 49.5 %collective-permute-start.4 = (bf16[32,128,128]{2,1,0:T(8,128)(2,1)S(1)}, bf16[32,128,128]{2,1,0:T(8,128)(2,1)}, u32[]{:S(2)}, u32[]{:S(2)}) collective-permute-start(bf16[32,128,128]{2,1,0:T(8,128)(2,1)S(1)} %constant_dynamic-slice_fusion), channel_id=1, source_target_pairs={{0,1},{8,2},{1,0},{9,3},{10,11},{2,8},{11,10},{3,9},{20,21},{28,22... | collective-permute-start | bytes 3145736 | tf_op jit(solution)/shard_map/ppermute | solution.py:620
  289.2 44.4 %collective-permute-start.5 = (bf16[32,96,128]{2,1,0:T(8,128)(2,1)S(1)}, bf16[32,96,128]{2,1,0:T(8,128)(2,1)}, u32[]{:S(2)}, u32[]{:S(2)}) collective-permute-start(bf16[32,96,128]{2,1,0:T(8,128)(2,1)S(1)} %slice.45), channel_id=1, source_target_pairs={{0,16},{1,17},{10,26},{11,27},{20,4},{21,5},{30,14},{31,15}} | collective-permute-start | bytes 2359304 | tf_op jit(solution)/shard_map/ppermute | solution.py:590
  291.9 41.7 %collective-permute-start.6 = (bf16[32,64,128]{2,1,0:T(8,128)(2,1)S(1)}, bf16[32,64,128]{2,1,0:T(8,128)(2,1)S(1)}, u32[]{:S(2)}, u32[]{:S(2)}) collective-permute-start(bf16[32,64,128]{2,1,0:T(8,128)(2,1)S(1)} %slice.46), channel_id=1, source_target_pairs={{0,24},{1,25},{10,18},{11,19},{20,12},{21,13},{30,6},{31,7}} | collective-permute-start | bytes 1572872 | tf_op jit(solution)/shard_map/ppermute | solution.py:590
  293.2 0.7 collective-permute-start.7
  293.9 41.2 %copy-start.8 = (bf16[32,32,128]{2,1,0:T(8,128)(2,1)}, bf16[32,32,128]{2,1,0:T(8,128)(2,1)S(1)}, u32[]{:S(2)}) copy-start(bf16[32,32,128]{2,1,0:T(8,128)(2,1)S(1)} %collective-permute-done.7.last_ref) | copy-start | bytes 786436
  333.6 0.8 copy-start.6
  369.8 18.8 %all-to-all-start.4 = ((bf16[32,64,128]{2,1,0:T(8,128)(2,1)}), bf16[32,64,128]{2,1,0:T(8,128)(2,1)S(1)}, u32[]{:S(2)}, u32[]{:S(2)}) async-start(bf16[32,64,128]{2,1,0:T(8,128)(2,1)} %get-tuple-element.13), calls=%async_computation.4 | async-start | bytes 1048576 | tf_op jit(solution)/shard_map/all_to_all | solution.py:631
  388.6 0.8 copy-start.2

commit v7 on v6

--- a/solution.py
+++ b/solution.py
@@ -148,6 +148,10 @@
     bins, samples = table.shape
     half, total, cols = first.shape
     count = last.shape[1]
+    last_spec = pl.BlockSpec((bins - half, step, cols), lambda i: (0, i, 0))
+    if count == step:
+        last = pltpu.with_memory_space_constraint(last, pltpu.VMEM)
+        last_spec = pl.BlockSpec(memory_space=pltpu.VMEM)
     skip = start // step
     return pl.pallas_call(
         inverse_kernel,
@@ -155,7 +159,7 @@
         in_specs=[
             pl.BlockSpec((bins, samples), lambda i: (0, 0)),
             pl.BlockSpec((half, step, cols), lambda i: (0, i + skip, 0)),
-            pl.BlockSpec((bins - half, step, cols), lambda i: (0, i, 0)),
+            last_spec,
         ]
         + ([] if prior is None else [pl.BlockSpec(memory_space=pl.ANY)]),
         out_specs=pl.BlockSpec((step, cols, samples), lambda i: (i + skip, 0, 0)),
@@ -520,6 +524,8 @@
 
 
 def owner(wave, recv, sources, groups, fold_in, fold_out):
+    if fold_in:
+        recv = pltpu.with_memory_space_constraint(recv, pltpu.VMEM)
     devices, _, cols = recv.shape
     total = groups * cols
     whole = 2 * (total // sources)

time: 394 us -> 392 us (level)
  transfers between devices with their start and end apart: 13 -> 13, of which waited for: 10 -> 10; matrix products, arithmetic and copies ran while one was open for 2% -> 3% of each run, Pallas kernels for 23% -> 23%
where the time goes in v7:
time: 392 us; the launch traced here: 391 us
  waiting for transfers between devices  238 us (61%)
  Pallas kernels  103 us (26%)
  starting transfers between devices  34 us (9%)
  local copies, waits for them, and re-layouts  14.6 us (4%)
    all_to_all x5, waiting for transfers between devices, exchange(): return lax.all_to_all(array, AXES, 0, 0, tiled=True)  168 us
    ppermute x6, waiting for transfers between devices, send_rows(): return lax.ppermute(array[:, start:stop], AXES, pairs)  67.8 us
    pallas_call x2, Pallas kernels, owner(): pl.pallas_call(functools.partial(owner_kernel, sources=sources, groups=gr...  49.7 us
    all_to_all x5, starting transfers between devices, exchange(): return lax.all_to_all(array, AXES, 0, 0, tiled=True)  20.3 us
    pallas_call x2, Pallas kernels, dft(): pl.pallas_call(functools.partial(dft_kernel, group=16), grid=(count // st...  20.2 us
    pallas_call x2, Pallas kernels, per_device(): pl.pallas_call(kernel, grid=(devices // step,), in_specs=[pl.BlockSpec(me...  20.1 us
    pallas_call x2, Pallas kernels, inverse_rows(): pl.pallas_call(inverse_kernel, grid=(count // step,), in_specs=[pl.BlockS...  12.9 us
  transfers between devices with their start and end apart: 13, of which 10 were waited for; matrix products, arithmetic and copies ran while one was open for 3% of the time, Pallas kernels for 23%

profile of v7, /device:TPU:0, one launch (start us, length us, event | category | flops | bytes accessed | tf_op | source)
XLA Modules:
  0.0 390.7 jit_solution(16839806155756384938)
XLA Ops:
  1.1 10.0 %forward_table.3 = bf16[64,256,128]{2,1,0:T(8,128)(2,1)} custom-call(bf16[64,256]{1,0:T(8,128)(2,1)} %slice.36.table_ref, bf16[256,128,256]{2,1,0:T(8,128)(2,1)} %wave_ref.3), custom_call_target="tpu_custom_call" | custom-call | flops 1073741824 | bytes 20971520 | tf_op jit(solution)/shard_map/forward_table/pallas_call | solution.py:118
  11.1 7.4 %all-to-all-start.2 = ((bf16[32,512,128]{2,1,0:T(8,128)(2,1)}), bf16[32,512,128]{2,1,0:T(8,128)(2,1)}, u32[]{:S(2)}, u32[]{:S(2)}) async-start(bf16[32,512,128]{2,1,0:T(8,128)(2,1)} %bitcast.16), calls=%async_computation.2 | async-start | bytes 8388608 | tf_op jit(solution)/shard_map/all_to_all | solution.py:637
  19.3 10.2 %forward_table.2 = bf16[64,256,128]{2,1,0:T(8,128)(2,1)} custom-call(bf16[64,256]{1,0:T(8,128)(2,1)} %slice.31.table_ref, bf16[256,128,256]{2,1,0:T(8,128)(2,1)} %wave_ref.3), custom_call_target="tpu_custom_call" | custom-call | flops 1073741824 | bytes 20971520 | tf_op jit(solution)/shard_map/forward_table/pallas_call | solution.py:118
  29.4 1.3 constant_dynamic-slice_fusion.1
  30.7 3.6 collective-permute-start
  34.3 1.2 slice.41
  35.5 1.3 collective-permute-start.1
  37.9 1.3 collective-permute-start.2
  41.6 21.5 %collective-permute-done.2.three_ref = bf16[32,64,128]{2,1,0:T(8,128)(2,1)S(1)} collective-permute-done((bf16[32,64,128]{2,1,0:T(8,128)(2,1)S(1)}, bf16[32,64,128]{2,1,0:T(8,128)(2,1)S(1)}, u32[]{:S(2)}, u32[]{:S(2)}) %collective-permute-start.2) | collective-permute-done | bytes 524320 | tf_op jit(solution)/shard_map/ppermute | solution.py:596
  63.1 9.7 %collective-permute-done.1.two_ref = bf16[32,96,128]{2,1,0:T(8,128)(2,1)S(1)} collective-permute-done((bf16[32,96,128]{2,1,0:T(8,128)(2,1)S(1)}, bf16[32,96,128]{2,1,0:T(8,128)(2,1)S(1)}, u32[]{:S(2)}, u32[]{:S(2)}) %collective-permute-start.1) | collective-permute-done | bytes 786464 | tf_op jit(solution)/shard_map/ppermute | solution.py:596
  74.7 10.2 %fold.1 = bf16[32,424,128]{2,1,0:T(8,128)(2,1)} custom-call(s32[3]{0:T(128)} %pad_add_fusion.place_ref, bf16[32,512,128]{2,1,0:T(8,128)(2,1)} %bitcast.15, bf16[32,128,128]{2,1,0:T(8,128)(2,1)} %copy-done, bf16[32,96,128]{2,1,0:T(8,128)(2,1)} %copy-done.2, bf16[32,64,128]{2,1,0:T(8,128)(2,1)} %copy-done.4, bf16[32,32,128]{2,1,0:T(8,128)(2,1)} %copy-done.6), custom_call_target="tpu_custom_call" | custom-call | flops 8388608 | bytes 16777216 | tf_op jit(solution)/shard_map/fold/pallas_call | solution.py:333
  84.9 29.4 %all-to-all-done.2.recv_ref = bf16[32,512,128]{2,1,0:T(8,128)(2,1)} async-done(((bf16[32,512,128]{2,1,0:T(8,128)(2,1)}), bf16[32,512,128]{2,1,0:T(8,128)(2,1)}, u32[]{:S(2)}, u32[]{:S(2)}) %all-to-all-start.2) | async-done | bytes 4194336 | tf_op jit(solution)/shard_map/all_to_all | solution.py:637
  114.3 3.0 all-to-all-start
  118.0 25.7 %owned_frequency.3 = bf16[32,424,128]{2,1,0:T(8,128)(2,1)} custom-call(f32[2]{0:T(128)} %get-tuple-element.15.wave_ref, bf16[32,512,128]{2,1,0:T(8,128)(2,1)} %all-to-all-done.2.recv_ref), custom_call_target="tpu_custom_call" | custom-call | flops 17179869184 | bytes 16777216 | tf_op jit(solution)/shard_map/owned_frequency/pallas_call | solution.py:533
  143.7 53.5 %all-to-all-done.recv_ref = bf16[32,424,128]{2,1,0:T(8,128)(2,1)S(1)} async-done(((bf16[32,424,128]{2,1,0:T(8,128)(2,1)}), bf16[32,424,128]{2,1,0:T(8,128)(2,1)S(1)}, u32[]{:S(2)}, u32[]{:S(2)}) %all-to-all-start) | async-done | bytes 3473440 | tf_op jit(solution)/shard_map/all_to_all | solution.py:637
  197.2 3.6 all-to-all-start.3
  200.7 24.0 %owned_frequency.2 = (bf16[32,448,128]{2,1,0:T(8,128)(2,1)}, bf16[32,64,128]{2,1,0:T(8,128)(2,1)}) custom-call(f32[2]{0:T(128)} %get-tuple-element.16.wave_ref, bf16[32,424,128]{2,1,0:T(8,128)(2,1)S(1)} %all-to-all-done.recv_ref), custom_call_target="tpu_custom_call" | custom-call | flops 17179869184 | bytes 16777216 | tf_op jit(solution)/shard_map/owned_frequency/pallas_call | solution.py:533
  224.7 56.1 %all-to-all-done.3.folded_ref = bf16[32,424,128]{2,1,0:T(8,128)(2,1)} async-done(((bf16[32,424,128]{2,1,0:T(8,128)(2,1)}), bf16[32,424,128]{2,1,0:T(8,128)(2,1)}, u32[]{:S(2)}, u32[]{:S(2)}) %all-to-all-start.3) | async-done | bytes 3473440 | tf_op jit(solution)/shard_map/all_to_all | solution.py:637
  280.8 3.6 all-to-all-start.1
  284.4 1.3 constant_dynamic-slice_fusion
  285.7 3.5 collective-permute-start.4
  289.2 1.2 slice.45
  290.4 1.3 collective-permute-start.5
  292.8 1.3 collective-permute-start.6
  295.9 36.6 %collective-permute-done.6.three_ref = bf16[32,64,128]{2,1,0:T(8,128)(2,1)S(1)} collective-permute-done((bf16[32,64,128]{2,1,0:T(8,128)(2,1)S(1)}, bf16[32,64,128]{2,1,0:T(8,128)(2,1)S(1)}, u32[]{:S(2)}, u32[]{:S(2)}) %collective-permute-start.6) | collective-permute-done | bytes 524320 | tf_op jit(solution)/shard_map/ppermute | solution.py:596
  332.5 1.5 collective-permute-done.4.swap_ref
  334.9 9.9 %unfold.1 = bf16[32,512,128]{2,1,0:T(8,128)(2,1)} custom-call(s32[3]{0:T(128)} %pad_add_fusion.place_ref, bf16[32,424,128]{2,1,0:T(8,128)(2,1)} %all-to-all-done.3.folded_ref, bf16[32,128,128]{2,1,0:T(8,128)(2,1)} %copy-done.1, bf16[32,96,128]{2,1,0:T(8,128)(2,1)} %copy-done.3, bf16[32,64,128]{2,1,0:T(8,128)(2,1)} %copy-done.5, bf16[32,32,128]{2,1,0:T(8,128)(2,1)} %copy-done.7), custom_call_target="tpu_custom_call" | custom-call | flops 6946816 | bytes 13893632 | tf_op jit(solution)/shard_map/unfold/pallas_call | solution.py:333
  344.9 23.8 %all-to-all-done.1 = bf16[32,448,128]{2,1,0:T(8,128)(2,1)} async-done(((bf16[32,448,128]{2,1,0:T(8,128)(2,1)}), bf16[32,448,128]{2,1,0:T(8,128)(2,1)}, u32[]{:S(2)}, u32[]{:S(2)}) %all-to-all-start.1) | async-done | bytes 3670048 | tf_op jit(solution)/shard_map/all_to_all | solution.py:637
  368.7 2.8 all-to-all-start.4
  372.2 9.7 %inverse_table.2.refs_0_ = bf16[256,128,256]{2,1,0:T(8,128)(2,1)} custom-call(bf16[128,256]{1,0:T(8,128)(2,1)} %convert_element_type.31.table_ref, bf16[64,256,128]{2,1,0:T(8,128)(2,1)} %bitcast.9, bf16[64,224,128]{2,1,0:T(8,128)(2,1)} %bitcast.7.last_ref), custom_call_target="tpu_custom_call" | custom-call | flops 1879048192 | bytes 22020096 | tf_op jit(solution)/shard_map/inverse_table/pallas_call | solution.py:156
  382.0 5.6 %all-to-all-done.4 = bf16[32,64,128]{2,1,0:T(8,128)(2,1)S(1)} async-done(((bf16[32,64,128]{2,1,0:T(8,128)(2,1)}), bf16[32,64,128]{2,1,0:T(8,128)(2,1)S(1)}, u32[]{:S(2)}, u32[]{:S(2)}) %all-to-all-start.4) | async-done | bytes 524320 | tf_op jit(solution)/shard_map/all_to_all | solution.py:637
  387.5 3.2 inverse_table.3
  (40 shorter events, 12.3 us)
Async XLA Ops:
  11.1 103.2 %all-to-all-start.2 = ((bf16[32,512,128]{2,1,0:T(8,128)(2,1)}), bf16[32,512,128]{2,1,0:T(8,128)(2,1)}, u32[]{:S(2)}, u32[]{:S(2)}) async-start(bf16[32,512,128]{2,1,0:T(8,128)(2,1)} %bitcast.16), calls=%async_computation.2 | async-start | bytes 8388608 | tf_op jit(solution)/shard_map/all_to_all | solution.py:637
  30.7 42.4 %collective-permute-start = (bf16[32,128,128]{2,1,0:T(8,128)(2,1)S(1)}, bf16[32,128,128]{2,1,0:T(8,128)(2,1)S(1)}, u32[]{:S(2)}, u32[]{:S(2)}) collective-permute-start(bf16[32,128,128]{2,1,0:T(8,128)(2,1)S(1)} %constant_dynamic-slice_fusion.1), channel_id=1, source_target_pairs={{0,1},{8,2},{1,0},{9,3},{10,11},{2,8},{11,10},{3,9},{20,21},{28,22... | collective-permute-start | bytes 3145736 | tf_op jit(solution)/shard_map/ppermute | solution.py:608
  35.5 37.2 %collective-permute-start.1 = (bf16[32,96,128]{2,1,0:T(8,128)(2,1)S(1)}, bf16[32,96,128]{2,1,0:T(8,128)(2,1)S(1)}, u32[]{:S(2)}, u32[]{:S(2)}) collective-permute-start(bf16[32,96,128]{2,1,0:T(8,128)(2,1)S(1)} %slice.41), channel_id=1, source_target_pairs={{16,0},{17,1},{26,10},{27,11},{4,20},{5,21},{14,30},{15,31}} | collective-permute-start | bytes 2359304 | tf_op jit(solution)/shard_map/ppermute | solution.py:596
  37.9 25.1 %collective-permute-start.2 = (bf16[32,64,128]{2,1,0:T(8,128)(2,1)S(1)}, bf16[32,64,128]{2,1,0:T(8,128)(2,1)S(1)}, u32[]{:S(2)}, u32[]{:S(2)}) collective-permute-start(bf16[32,64,128]{2,1,0:T(8,128)(2,1)S(1)} %slice.42), channel_id=1, source_target_pairs={{24,0},{25,1},{18,10},{19,11},{12,20},{13,21},{6,30},{7,31}} | collective-permute-start | bytes 1572872 | tf_op jit(solution)/shard_map/ppermute | solution.py:596
  40.2 1.4 collective-permute-start.3
  41.6 31.5 %copy-start.6 = (bf16[32,32,128]{2,1,0:T(8,128)(2,1)}, bf16[32,32,128]{2,1,0:T(8,128)(2,1)S(1)}, u32[]{:S(2)}) copy-start(bf16[32,32,128]{2,1,0:T(8,128)(2,1)S(1)} %collective-permute-done.3.last_ref) | copy-start | bytes 786436
  63.1 10.1 %copy-start.4 = (bf16[32,64,128]{2,1,0:T(8,128)(2,1)}, bf16[32,64,128]{2,1,0:T(8,128)(2,1)S(1)}, u32[]{:S(2)}) copy-start(bf16[32,64,128]{2,1,0:T(8,128)(2,1)S(1)} %collective-permute-done.2.three_ref) | copy-start | bytes 1572868
  72.8 0.9 copy-start.2
  73.7 1.0 copy-start
  84.9 32.4 %copy-start.8 = (f32[2,64]{1,0:T(2,128)S(1)}, f32[2,64]{1,0:T(2,128)}, u32[]{:S(2)}) copy-start(f32[2,64]{1,0:T(2,128)} %param.3) | copy-start | bytes 1540
  114.3 82.9 %all-to-all-start = ((bf16[32,424,128]{2,1,0:T(8,128)(2,1)}), bf16[32,424,128]{2,1,0:T(8,128)(2,1)S(1)}, u32[]{:S(2)}, u32[]{:S(2)}) async-start(bf16[32,424,128]{2,1,0:T(8,128)(2,1)} %fold.1), calls=%async_computation | async-start | bytes 6946816 | tf_op jit(solution)/shard_map/all_to_all | solution.py:637
  197.2 83.7 %all-to-all-start.3 = ((bf16[32,424,128]{2,1,0:T(8,128)(2,1)}), bf16[32,424,128]{2,1,0:T(8,128)(2,1)}, u32[]{:S(2)}, u32[]{:S(2)}) async-start(bf16[32,424,128]{2,1,0:T(8,128)(2,1)} %owned_frequency.3), calls=%async_computation.3 | async-start | bytes 6946816 | tf_op jit(solution)/shard_map/all_to_all | solution.py:637
  280.8 87.8 %all-to-all-start.1 = ((bf16[32,448,128]{2,1,0:T(8,128)(2,1)}), bf16[32,448,128]{2,1,0:T(8,128)(2,1)}, u32[]{:S(2)}, u32[]{:S(2)}) async-start(bf16[32,448,128]{2,1,0:T(8,128)(2,1)} %get-tuple-element.10), calls=%async_computation.1 | async-start | bytes 7340032 | tf_op jit(solution)/shard_map/all_to_all | solution.py:637
  285.7 48.2 %collective-permute-start.4 = (bf16[32,128,128]{2,1,0:T(8,128)(2,1)S(1)}, bf16[32,128,128]{2,1,0:T(8,128)(2,1)S(1)}, u32[]{:S(2)}, u32[]{:S(2)}) collective-permute-start(bf16[32,128,128]{2,1,0:T(8,128)(2,1)S(1)} %constant_dynamic-slice_fusion), channel_id=1, source_target_pairs={{0,1},{8,2},{1,0},{9,3},{10,11},{2,8},{11,10},{3,9},{20,21},{28,22... | collective-permute-start | bytes 3145736 | tf_op jit(solution)/shard_map/ppermute | solution.py:626
  290.4 42.0 %collective-permute-start.5 = (bf16[32,96,128]{2,1,0:T(8,128)(2,1)S(1)}, bf16[32,96,128]{2,1,0:T(8,128)(2,1)S(1)}, u32[]{:S(2)}, u32[]{:S(2)}) collective-permute-start(bf16[32,96,128]{2,1,0:T(8,128)(2,1)S(1)} %slice.45), channel_id=1, source_target_pairs={{0,16},{1,17},{10,26},{11,27},{20,4},{21,5},{30,14},{31,15}} | collective-permute-start | bytes 2359304 | tf_op jit(solution)/shard_map/ppermute | solution.py:596
  292.8 39.6 %collective-permute-start.6 = (bf16[32,64,128]{2,1,0:T(8,128)(2,1)S(1)}, bf16[32,64,128]{2,1,0:T(8,128)(2,1)S(1)}, u32[]{:S(2)}, u32[]{:S(2)}) collective-permute-start(bf16[32,64,128]{2,1,0:T(8,128)(2,1)S(1)} %slice.46), channel_id=1, source_target_pairs={{0,24},{1,25},{10,18},{11,19},{20,12},{21,13},{30,6},{31,7}} | collective-permute-start | bytes 1572872 | tf_op jit(solution)/shard_map/ppermute | solution.py:596
  295.2 0.7 collective-permute-start.7
  295.9 38.1 %copy-start.7 = (bf16[32,32,128]{2,1,0:T(8,128)(2,1)}, bf16[32,32,128]{2,1,0:T(8,128)(2,1)S(1)}, u32[]{:S(2)}) copy-start(bf16[32,32,128]{2,1,0:T(8,128)(2,1)S(1)} %collective-permute-done.7.last_ref) | copy-start | bytes 786436
  332.5 1.5 copy-start.5
  332.5 1.5 copy-start.3
  333.9 1.0 copy-start.1
  368.7 18.8 %all-to-all-start.4 = ((bf16[32,64,128]{2,1,0:T(8,128)(2,1)}), bf16[32,64,128]{2,1,0:T(8,128)(2,1)S(1)}, u32[]{:S(2)}, u32[]{:S(2)}) async-start(bf16[32,64,128]{2,1,0:T(8,128)(2,1)} %get-tuple-element.13), calls=%async_computation.4 | async-start | bytes 1048576 | tf_op jit(solution)/shard_map/all_to_all | solution.py:637

commit v8 on v7

--- a/solution.py
+++ b/solution.py
@@ -98,7 +98,7 @@
 
 NT_DIMS = (((1,), (1,)), ((), ()))
 TN_DIMS = (((0,), (0,)), ((), ()))
-EDGE = 32
+EDGE = 16
 
 
 def dft_kernel(table_ref, wave_ref, out_ref, *, group):

time: 392 us -> 392 us (level)
  transfers between devices with their start and end apart: 13 -> 13, of which waited for: 10 -> 9; matrix products, arithmetic and copies ran while one was open for 3% -> 3% of each run, Pallas kernels for 23% -> 23%
where the time goes in v8:
time: 392 us; the launch traced here: 391 us
  waiting for transfers between devices  238 us (61%)
  Pallas kernels  103 us (26%)
  starting transfers between devices  34 us (9%)
  local copies, waits for them, and re-layouts  14.6 us (4%)
    all_to_all x5, waiting for transfers between devices, exchange(): return lax.all_to_all(array, AXES, 0, 0, tiled=True)  166 us
    ppermute x6, waiting for transfers between devices, send_rows(): return lax.ppermute(array[:, start:stop], AXES, pairs)  70 us
    pallas_call x2, Pallas kernels, owner(): pl.pallas_call(functools.partial(owner_kernel, sources=sources, groups=gr...  49.7 us
    all_to_all x5, starting transfers between devices, exchange(): return lax.all_to_all(array, AXES, 0, 0, tiled=True)  20.3 us
    pallas_call x2, Pallas kernels, dft(): pl.pallas_call(functools.partial(dft_kernel, group=16), grid=(count // st...  20.2 us
    pallas_call x2, Pallas kernels, per_device(): pl.pallas_call(kernel, grid=(devices // step,), in_specs=[pl.BlockSpec(me...  20.1 us
    pallas_call x2, Pallas kernels, inverse_rows(): pl.pallas_call(inverse_kernel, grid=(count // step,), in_specs=[pl.BlockS...  12.7 us
  transfers between devices with their start and end apart: 13, of which 9 were waited for; matrix products, arithmetic and copies ran while one was open for 3% of the time, Pallas kernels for 23%

profile of v8, /device:TPU:0, one launch (start us, length us, event | category | flops | bytes accessed | tf_op | source)
XLA Modules:
  0.0 390.6 jit_solution(12416847215085493494)
XLA Ops:
  1.1 10.0 %forward_table.3 = bf16[64,256,128]{2,1,0:T(8,128)(2,1)} custom-call(bf16[64,256]{1,0:T(8,128)(2,1)} %slice.36.table_ref, bf16[256,128,256]{2,1,0:T(8,128)(2,1)} %wave_ref.3), custom_call_target="tpu_custom_call" | custom-call | flops 1073741824 | bytes 20971520 | tf_op jit(solution)/shard_map/forward_table/pallas_call | solution.py:118
  11.1 7.4 %all-to-all-start.2 = ((bf16[32,512,128]{2,1,0:T(8,128)(2,1)}), bf16[32,512,128]{2,1,0:T(8,128)(2,1)}, u32[]{:S(2)}, u32[]{:S(2)}) async-start(bf16[32,512,128]{2,1,0:T(8,128)(2,1)} %bitcast.16), calls=%async_computation.2 | async-start | bytes 8388608 | tf_op jit(solution)/shard_map/all_to_all | solution.py:637
  19.3 10.2 %forward_table.2 = bf16[64,256,128]{2,1,0:T(8,128)(2,1)} custom-call(bf16[64,256]{1,0:T(8,128)(2,1)} %slice.31.table_ref, bf16[256,128,256]{2,1,0:T(8,128)(2,1)} %wave_ref.3), custom_call_target="tpu_custom_call" | custom-call | flops 1073741824 | bytes 20971520 | tf_op jit(solution)/shard_map/forward_table/pallas_call | solution.py:118
  29.4 1.3 constant_dynamic-slice_fusion.1
  30.7 3.6 collective-permute-start
  34.3 1.2 slice.41
  35.5 1.3 collective-permute-start.1
  36.8 1.1 slice.42
  37.9 1.3 collective-permute-start.2
  41.6 21.5 %collective-permute-done.2.three_ref = bf16[32,64,128]{2,1,0:T(8,128)(2,1)S(1)} collective-permute-done((bf16[32,64,128]{2,1,0:T(8,128)(2,1)S(1)}, bf16[32,64,128]{2,1,0:T(8,128)(2,1)S(1)}, u32[]{:S(2)}, u32[]{:S(2)}) %collective-permute-start.2) | collective-permute-done | bytes 524320 | tf_op jit(solution)/shard_map/ppermute | solution.py:596
  63.1 9.7 %collective-permute-done.1.two_ref = bf16[32,96,128]{2,1,0:T(8,128)(2,1)S(1)} collective-permute-done((bf16[32,96,128]{2,1,0:T(8,128)(2,1)S(1)}, bf16[32,96,128]{2,1,0:T(8,128)(2,1)S(1)}, u32[]{:S(2)}, u32[]{:S(2)}) %collective-permute-start.1) | collective-permute-done | bytes 786464 | tf_op jit(solution)/shard_map/ppermute | solution.py:596
  74.7 10.2 %fold.1 = bf16[32,424,128]{2,1,0:T(8,128)(2,1)} custom-call(s32[3]{0:T(128)} %pad_add_fusion.place_ref, bf16[32,512,128]{2,1,0:T(8,128)(2,1)} %bitcast.15, bf16[32,128,128]{2,1,0:T(8,128)(2,1)} %copy-done, bf16[32,96,128]{2,1,0:T(8,128)(2,1)} %copy-done.2, bf16[32,64,128]{2,1,0:T(8,128)(2,1)} %copy-done.4, bf16[32,32,128]{2,1,0:T(8,128)(2,1)} %copy-done.6), custom_call_target="tpu_custom_call" | custom-call | flops 8388608 | bytes 16777216 | tf_op jit(solution)/shard_map/fold/pallas_call | solution.py:333
  84.9 29.4 %all-to-all-done.2.recv_ref = bf16[32,512,128]{2,1,0:T(8,128)(2,1)} async-done(((bf16[32,512,128]{2,1,0:T(8,128)(2,1)}), bf16[32,512,128]{2,1,0:T(8,128)(2,1)}, u32[]{:S(2)}, u32[]{:S(2)}) %all-to-all-start.2) | async-done | bytes 4194336 | tf_op jit(solution)/shard_map/all_to_all | solution.py:637
  114.3 3.0 all-to-all-start
  118.0 25.7 %owned_frequency.3 = bf16[32,424,128]{2,1,0:T(8,128)(2,1)} custom-call(f32[2]{0:T(128)} %get-tuple-element.15.wave_ref, bf16[32,512,128]{2,1,0:T(8,128)(2,1)} %all-to-all-done.2.recv_ref), custom_call_target="tpu_custom_call" | custom-call | flops 17179869184 | bytes 16777216 | tf_op jit(solution)/shard_map/owned_frequency/pallas_call | solution.py:533
  143.7 53.5 %all-to-all-done.recv_ref = bf16[32,424,128]{2,1,0:T(8,128)(2,1)S(1)} async-done(((bf16[32,424,128]{2,1,0:T(8,128)(2,1)}), bf16[32,424,128]{2,1,0:T(8,128)(2,1)S(1)}, u32[]{:S(2)}, u32[]{:S(2)}) %all-to-all-start) | async-done | bytes 3473440 | tf_op jit(solution)/shard_map/all_to_all | solution.py:637
  197.2 3.6 all-to-all-start.3
  200.7 24.0 %owned_frequency.2 = (bf16[32,480,128]{2,1,0:T(8,128)(2,1)}, bf16[32,32,128]{2,1,0:T(8,128)(2,1)}) custom-call(f32[2]{0:T(128)} %get-tuple-element.16.wave_ref, bf16[32,424,128]{2,1,0:T(8,128)(2,1)S(1)} %all-to-all-done.recv_ref), custom_call_target="tpu_custom_call" | custom-call | flops 17179869184 | bytes 16777216 | tf_op jit(solution)/shard_map/owned_frequency/pallas_call | solution.py:533
  224.7 56.1 %all-to-all-done.3.folded_ref = bf16[32,424,128]{2,1,0:T(8,128)(2,1)} async-done(((bf16[32,424,128]{2,1,0:T(8,128)(2,1)}), bf16[32,424,128]{2,1,0:T(8,128)(2,1)}, u32[]{:S(2)}, u32[]{:S(2)}) %all-to-all-start.3) | async-done | bytes 3473440 | tf_op jit(solution)/shard_map/all_to_all | solution.py:637
  280.8 3.6 all-to-all-start.1
  284.4 1.3 constant_dynamic-slice_fusion
  285.7 3.5 collective-permute-start.4
  289.2 1.2 slice.45
  290.4 1.3 collective-permute-start.5
  292.9 1.3 collective-permute-start.6
  295.9 38.8 %collective-permute-done.6.three_ref = bf16[32,64,128]{2,1,0:T(8,128)(2,1)S(1)} collective-permute-done((bf16[32,64,128]{2,1,0:T(8,128)(2,1)S(1)}, bf16[32,64,128]{2,1,0:T(8,128)(2,1)S(1)}, u32[]{:S(2)}, u32[]{:S(2)}) %collective-permute-start.6) | collective-permute-done | bytes 524320 | tf_op jit(solution)/shard_map/ppermute | solution.py:596
  334.7 1.7 collective-permute-done.4.swap_ref
  337.4 9.9 %unfold.1 = bf16[32,512,128]{2,1,0:T(8,128)(2,1)} custom-call(s32[3]{0:T(128)} %pad_add_fusion.place_ref, bf16[32,424,128]{2,1,0:T(8,128)(2,1)} %all-to-all-done.3.folded_ref, bf16[32,128,128]{2,1,0:T(8,128)(2,1)} %copy-done.1, bf16[32,96,128]{2,1,0:T(8,128)(2,1)} %copy-done.3, bf16[32,64,128]{2,1,0:T(8,128)(2,1)} %copy-done.5, bf16[32,32,128]{2,1,0:T(8,128)(2,1)} %copy-done.7), custom_call_target="tpu_custom_call" | custom-call | flops 6946816 | bytes 13893632 | tf_op jit(solution)/shard_map/unfold/pallas_call | solution.py:333
  347.4 27.0 %all-to-all-done.1 = bf16[32,480,128]{2,1,0:T(8,128)(2,1)} async-done(((bf16[32,480,128]{2,1,0:T(8,128)(2,1)}), bf16[32,480,128]{2,1,0:T(8,128)(2,1)}, u32[]{:S(2)}, u32[]{:S(2)}) %all-to-all-start.1) | async-done | bytes 3932192 | tf_op jit(solution)/shard_map/all_to_all | solution.py:637
  374.4 2.8 all-to-all-start.4
  377.9 10.3 %inverse_table.2.refs_0_ = bf16[256,128,256]{2,1,0:T(8,128)(2,1)} custom-call(bf16[128,256]{1,0:T(8,128)(2,1)} %convert_element_type.31.table_ref, bf16[64,256,128]{2,1,0:T(8,128)(2,1)} %bitcast.9, bf16[64,240,128]{2,1,0:T(8,128)(2,1)} %bitcast.7.last_ref), custom_call_target="tpu_custom_call" | custom-call | flops 2013265920 | bytes 23592960 | tf_op jit(solution)/shard_map/inverse_table/pallas_call | solution.py:156
  388.2 2.5 inverse_table.3
  (40 shorter events, 11.2 us)
Async XLA Ops:
  11.1 103.2 %all-to-all-start.2 = ((bf16[32,512,128]{2,1,0:T(8,128)(2,1)}), bf16[32,512,128]{2,1,0:T(8,128)(2,1)}, u32[]{:S(2)}, u32[]{:S(2)}) async-start(bf16[32,512,128]{2,1,0:T(8,128)(2,1)} %bitcast.16), calls=%async_computation.2 | async-start | bytes 8388608 | tf_op jit(solution)/shard_map/all_to_all | solution.py:637
  30.7 42.4 %collective-permute-start = (bf16[32,128,128]{2,1,0:T(8,128)(2,1)S(1)}, bf16[32,128,128]{2,1,0:T(8,128)(2,1)S(1)}, u32[]{:S(2)}, u32[]{:S(2)}) collective-permute-start(bf16[32,128,128]{2,1,0:T(8,128)(2,1)S(1)} %constant_dynamic-slice_fusion.1), channel_id=1, source_target_pairs={{0,1},{8,2},{1,0},{9,3},{10,11},{2,8},{11,10},{3,9},{20,21},{28,22... | collective-permute-start | bytes 3145736 | tf_op jit(solution)/shard_map/ppermute | solution.py:608
  35.5 37.2 %collective-permute-start.1 = (bf16[32,96,128]{2,1,0:T(8,128)(2,1)S(1)}, bf16[32,96,128]{2,1,0:T(8,128)(2,1)S(1)}, u32[]{:S(2)}, u32[]{:S(2)}) collective-permute-start(bf16[32,96,128]{2,1,0:T(8,128)(2,1)S(1)} %slice.41), channel_id=1, source_target_pairs={{16,0},{17,1},{26,10},{27,11},{4,20},{5,21},{14,30},{15,31}} | collective-permute-start | bytes 2359304 | tf_op jit(solution)/shard_map/ppermute | solution.py:596
  37.9 25.1 %collective-permute-start.2 = (bf16[32,64,128]{2,1,0:T(8,128)(2,1)S(1)}, bf16[32,64,128]{2,1,0:T(8,128)(2,1)S(1)}, u32[]{:S(2)}, u32[]{:S(2)}) collective-permute-start(bf16[32,64,128]{2,1,0:T(8,128)(2,1)S(1)} %slice.42), channel_id=1, source_target_pairs={{24,0},{25,1},{18,10},{19,11},{12,20},{13,21},{6,30},{7,31}} | collective-permute-start | bytes 1572872 | tf_op jit(solution)/shard_map/ppermute | solution.py:596
  40.2 1.4 collective-permute-start.3
  41.6 31.5 %copy-start.6 = (bf16[32,32,128]{2,1,0:T(8,128)(2,1)}, bf16[32,32,128]{2,1,0:T(8,128)(2,1)S(1)}, u32[]{:S(2)}) copy-start(bf16[32,32,128]{2,1,0:T(8,128)(2,1)S(1)} %collective-permute-done.3.last_ref) | copy-start | bytes 786436
  63.1 10.1 %copy-start.4 = (bf16[32,64,128]{2,1,0:T(8,128)(2,1)}, bf16[32,64,128]{2,1,0:T(8,128)(2,1)S(1)}, u32[]{:S(2)}) copy-start(bf16[32,64,128]{2,1,0:T(8,128)(2,1)S(1)} %collective-permute-done.2.three_ref) | copy-start | bytes 1572868
  72.8 0.9 copy-start.2
  73.7 1.0 copy-start
  84.9 32.4 %copy-start.8 = (f32[2,64]{1,0:T(2,128)S(1)}, f32[2,64]{1,0:T(2,128)}, u32[]{:S(2)}) copy-start(f32[2,64]{1,0:T(2,128)} %param.3) | copy-start | bytes 1540
  114.3 82.9 %all-to-all-start = ((bf16[32,424,128]{2,1,0:T(8,128)(2,1)}), bf16[32,424,128]{2,1,0:T(8,128)(2,1)S(1)}, u32[]{:S(2)}, u32[]{:S(2)}) async-start(bf16[32,424,128]{2,1,0:T(8,128)(2,1)} %fold.1), calls=%async_computation | async-start | bytes 6946816 | tf_op jit(solution)/shard_map/all_to_all | solution.py:637
  197.2 83.7 %all-to-all-start.3 = ((bf16[32,424,128]{2,1,0:T(8,128)(2,1)}), bf16[32,424,128]{2,1,0:T(8,128)(2,1)}, u32[]{:S(2)}, u32[]{:S(2)}) async-start(bf16[32,424,128]{2,1,0:T(8,128)(2,1)} %owned_frequency.3), calls=%async_computation.3 | async-start | bytes 6946816 | tf_op jit(solution)/shard_map/all_to_all | solution.py:637
  280.8 93.5 %all-to-all-start.1 = ((bf16[32,480,128]{2,1,0:T(8,128)(2,1)}), bf16[32,480,128]{2,1,0:T(8,128)(2,1)}, u32[]{:S(2)}, u32[]{:S(2)}) async-start(bf16[32,480,128]{2,1,0:T(8,128)(2,1)} %get-tuple-element.10), calls=%async_computation.1 | async-start | bytes 7864320 | tf_op jit(solution)/shard_map/all_to_all | solution.py:637
  285.7 50.7 %collective-permute-start.4 = (bf16[32,128,128]{2,1,0:T(8,128)(2,1)S(1)}, bf16[32,128,128]{2,1,0:T(8,128)(2,1)S(1)}, u32[]{:S(2)}, u32[]{:S(2)}) collective-permute-start(bf16[32,128,128]{2,1,0:T(8,128)(2,1)S(1)} %constant_dynamic-slice_fusion), channel_id=1, source_target_pairs={{0,1},{8,2},{1,0},{9,3},{10,11},{2,8},{11,10},{3,9},{20,21},{28,22... | collective-permute-start | bytes 3145736 | tf_op jit(solution)/shard_map/ppermute | solution.py:626
  290.4 44.3 %collective-permute-start.5 = (bf16[32,96,128]{2,1,0:T(8,128)(2,1)S(1)}, bf16[32,96,128]{2,1,0:T(8,128)(2,1)S(1)}, u32[]{:S(2)}, u32[]{:S(2)}) collective-permute-start(bf16[32,96,128]{2,1,0:T(8,128)(2,1)S(1)} %slice.45), channel_id=1, source_target_pairs={{0,16},{1,17},{10,26},{11,27},{20,4},{21,5},{30,14},{31,15}} | collective-permute-start | bytes 2359304 | tf_op jit(solution)/shard_map/ppermute | solution.py:596
  292.9 41.8 %collective-permute-start.6 = (bf16[32,64,128]{2,1,0:T(8,128)(2,1)S(1)}, bf16[32,64,128]{2,1,0:T(8,128)(2,1)S(1)}, u32[]{:S(2)}, u32[]{:S(2)}) collective-permute-start(bf16[32,64,128]{2,1,0:T(8,128)(2,1)S(1)} %slice.46), channel_id=1, source_target_pairs={{0,24},{1,25},{10,18},{11,19},{20,12},{21,13},{30,6},{31,7}} | collective-permute-start | bytes 1572872 | tf_op jit(solution)/shard_map/ppermute | solution.py:596
  295.2 0.7 collective-permute-start.7
  295.9 40.5 %copy-start.7 = (bf16[32,32,128]{2,1,0:T(8,128)(2,1)}, bf16[32,32,128]{2,1,0:T(8,128)(2,1)S(1)}, u32[]{:S(2)}) copy-start(bf16[32,32,128]{2,1,0:T(8,128)(2,1)S(1)} %collective-permute-done.7.last_ref) | copy-start | bytes 786436
  334.7 1.7 copy-start.5
  334.7 1.7 copy-start.3
  336.4 1.0 copy-start.1
  374.4 13.8 %all-to-all-start.4 = ((bf16[32,32,128]{2,1,0:T(8,128)(2,1)}), bf16[32,32,128]{2,1,0:T(8,128)(2,1)S(1)}, u32[]{:S(2)}, u32[]{:S(2)}) async-start(bf16[32,32,128]{2,1,0:T(8,128)(2,1)} %get-tuple-element.13), calls=%async_computation.4 | async-start | bytes 524288 | tf_op jit(solution)/shard_map/all_to_all | solution.py:637
